TPU v7x, 512 devices: a whole 4x8x8 slice. The times are simulated.
512 devices in a mesh: seq: 128 (over y, z, core), tp: 4 (over x).
Axes of the slice: x: 4, y: 8, z: 8, core: 2. Of those that a mesh axis runs over, the one named last changes fastest.
Arguments:
- queries: bfloat16 [16384, 4096], P('seq', 'tp'), may hold values from -12 to 12
- keys: bfloat16 [16384, 512], P('seq', 'tp'), may hold values from -12 to 12
- values: bfloat16 [16384, 512], P('seq', 'tp'), may hold values from -6 to 6
- sinks: float32 [64], P('tp'), may hold values from 0.5 to 4.5
- session_start: int32 [16384], P('seq'), may hold values from 0 to 16383, as said below
- residual: bfloat16 [16384, 2880], P('seq', 'tp'), may hold values from -40 to 40
- w_out: bfloat16 [4096, 2880], P('seq', 'tp'), may hold values from -0.09375 to 0.09375
- norm_gain: float32 [2880], P('tp'), may hold values from 0.1 to 1.9
- expert_ids: int32 [16384, 4], P('seq'), may hold values from 0 to 63, all different within a row; in each aligned block of 128 rows (0 to 127, 128 to 255, ...) at most 10 rows name the same one
- expert_gates: bfloat16 [16384, 4], P('seq'), may hold values from 0.099609375 to 0.59765625
- w_gate: bfloat16 [2880, 92160], P('tp', 'seq'), may hold values from -0.109375 to 0.109375
- w_up: bfloat16 [2880, 92160], P('tp', 'seq'), may hold values from -0.109375 to 0.109375
- w_down: bfloat16 [92160, 2880], P('seq', 'tp'), may hold values from -0.15625 to 0.15625
Outputs:
- layer_out: bfloat16 [16384, 2880], P('seq', 'tp')
Inputs may be any that keep to these rules, and one draw needn't show every extreme that they name: `expert_ids`: each row names 4 different experts. Within the rows of one seq index (aligned blocks of 128 rows) no expert is named by more than 10 rows, a bound that some block reaches. `session_start`: nondecreasing; each entry is the first position of its token's session, so session_start[i] <= i, with equality at a session's first token.
All inputs are finite; a program needn't handle non-finite values.
Results may differ from a plain program's by a relative error of at most 0.013.
Values may be sent and summed in bfloat16 or wider, within the bound.
No kernel may reach another device: no remote copies, remote signals or barrier semaphores. Data moves between devices by JAX's collectives and lax.ppermute only.
A program may use at most 64 MiB of HBM per device.

v0:
```python
import jax
import jax.numpy as jnp
from jax import lax
from jax.sharding import PartitionSpec as P

D = 2880
HEAD_SIZE = 64
WINDOW_SPAN = 128
TOP = 4


NEGATIVE = -1e30
EPSILON = 1e-05


def passed_along(block, axis, distance):
    devices = range(lax.axis_size(axis))
    route = [(i - distance, i) for i in devices if i - distance in devices]
    return lax.ppermute(block, axis, route)


def shards(
    queries,
    keys,
    values,
    sinks,
    session_start,
    residual,
    w_out,
    norm_gain,
    expert_ids,
    expert_gates,
    w_gate,
    w_up,
    w_down,
):
    tok_count = queries.shape[0]
    kv_heads = keys.shape[1] // HEAD_SIZE
    q_heads = queries.shape[1] // HEAD_SIZE
    query_groups = q_heads // kv_heads
    seq_index = lax.axis_index("seq")
    first_pos = seq_index * tok_count
    tail_rows = passed_along((keys, values), "seq", 1)
    all_keys = jnp.concatenate([tail_rows[0], keys], axis=0)
    all_values = jnp.concatenate([tail_rows[1], values], axis=0)
    key_count = all_keys.shape[0]
    query_pos = first_pos + jnp.arange(tok_count, dtype=jnp.int32)
    key_pos = first_pos - WINDOW_SPAN + jnp.arange(key_count, dtype=jnp.int32)
    distance = query_pos[:, None] - key_pos[None, :]
    allowed = (
        (distance >= 0) & (distance < WINDOW_SPAN) & (key_pos[None, :] >= session_start[:, None])
    )
    blocked_queries = queries.reshape(tok_count, kv_heads, query_groups, HEAD_SIZE)
    blocked_keys = all_keys.reshape(key_count, kv_heads, HEAD_SIZE)
    blocked_values = all_values.reshape(key_count, kv_heads, HEAD_SIZE)
    scores = jnp.einsum(
        "qhgd,khd->hgqk", blocked_queries, blocked_keys, preferred_element_type=jnp.float32
    ) * HEAD_SIZE ** (-0.5)
    scores = jnp.where(allowed[None, None], scores, NEGATIVE)
    sink_column = sinks.reshape(kv_heads, query_groups)[:, :, None, None]
    row_max = jnp.maximum(jnp.max(scores, axis=-1, keepdims=True), sink_column)
    numerator = jnp.exp(scores - row_max) * allowed[None, None].astype(jnp.float32)
    denominator = jnp.sum(numerator, axis=-1, keepdims=True) + jnp.exp(sink_column - row_max)
    weights = (numerator / denominator).astype(jnp.bfloat16)
    head_out = jnp.einsum(
        "hgqk,khd->qhgd", weights, blocked_values, preferred_element_type=jnp.float32
    )
    head_out = head_out.astype(jnp.bfloat16).reshape(tok_count, q_heads * HEAD_SIZE)
    gathered = lax.all_gather(head_out, "tp", axis=1, tiled=True)
    attended = jnp.dot(
        gathered,
        lax.all_gather(w_out, "seq", axis=0, tiled=True),
        preferred_element_type=jnp.float32,
    )
    stream = residual.astype(jnp.float32) + attended
    squares = lax.psum(jnp.sum(stream * stream, axis=1), "tp")
    normed = (stream * lax.rsqrt(squares / D + EPSILON)[:, None] * norm_gain[None, :]).astype(
        jnp.bfloat16
    )
    seq_count = lax.axis_size("seq")
    experts = seq_count // 2
    capacity = 2 * ((5 * tok_count * TOP + 8 * experts - 1) // (8 * experts))
    present = expert_ids[:, :, None] == jnp.arange(experts, dtype=jnp.int32)[None, None, :]
    per_row = jnp.sum(present.astype(jnp.int32), axis=1)
    before = jnp.cumsum(per_row, axis=0) - per_row
    position = jnp.sum(jnp.where(present, before[:, None, :], 0), axis=2)
    halves = jnp.arange(2, dtype=jnp.int32)
    targets = (2 * expert_ids[:, :, None] + halves[None, None, :]) * capacity + position[:, :, None]
    slot_count = seq_count * capacity
    slot_ids = jnp.arange(slot_count, dtype=jnp.int32)
    quarter = normed.shape[1]
    matches = (slot_ids[:, None, None, None] == targets[None]).astype(jnp.bfloat16)
    routing = jnp.sum(matches, axis=(2, 3))
    sending = jnp.dot(routing, normed, preferred_element_type=jnp.float32).astype(jnp.bfloat16)
    arrived = lax.all_to_all(
        sending.reshape(seq_count, capacity, quarter),
        "seq",
        split_axis=0,
        concat_axis=0,
        tiled=True,
    )
    expert_rows = arrived.reshape(slot_count, quarter)
    gate_part = jnp.dot(expert_rows, w_gate, preferred_element_type=jnp.float32)
    up_part = jnp.dot(expert_rows, w_up, preferred_element_type=jnp.float32)
    gate_sum, up_sum = (
        lax.psum_scatter(
            gate_part.astype(jnp.bfloat16), "tp", scatter_dimension=1, tiled=True
        ).astype(jnp.float32),
        lax.psum_scatter(
            up_part.astype(jnp.bfloat16), "tp", scatter_dimension=1, tiled=True
        ).astype(jnp.float32),
    )
    active = (jax.nn.silu(gate_sum) * up_sum).astype(jnp.bfloat16)
    produced = jnp.dot(
        lax.all_gather(active, "tp", axis=1, tiled=True), w_down, preferred_element_type=jnp.float32
    )
    produced = produced.astype(jnp.bfloat16).reshape(seq_count, capacity, quarter)
    returned = lax.all_to_all(produced, "seq", split_axis=0, concat_axis=0, tiled=True)
    both = returned.reshape(experts, 2, capacity, quarter)
    paired = (both[:, 0].astype(jnp.float32) + both[:, 1].astype(jnp.float32)).astype(jnp.bfloat16)
    paired = paired.reshape(experts * capacity, quarter)
    pair_slot = expert_ids * capacity + position
    pair_ids = jnp.arange(experts * capacity, dtype=jnp.int32)
    mixing = jnp.where(
        pair_ids[None, :, None] == pair_slot[:, None, :],
        expert_gates[:, None, :],
        jnp.zeros((), jnp.bfloat16),
    )
    mixing = jnp.sum(mixing, axis=2)
    blended = jnp.dot(mixing, paired, preferred_element_type=jnp.float32)
    return (stream + blended).astype(jnp.bfloat16)


def solution(mesh):
    return jax.shard_map(
        shards,
        mesh=mesh,
        in_specs=(
            P("seq", "tp"),
            P("seq", "tp"),
            P("seq", "tp"),
            P("tp"),
            P("seq"),
            P("seq", "tp"),
            P("seq", "tp"),
            P("tp"),
            P("seq", None),
            P("seq", None),
            P("tp", "seq"),
            P("tp", "seq"),
            P("seq", "tp"),
        ),
        out_specs=P("seq", "tp"),
        check_vma=False,
    )
```

profile of v0, /device:TPU:1, one launch (start us, length us, event | category | flops | bytes accessed | tf_op | source)
XLA Modules:
  0.0 458.9 jit_solution(16349413189414434142)
XLA Ops:
  6.5 0.0 copy-start
  6.5 0.0 all-gather.5.cloned.1.call-start
  6.5 5.5 %collective-permute-start.1 = (bf16[128,128]{1,0:T(8,128)(2,1)}, bf16[128,128]{1,0:T(8,128)(2,1)S(1)}, u32[]{:S(2)}, u32[]{:S(2)}) collective-permute-start(bf16[128,128]{1,0:T(8,128)(2,1)} %param.14), channel_id=1, source_target_pairs={{0,4},{4,8},{8,12},{12,16},{16,20},{20,24},{24,28},{28,32},{32,36}... | collective-permute-start | bytes 98312 | tf_op jit(solution)/shard_map/ppermute | solution.py:19
  12.1 1.9 collective-permute-start
  14.0 1.4 fusion.18
  15.4 1.1 copy.51
  16.6 0.7 max.18
  17.3 0.0 collective-permute-done.1
  17.3 0.8 pad_maximum_fusion.1
  18.1 0.7 copy.50
  18.8 1.4 fusion.4
  20.2 0.0 copy-start.2
  20.2 0.1 broadcast_maximum_fusion
  20.3 0.5 fusion.5
  20.8 0.1 exponential_add_fusion
  20.8 0.0 collective-permute-done
  20.9 0.0 copy-done.3
  20.9 0.1 copy.49
  21.0 0.1 copy-done.2
  21.1 1.4 convolution_convert_fusion.4
  22.5 0.0 all-gather.5.cloned.1.call-update
  22.5 0.0 all-gather.7.cloned.1.call-start
  22.6 0.7 all-gather.7.cloned.1.call-update
  23.3 0.0 all-gather.9.cloned.1.call-start
  23.3 0.0 copy-done.4
  23.4 0.1 copy.53
  23.5 0.2 reduce_window_sum.11
  23.6 0.1 copy.55
  23.8 0.7 fusion.3
  24.4 0.0 copy-start.5
  24.4 30.2 %all-gather.5.cloned.1.call-done = bf16[128,4096]{0,1:T(8,128)(2,1)} async-done(((bf16[128,1024]{0,1:T(8,128)(2,1)}), bf16[128,4096]{0,1:T(8,128)(2,1)}) %all-gather.5.cloned.1.call-update) | async-done | bytes 1048592 | tf_op jit(solution)/shard_map/all_gather | solution.py:69
  54.6 91.3 %all-gather.7.cloned.1.call-done = bf16[4096,720]{1,0:T(8,128)(2,1)} async-done(((bf16[32,720]{1,0:T(8,128)(2,1)}), bf16[4096,720]{1,0:T(8,128)(2,1)}) %all-gather.7.cloned.1.call-update) | async-done | bytes 5898256 | tf_op jit(solution)/shard_map/all_gather | solution.py:72
  146.0 5.1 %multiply_reduce_fusion = (f32[128]{0:T(128)S(1)}, f32[128,720]{0,1:T(8,128)S(1)}) fusion(bf16[128,4096]{0,1:T(8,128)(2,1)} %all-gather.5.cloned.1.call-done, bf16[4096,720]{1,0:T(8,128)(2,1)} %all-gather.7.cloned.1.call-done, bf16[128,720]{0,1:T(8,128)(2,1)} %param.18), kind=kOutput, calls=%fused_computation.31 | convolution fusion | flops 755343232 | bytes 7500288 | tf_op jit(solution)/shard_map/dot_general | solution.py:70
  151.1 8.4 %psum.7 = f32[128]{0:T(128)S(1)} all-reduce(f32[128]{0:T(128)S(1)} %get-tuple-element.15), channel_id=1, replica_groups=mesh['seq'=128,'tp'=4] {'tp'}, use_global_device_ids=true, to_apply=%region_8.9 | all-reduce | flops 128 | bytes 1024 | tf_op jit(solution)/shard_map/psum | solution.py:76
  159.5 2.0 convolution_convert_fusion
  161.5 2.6 copy.56
  164.1 2.5 reshape.190
  166.6 84.7 %all_to_all.10 = bf16[128,10,720]{2,1,0:T(8,128)(2,1)} all-to-all(bf16[128,10,720]{2,1,0:T(8,128)(2,1)} %reshape.190), channel_id=1, replica_groups=mesh['seq'=128,'tp'=4] {'seq'}, dimensions={0} | all-to-all | bytes 3686400 | tf_op jit(solution)/shard_map/all_to_all | solution.py:95
  251.3 3.9 reshape.191
  255.2 0.0 copy-start.7
  255.2 3.0 convolution_convert_fusion.2
  258.2 2.9 convolution_convert_fusion.3
  261.2 45.6 %fusion.22 = (bf16[1280,184]{0,1:T(8,128)(2,1)S(1)}, bf16[1280,184]{0,1:T(8,128)(2,1)S(1)}) fusion(bf16[1280,720]{0,1:T(8,128)(2,1)} %convolution_convert_fusion.2, bf16[1280,720]{0,1:T(8,128)(2,1)} %convolution_convert_fusion.3), kind=kCustom, calls=%all-reduce-scatter.2 | all-reduce-scatter fusion | flops 1884161 | bytes 4630528
  306.8 1.3 collective-permute-start.2
  308.1 2.8 collective-permute-start.3
  310.8 1.3 dynamic-slice.6
  312.8 0.0 collective-permute-done.2
  312.8 0.6 concatenate.8
  313.4 0.0 collective-permute-done.3
  313.4 0.6 concatenate.9
  314.1 1.2 fusion.14
  315.2 0.0 all-gather.9.cloned.1.call-update
  315.3 32.2 %all-gather.9.cloned.1.call-done = bf16[4,180,1280]{2,1,0:T(8,128)(2,1)} async-done(((bf16[1,180,1280]{2,1,0:T(8,128)(2,1)}), bf16[4,180,1280]{2,1,0:T(8,128)(2,1)}) %all-gather.9.cloned.1.call-update) | async-done | bytes 1843216 | tf_op jit(solution)/shard_map/all_gather | solution.py:115
  347.5 1.7 reshape.195
  349.2 4.2 convolution_convert_fusion.1
  353.4 2.6 copy.57
  356.1 2.5 reshape.192
  358.6 14.8 %all-to-all-start.1 = ((bf16[128,10,720]{2,1,0:T(8,128)(2,1)}), bf16[128,10,720]{2,1,0:T(8,128)(2,1)}, u32[]{:S(2)}, u32[]{:S(2)}) async-start(bf16[128,10,720]{2,1,0:T(8,128)(2,1)} %reshape.192), calls=%async_computation.1 | async-start | bytes 6291456 | tf_op jit(solution)/shard_map/all_to_all | solution.py:118
  373.4 0.0 copy-done.6
  373.4 0.2 fusion.13
  373.6 72.6 %all-to-all-done.1 = bf16[128,10,720]{2,1,0:T(8,128)(2,1)} async-done(((bf16[128,10,720]{2,1,0:T(8,128)(2,1)}), bf16[128,10,720]{2,1,0:T(8,128)(2,1)}, u32[]{:S(2)}, u32[]{:S(2)}) %all-to-all-start.1) | async-done | bytes 1843232 | tf_op jit(solution)/shard_map/all_to_all | solution.py:118
  446.2 2.3 add_convert_fusion
  448.5 1.4 convert_element_type.92
  449.9 2.4 fusion.7
  (19 shorter events, 0.2 us)
Async XLA Ops:
  6.5 248.7 %copy-start = (bf16[720,720]{1,0:T(8,128)(2,1)S(1)}, bf16[720,720]{1,0:T(8,128)(2,1)}, u32[]{:S(2)}) copy-start(bf16[720,720]{1,0:T(8,128)(2,1)} %param.24) | copy-start | bytes 3110404
  6.5 48.1 %all-gather.5.cloned.1.call-start = ((), (), s32[]{:S(2)}) async-start(), calls=%async_computation.2 | async-start | bytes 1310720 | tf_op jit(solution)/shard_map/all_gather | solution.py:69
  6.5 10.8 %collective-permute-start.1 = (bf16[128,128]{1,0:T(8,128)(2,1)}, bf16[128,128]{1,0:T(8,128)(2,1)S(1)}, u32[]{:S(2)}, u32[]{:S(2)}) collective-permute-start(bf16[128,128]{1,0:T(8,128)(2,1)} %param.14), channel_id=1, source_target_pairs={{0,4},{4,8},{8,12},{12,16},{16,20},{20,24},{24,28},{28,32},{32,36}... | collective-permute-start | bytes 98312 | tf_op jit(solution)/shard_map/ppermute | solution.py:19
  12.1 8.8 %collective-permute-start = (bf16[128,128]{1,0:T(8,128)(2,1)}, bf16[128,128]{1,0:T(8,128)(2,1)S(1)}, u32[]{:S(2)}, u32[]{:S(2)}) collective-permute-start(bf16[128,128]{1,0:T(8,128)(2,1)} %param.15), channel_id=1, source_target_pairs={{0,4},{4,8},{8,12},{12,16},{16,20},{20,24},{24,28},{28,32},{32,36}... | collective-permute-start | bytes 98312 | tf_op jit(solution)/shard_map/ppermute | solution.py:19
  18.8 1.5 copy-start.1
  18.8 2.0 copy-start.3
  20.2 0.9 copy-start.2
  21.1 2.2 copy-start.4
  22.5 123.4 %all-gather.7.cloned.1.call-start = ((), (), s32[]{:S(2)}) async-start(), calls=%async_computation.3 | async-start | bytes 6340608 | tf_op jit(solution)/shard_map/all_gather | solution.py:72
  23.3 324.2 %all-gather.9.cloned.1.call-start = ((), (), s32[]{:S(2)}) async-start(), calls=%async_computation.4 | async-start | bytes 2355200 | tf_op jit(solution)/shard_map/all_gather | solution.py:115
  24.4 135.1 %copy-start.5 = (f32[720]{0:T(1024)S(1)}, f32[720]{0:T(1024)}, u32[]{:S(2)}) copy-start(f32[720]{0:T(1024)} %param.20) | copy-start | bytes 8644
  255.2 3.0 copy-start.7
  306.8 6.0 %collective-permute-start.2 = (bf16[1280,12]{0,1:T(8,128)(2,1)S(1)}, bf16[1280,12]{0,1:T(8,128)(2,1)S(1)}, u32[]{:S(2)}, u32[]{:S(2)}) collective-permute-start(bf16[1280,12]{0,1:T(8,128)(2,1)S(1)} %slice.10), channel_id=1, source_target_pairs={{0,1},{1,2},{2,3},{4,5},{5,6},{6,7},{8,9},{9,10},{10,11},{12,13},{... | collective-permute-start | bytes 92168
  308.1 5.3 %collective-permute-start.3 = (bf16[1280,12]{0,1:T(8,128)(2,1)S(1)}, bf16[1280,12]{0,1:T(8,128)(2,1)S(1)}, u32[]{:S(2)}, u32[]{:S(2)}) collective-permute-start(bf16[1280,12]{0,1:T(8,128)(2,1)S(1)} %slice.11), channel_id=1, source_target_pairs={{0,1},{1,2},{2,3},{4,5},{5,6},{6,7},{8,9},{9,10},{10,11},{12,13},{... | collective-permute-start | bytes 92168
  358.6 14.8 %copy-start.6 = (bf16[128,4]{0,1:T(4,128)(2,1)S(1)}, bf16[128,4]{0,1:T(4,128)(2,1)}, u32[]{:S(2)}) copy-start(bf16[128,4]{0,1:T(4,128)(2,1)} %param.22) | copy-start | bytes 3076
  358.6 87.7 %all-to-all-start.1 = ((bf16[128,10,720]{2,1,0:T(8,128)(2,1)}), bf16[128,10,720]{2,1,0:T(8,128)(2,1)}, u32[]{:S(2)}, u32[]{:S(2)}) async-start(bf16[128,10,720]{2,1,0:T(8,128)(2,1)} %reshape.192), calls=%async_computation.1 | async-start | bytes 6291456 | tf_op jit(solution)/shard_map/all_to_all | solution.py:118
Sparse Core Ops, SparseCore 0:
  22.6 31.9 all-gather.4
  57.8 88.1 all-gather.6
  315.4 32.0 all-gather.8
where the time goes:
time: 460 us; the launch traced here: 459 us
  waiting for transfers between devices  227 us (49%)
  blocking collectives  139 us (30%)
  starting transfers between devices  26.4 us (6%)
  local copies, waits for them, and re-layouts  22.8 us (5%)
  matrix products  22.4 us (5%)
  between operations  14.1 us (3%)
  other arithmetic  7.47 us (2%)
    all_gather x1, waiting for transfers between devices, shards(): lax.all_gather(w_out, 'seq', axis=0, tiled=True)  91.3 us
    all_to_all x1, blocking collectives, shards(): lax.all_to_all(sending.reshape(seq_count, capacity, quarter), 'seq', spli...  84.7 us
    all_to_all x1, waiting for transfers between devices, shards(): lax.all_to_all(produced, 'seq', split_axis=0, concat_axis=0, tiled=True)  72.6 us
    unnamed x1, blocking collectives  45.6 us
    all_gather x1, waiting for transfers between devices, shards(): lax.all_gather(active, 'tp', axis=1, tiled=True)  32.2 us
    all_gather x1, waiting for transfers between devices, shards(): gathered = lax.all_gather(head_out, 'tp', axis=1, tiled=True)  30.2 us
    all_to_all x1, starting transfers between devices, shards(): lax.all_to_all(produced, 'seq', split_axis=0, concat_axis=0, tiled=True)  14.8 us
  transfers between devices with their start and end apart: 8, of which 4 were waited for; matrix products, arithmetic and copies ran while one was open for 2% of the time, Pallas kernels for 0%

commit v1 on v0

v1 whole, which is shorter than its diff:
```python
import jax
import jax.numpy as jnp
from jax import lax
from jax.experimental import pallas as pl
from jax.experimental.pallas import tpu as pltpu
from jax.sharding import Mesh, PartitionSpec as P

D = 2880
HEAD = 64
HALF = 32
GROUPS = 8
WINDOW = 128
EXPERTS = 64
TP = 4
QUARTER = 720
PADDED = 768
BLOCKS = 24
CLASS_SLOTS = 3
SLOTS = EXPERTS * CLASS_SLOTS
EPSILON = 1e-05
NEGATIVE = -1e30
F32 = jnp.float32
BF16 = jnp.bfloat16
SEQ = ("y", "z", "core")
CHIPS = ("y", "z")


def shifted(block, axis, distance):
    size = lax.axis_size(axis)
    return lax.ppermute(block, axis, [(i, (i + distance) % size) for i in range(size)])


def call(kernel, out_shape, args, scratch=(), spaces=None, flops=0, moved=0):
    spaces = spaces or [pltpu.VMEM] * len(args)
    return pl.pallas_call(
        kernel,
        out_shape=out_shape,
        in_specs=[pl.BlockSpec(memory_space=s) for s in spaces],
        out_specs=jax.tree.map(lambda _: pl.BlockSpec(memory_space=pltpu.VMEM), out_shape),
        scratch_shapes=list(scratch),
        cost_estimate=pl.CostEstimate(flops=flops, bytes_accessed=moved, transcendentals=0),
        compiler_params=pltpu.CompilerParams(vmem_limit_bytes=48 * 1024 * 1024),
    )(*args)


def attention_kernel(q_ref, own_ref, before_ref, start_ref, sink_ref, out_ref):
    rows = q_ref.shape[0]
    i = lax.broadcasted_iota(jnp.int32, (rows, rows), 0)
    j = lax.broadcasted_iota(jnp.int32, (rows, rows), 1)
    start = start_ref[...]
    allowed_before = (j > i) & (j >= start)
    allowed_own = (j <= i) & (j + WINDOW >= start)
    row = lax.broadcasted_iota(jnp.int32, (2 * HEAD, GROUPS * HALF), 0)
    col = lax.broadcasted_iota(jnp.int32, (2 * HEAD, GROUPS * HALF), 1)
    group_of_lane = lax.broadcasted_iota(jnp.int32, (rows, GROUPS * HALF), 1) // HALF
    contract = (((1,), (1,)), ((), ()))
    for h in range(2):
        lanes = slice(h * HEAD, (h + 1) * HEAD)
        k_own, k_before = own_ref[:, lanes], before_ref[:, lanes]
        spread = []
        for c in range(2):
            pick = (row == h * HEAD + c * HALF + col % HALF).astype(BF16)
            spread.append(
                [
                    jnp.dot(ref[:, 2 * HEAD :], pick, preferred_element_type=F32).astype(BF16)
                    for ref in (before_ref, own_ref)
                ]
            )
        totals = [jnp.zeros((rows, GROUPS * HALF), F32) for _ in range(2)]
        for g in range(GROUPS):
            head = h * GROUPS + g
            q = q_ref[:, head * HEAD : (head + 1) * HEAD]
            s_before = lax.dot_general(q, k_before, contract, preferred_element_type=F32)
            s_own = lax.dot_general(q, k_own, contract, preferred_element_type=F32)
            s_before = jnp.where(allowed_before, s_before * HEAD**-0.5, NEGATIVE)
            s_own = jnp.where(allowed_own, s_own * HEAD**-0.5, NEGATIVE)
            sink = sink_ref[head]
            top = jnp.max(jnp.maximum(s_before, s_own), axis=1, keepdims=True)
            top = jnp.maximum(top, sink)
            e_before = jnp.exp(s_before - top)
            e_own = jnp.exp(s_own - top)
            total = jnp.sum(e_before + e_own, axis=1, keepdims=True) + jnp.exp(sink - top)
            p_before = (e_before / total).astype(BF16)
            p_own = (e_own / total).astype(BF16)
            for c in range(2):
                v_before, v_own = spread[c]
                zero = jnp.zeros_like(v_own)
                mine = group_of_lane == g
                totals[c] += jnp.dot(
                    p_before, jnp.where(mine, v_before, zero), preferred_element_type=F32
                ) + jnp.dot(p_own, jnp.where(mine, v_own, zero), preferred_element_type=F32)
        for c in range(2):
            made = totals[c].astype(BF16)
            for t in range(TP):
                out_ref[c, t, h] = made


def projection_kernel(index_ref, heads_ref, *refs):
    shards, (own_ref, other_ref, total) = refs[:9], refs[9:]
    me = index_ref[8]
    rows = own_ref.shape[0]
    for half in range(2):
        acc = jnp.zeros((rows, QUARTER), F32)
        for n in range(7):
            chunk = heads_ref[half, index_ref[n]]
            acc += jnp.dot(chunk, shards[n][...], preferred_element_type=F32)
        chunk = heads_ref[half, index_ref[7]]
        depth = chunk.shape[1] // 2
        acc += jnp.dot(chunk[:, :depth], shards[7][...], preferred_element_type=F32)
        acc += jnp.dot(chunk[:, depth:], shards[8][...], preferred_element_type=F32)
        total[half] = acc
    own_ref[...] = total[me]
    other_ref[...] = total[1 - me]


def stream_kernel(residual_ref, own_ref, got_ref, gain_ref, stream_ref, rows_ref):
    stream = residual_ref[...].astype(F32) + (own_ref[...] + got_ref[...])
    stream_ref[...] = stream
    squares = jnp.sum(stream * stream, axis=1, keepdims=True)
    scaled = (stream * gain_ref[...]).astype(BF16)
    lane = lax.broadcasted_iota(jnp.int32, (stream.shape[0], PADDED - QUARTER), 1)
    high = squares.astype(BF16).astype(F32)
    middle = (squares - high).astype(BF16).astype(F32)
    low = squares - high - middle
    extra = jnp.where(lane == 0, high, jnp.where(lane == 1, middle, jnp.where(lane == 2, low, 0.0)))
    extra = extra.astype(BF16)
    for t in range(TP):
        rows_ref[t, :, :QUARTER] = scaled
        rows_ref[t, :, QUARTER:] = extra


def dispatch_kernel(rows_ref, routing_ref, out_ref, flat):
    squares = jnp.zeros((rows_ref.shape[1], 1), F32)
    for t in range(TP):
        squares += jnp.sum(rows_ref[t, :, QUARTER:].astype(F32), axis=1, keepdims=True)
    scale = lax.rsqrt(squares / D + EPSILON)
    routing = routing_ref[...]
    for t in range(TP):
        normed = (rows_ref[t].astype(F32) * scale).astype(BF16)
        picked = jnp.dot(routing, normed, preferred_element_type=F32)
        for b in range(6):
            flat[pl.ds(t * 6 + b, SLOTS, stride=BLOCKS), :] = picked[:, b * 128 : (b + 1) * 128]
    out_ref[...] = flat[...].astype(BF16)


def expert_kernel(mine_ref, other_ref, weights_ref, to_mine_ref, to_other_ref, flat, rows, w, sem):
    copies = [pltpu.make_async_copy(weights_ref.at[t], w.at[t], sem.at[t]) for t in range(TP)]
    for copy in copies:
        copy.start()
    for n, ref in enumerate((mine_ref, other_ref)):
        flat[...] = ref[...].astype(F32)
        for b in range(BLOCKS):
            rows[n * SLOTS : (n + 1) * SLOTS, b * 128 : (b + 1) * 128] = flat[
                pl.ds(b, SLOTS, stride=BLOCKS), :
            ].astype(BF16)
    gate = jnp.zeros((2 * SLOTS, QUARTER), F32)
    up = jnp.zeros((2 * SLOTS, QUARTER), F32)
    for t in range(TP):
        copies[t].wait()
        part = rows[:, t * PADDED : t * PADDED + QUARTER]
        gate += jnp.dot(part, w[t, :QUARTER, :], preferred_element_type=F32)
        up += jnp.dot(part, w[t, QUARTER : 2 * QUARTER, :], preferred_element_type=F32)
    active = (gate / (1.0 + jnp.exp(-gate)) * up).astype(BF16)
    for n, ref in enumerate((to_mine_ref, to_other_ref)):
        part = active[n * SLOTS : (n + 1) * SLOTS]
        for t in range(TP):
            made = jnp.dot(part, w[t, 2 * QUARTER :, :], preferred_element_type=F32)
            made = jnp.concatenate([made, jnp.zeros((SLOTS, PADDED - QUARTER), F32)], axis=1)
            for b in range(6):
                flat[pl.ds(t * 6 + b, SLOTS, stride=BLOCKS), :] = made[:, b * 128 : (b + 1) * 128]
        ref[...] = flat[...].astype(BF16)


def combine_kernel(back_ref, mixing_ref, out_ref, flat):
    flat[...] = back_ref[...].astype(F32)
    mixing = mixing_ref[...]
    for t in range(TP):
        for b in range(6):
            part = flat[pl.ds(t * 6 + b, SLOTS, stride=BLOCKS), :].astype(BF16)
            out_ref[t, :, b * 128 : (b + 1) * 128] = jnp.dot(
                mixing, part, preferred_element_type=F32
            ).astype(BF16)


def shards(
    queries,
    keys,
    values,
    sinks,
    session_start,
    residual,
    w_out,
    norm_gain,
    expert_ids,
    expert_gates,
    w_gate,
    w_up,
    w_down,
):
    count = queries.shape[0]
    y, core, tp = lax.axis_index("y"), lax.axis_index("core"), lax.axis_index("tp")
    seq_index = lax.axis_index(SEQ)
    seq_size = lax.axis_size("y") * lax.axis_size("z") * lax.axis_size("core")
    y_size, z_size = lax.axis_size("y"), lax.axis_size("z")

    with jax.named_scope("expert_weights"):
        blocks = jnp.concatenate([w_gate, w_up, w_down], axis=0)
        weights = lax.all_gather(blocks, "tp", axis=0, tiled=False)

    with jax.named_scope("projection_rows"):
        spread = jnp.broadcast_to(w_out[None], (z_size,) + w_out.shape)
        column = lax.all_to_all(spread, "z", 0, 0, tiled=True)
        column = column.reshape(z_size * w_out.shape[0], QUARTER)
        half = column.shape[0] // 2
        ahead, behind, pieces = column, column, [column]
        for _ in range(y_size // 2 - 1):
            ahead, behind = shifted(ahead, "y", 1), shifted(behind, "y", -1)
            pieces += [ahead, behind]
        pieces += [shifted(ahead[:half], "y", 1), shifted(behind[half:], "y", -1)]
        sources = [y]
        for k in range(1, y_size // 2):
            sources += [(y - k) % y_size, (y + k) % y_size]
        sources.append((y + y_size // 2) % y_size)
        index = jnp.stack([jnp.asarray(v, jnp.int32) for v in sources + [core]])

    with jax.named_scope("attention"):
        pair = jnp.concatenate([keys, values], axis=1)
        before = lax.ppermute(pair, SEQ, [(i, i + 1) for i in range(seq_size - 1)])
        start = (session_start - seq_index * count + WINDOW)[:, None]
        heads = call(
            attention_kernel,
            jax.ShapeDtypeStruct((2, TP, 2, count, GROUPS * HALF), BF16),
            (queries, pair, before, start, sinks),
            spaces=[pltpu.VMEM] * 4 + [pltpu.SMEM],
            flops=2_000_000_000,
            moved=2_000_000,
        )
        heads = lax.all_to_all(
            heads.reshape(2 * TP, 2, count, GROUPS * HALF), ("core", "tp"), 0, 0, tiled=True
        )
        heads = heads.reshape(2, TP * 2, count, GROUPS * HALF)

    with jax.named_scope("stream"):
        own, other = call(
            projection_kernel,
            [jax.ShapeDtypeStruct((count, QUARTER), F32)] * 2,
            (index, heads, *pieces),
            scratch=[pltpu.VMEM((2, count, QUARTER), F32)],
            spaces=[pltpu.SMEM] + [pltpu.VMEM] * 10,
            flops=800_000_000,
            moved=4_000_000,
        )
        got = shifted(other, "core", 1)
        stream, scaled = call(
            stream_kernel,
            [
                jax.ShapeDtypeStruct((count, QUARTER), F32),
                jax.ShapeDtypeStruct((TP, count, PADDED), BF16),
            ],
            (residual, own, got, norm_gain[None, :]),
        )
        scaled = lax.all_to_all(scaled, "tp", 0, 0, tiled=True)

    with jax.named_scope("routing"):
        present = expert_ids[:, :, None] == jnp.arange(EXPERTS, dtype=jnp.int32)[None, None, :]
        per_row = jnp.sum(present.astype(jnp.int32), axis=1)
        earlier = jnp.cumsum(per_row, axis=0) - per_row
        position = jnp.sum(jnp.where(present, earlier[:, None, :], 0), axis=2)
        target = jnp.where(
            position % TP == tp, expert_ids * CLASS_SLOTS + position // TP, -1
        )
        slots = jnp.arange(SLOTS, dtype=jnp.int32)
        routing = jnp.sum((slots[:, None, None] == target[None]).astype(BF16), axis=2)
        mixing = jnp.sum(
            jnp.where(
                slots[None, :, None] == target[:, None, :],
                expert_gates[:, None, :],
                jnp.zeros((), BF16),
            ),
            axis=2,
        )

    flat_scratch = pltpu.VMEM((SLOTS * BLOCKS, 128), F32)
    block = (EXPERTS, CLASS_SLOTS * BLOCKS, 128)
    flat_shape = jax.ShapeDtypeStruct((SLOTS * BLOCKS, 128), BF16)
    with jax.named_scope("dispatch"):
        sending = call(dispatch_kernel, flat_shape, (scaled, routing), scratch=[flat_scratch])
        arrived = lax.all_to_all(sending.reshape(block), CHIPS, 0, 0, tiled=True)
        partner = shifted(arrived, "core", 1)

    with jax.named_scope("experts"):
        to_mine, to_other = call(
            expert_kernel,
            [flat_shape] * 2,
            (arrived.reshape(flat_shape.shape), partner.reshape(flat_shape.shape), weights),
            scratch=[
                flat_scratch,
                pltpu.VMEM((2 * SLOTS, TP * PADDED), BF16),
                pltpu.VMEM((TP, 3 * QUARTER, QUARTER), BF16),
                pltpu.SemaphoreType.DMA((TP,)),
            ],
            spaces=[pltpu.VMEM] * 2 + [pl.ANY],
            flops=5_000_000_000,
            moved=15_000_000,
        )
        received = shifted(to_other, "core", 1)
        both = (to_mine.astype(F32) + received.astype(F32)).astype(BF16)

    with jax.named_scope("combine"):
        back = lax.all_to_all(both.reshape(block), CHIPS, 0, 0, tiled=True)
        mixed = call(
            combine_kernel,
            jax.ShapeDtypeStruct((TP, count, PADDED), BF16),
            (back.reshape(flat_shape.shape), mixing),
            scratch=[flat_scratch],
        )
        mixed = lax.all_to_all(mixed, "tp", 0, 0, tiled=True)
        moe = jnp.sum(mixed[:, :, :QUARTER].astype(F32), axis=0)
        return (stream + moe).astype(BF16)


def solution(mesh):
    whole = Mesh(mesh.devices.reshape(8, 8, 2, 4), ("y", "z", "core", "tp"))
    return jax.shard_map(
        shards,
        mesh=whole,
        in_specs=(
            P(SEQ, "tp"),
            P(SEQ, "tp"),
            P(SEQ, "tp"),
            P("tp"),
            P(SEQ),
            P(SEQ, "tp"),
            P(SEQ, "tp"),
            P("tp"),
            P(SEQ, None),
            P(SEQ, None),
            P("tp", SEQ),
            P("tp", SEQ),
            P(SEQ, "tp"),
        ),
        out_specs=P(SEQ, "tp"),
        check_vma=False,
    )
```

time: 460 us -> 277 us (0.60)
  waiting for transfers between devices: 227 us -> 67.1 us
  blocking collectives: 139 us -> 71.5 us
  starting transfers between devices: 26.4 us -> 62.5 us
  Pallas kernels: 0 us -> 23 us
  matrix products: 22.4 us -> 0 us
  local copies, waits for them, and re-layouts: 22.8 us -> 33.3 us
  other arithmetic: 7.47 us -> 1.87 us
    all_gather x3 -> x1, waiting for transfers between devices: 154 us -> 0.02 us  [shards(): weights = lax.all_gather(blocks, 'tp', axis=0, tiled=False)]
    unnamed x1 -> x0, blocking collectives: 45.6 us -> none
    ppermute x2 -> x12, starting transfers between devices: 7.43 us -> 44.6 us  [the longest x11 40.2 us: shifted(): lax.ppermute(block, axis, [(i, (i + distance) % size) for i in range(size)])]
    pallas_call x0 -> x6, Pallas kernels: none -> 23 us  [call(): pl.pallas_call(kernel, out_shape=out_shape, in_specs=[pl.BlockSpec(memory...]
    dot_general x8 -> x0, matrix products: 22.4 us -> none  [the longest x1 5.11 us: shards(): jnp.dot(gathered, lax.all_gather(w_out, 'seq', axis=0, tiled=True), prefe...]
    all_to_all x1 -> x3, waiting for transfers between devices: 72.6 us -> 51.3 us  [the longest x1 30 us: shards(): back = lax.all_to_all(both.reshape(block), CHIPS, 0, 0, tiled=True)]
    all_gather x0 -> x1, local copies, waits for them, and re-layouts: none -> 18.1 us  [shards(): weights = lax.all_gather(blocks, 'tp', axis=0, tiled=False)]
    ppermute x2 -> x12, waiting for transfers between devices: 0.01 us -> 15.7 us  [the longest x11 15.7 us: shifted(): lax.ppermute(block, axis, [(i, (i + distance) % size) for i in range(size)])]
  transfers between devices with their start and end apart: 8 -> 16, of which waited for: 4 -> 8; matrix products, arithmetic and copies ran while one was open for 2% -> 8% of each run, Pallas kernels for 0% -> 5%
where the time goes in v1:
time: 277 us; the launch traced here: 273 us
  blocking collectives  71.5 us (26%)
  waiting for transfers between devices  67.1 us (24%)
  starting transfers between devices  62.5 us (23%)
  local copies, waits for them, and re-layouts  33.3 us (12%)
  Pallas kernels  23 us (8%)
  between operations  13.9 us (5%)
    ppermute x11, starting transfers between devices, shifted(): lax.ppermute(block, axis, [(i, (i + distance) % size) for i in range(size)])  40.2 us
    all_to_all x1, blocking collectives, shards(): arrived = lax.all_to_all(sending.reshape(block), CHIPS, 0, 0, tiled=True)  34.8 us
    all_to_all x1, waiting for transfers between devices, shards(): back = lax.all_to_all(both.reshape(block), CHIPS, 0, 0, tiled=True)  30 us
    all_to_all x1, blocking collectives, shards(): column = lax.all_to_all(spread, 'z', 0, 0, tiled=True)  24.3 us
    pallas_call x6, Pallas kernels, call(): pl.pallas_call(kernel, out_shape=out_shape, in_specs=[pl.BlockSpec(memory...  23 us
    all_to_all x1, waiting for transfers between devices, shards(): scaled = lax.all_to_all(scaled, 'tp', 0, 0, tiled=True)  20.4 us
    all_gather x1, local copies, waits for them, and re-layouts, shards(): weights = lax.all_gather(blocks, 'tp', axis=0, tiled=False)  18.1 us
    ppermute x11, waiting for transfers between devices, shifted(): lax.ppermute(block, axis, [(i, (i + distance) % size) for i in range(size)])  15.7 us
  transfers between devices with their start and end apart: 16, of which 8 were waited for; matrix products, arithmetic and copies ran while one was open for 8% of the time, Pallas kernels for 5%

profile of v1, /device:TPU:1, one launch (start us, length us, event | category | flops | bytes accessed | tf_op | source)
XLA Modules:
  0.0 273.0 jit_solution(10469891021297805182)
XLA Ops:
  6.5 0.0 all-gather.4.cloned.1.call-start
  6.5 1.8 copy.37
  8.4 0.8 copy.38
  9.3 1.8 copy.39
  11.0 4.4 %concatenate.7 = bf16[2160,720]{0,1:T(8,128)(2,1)} concatenate(bf16[720,720]{0,1:T(8,128)(2,1)S(1)} %copy.37, bf16[720,720]{0,1:T(8,128)(2,1)S(1)} %copy.38, bf16[720,720]{0,1:T(8,128)(2,1)S(1)} %copy.39), dimensions={0} | concatenate | bytes 6220800 | tf_op jit(solution)/shard_map/expert_weights/concatenate | solution.py:207
  15.5 0.0 all-gather.4.cloned.1.call-update
  15.5 0.8 copy-done.5
  16.3 0.0 copy-start.3
  16.3 24.3 %all_to_all.30 = bf16[8,32,720]{2,1,0:T(8,128)(2,1)S(1)} all-to-all(bf16[8,32,720]{2,1,0:T(8,128)(2,1)S(1)} %broadcast_in_dim.47), channel_id=1, replica_groups=mesh['y'=8,'z'=8,'core'=2,'tp'=4] {'z'}, dimensions={0} | all-to-all | bytes 737280 | tf_op jit(solution)/shard_map/projection_rows/all_to_all | solution.py:212
  40.6 5.1 %collective-permute-start.2 = (bf16[256,720]{1,0:T(8,128)(2,1)S(1)}, bf16[256,720]{1,0:T(8,128)(2,1)S(1)}, u32[]{:S(2)}, u32[]{:S(2)}) collective-permute-start(bf16[256,720]{1,0:T(8,128)(2,1)S(1)} %bitcast.23), channel_id=1, source_target_pairs={{0,448},{64,0},{128,64},{192,128},{256,192},{320,256},{384,320},{4... | collective-permute-start | bytes 1105928 | tf_op jit(solution)/shard_map/projection_rows/ppermute | solution.py:30
  45.7 1.9 collective-permute-start.1
  47.7 4.5 %collective-permute-start = (bf16[128,256]{1,0:T(8,128)(2,1)S(1)}, bf16[128,256]{1,0:T(8,128)(2,1)S(1)}, u32[]{:S(2)}, u32[]{:S(2)}) collective-permute-start(bf16[128,256]{1,0:T(8,128)(2,1)S(1)} %constant_dynamic-update-slice_fusion.own_ref), channel_id=1, source_target_pairs={{0,4},{4,8},{8,12},{12,16},{16,20},{20,24},{24,28},{28,32},{32,36}... | collective-permute-start | bytes 196616 | tf_op jit(solution)/shard_map/attention/ppermute | solution.py:228
  52.2 0.1 copy.32.start_ref
  52.3 0.0 collective-permute-done.2.refs_2_
  52.3 5.1 %collective-permute-start.4 = (bf16[256,720]{1,0:T(8,128)(2,1)S(1)}, bf16[256,720]{1,0:T(8,128)(2,1)S(1)}, u32[]{:S(2)}, u32[]{:S(2)}) collective-permute-start(bf16[256,720]{1,0:T(8,128)(2,1)S(1)} %collective-permute-done.2.refs_2_), channel_id=1, source_target_pairs={{0,448},{64,0},{128,64},{192,128},{256,192},{320,256},{384,320},{4... | collective-permute-start | bytes 1105928 | tf_op jit(solution)/shard_map/projection_rows/ppermute | solution.py:30
  57.4 0.0 collective-permute-done.1.refs_1_
  57.4 1.9 collective-permute-start.3
  59.3 0.0 collective-permute-done.before_ref
  59.4 7.8 %attention.1 = bf16[2,4,2,128,256]{4,3,2,1,0:T(8,128)(2,1)} custom-call(bf16[128,1024]{1,0:T(8,128)(2,1)S(1)} %copy-done.2, bf16[128,256]{1,0:T(8,128)(2,1)S(1)} %constant_dynamic-update-slice_fusion.own_ref, bf16[128,256]{1,0:T(8,128)(2,1)S(1)} %collective-permute-done.before_ref, s32[128,1]{1,0:T(8,128)S(1)} %copy.32.start_ref, f32[16]{0:T(128)S(1)} %copy-done.3), custom_call_target="tpu_custom_call" | custom-call | flops 2000000000 | bytes 2000000 | tf_op jit(solution)/shard_map/attention/pallas_call | solution.py:35
  67.2 7.5 %all-to-all-start = ((bf16[8,2,128,256]{3,2,1,0:T(8,128)(2,1)}), bf16[8,2,128,256]{3,2,1,0:T(8,128)(2,1)S(1)}, u32[]{:S(2)}, u32[]{:S(2)}) async-start(bf16[8,2,128,256]{3,2,1,0:T(8,128)(2,1)} %bitcast.10), calls=%async_computation | async-start | bytes 2097152 | tf_op jit(solution)/shard_map/attention/all_to_all | solution.py:238
  74.7 0.0 collective-permute-done.4.refs_4_
  74.7 4.9 %collective-permute-start.6 = (bf16[256,720]{1,0:T(8,128)(2,1)S(1)}, bf16[256,720]{1,0:T(8,128)(2,1)S(1)}, u32[]{:S(2)}, u32[]{:S(2)}) collective-permute-start(bf16[256,720]{1,0:T(8,128)(2,1)S(1)} %collective-permute-done.4.refs_4_), channel_id=1, source_target_pairs={{0,448},{64,0},{128,64},{192,128},{256,192},{320,256},{384,320},{4... | collective-permute-start | bytes 1105928 | tf_op jit(solution)/shard_map/projection_rows/ppermute | solution.py:30
  79.6 0.0 collective-permute-done.3.refs_3_
  79.6 1.9 collective-permute-start.5
  81.5 6.6 %collective-permute-done.6.refs_6_ = bf16[256,720]{1,0:T(8,128)(2,1)S(1)} collective-permute-done((bf16[256,720]{1,0:T(8,128)(2,1)S(1)}, bf16[256,720]{1,0:T(8,128)(2,1)S(1)}, u32[]{:S(2)}, u32[]{:S(2)}) %collective-permute-start.6) | collective-permute-done | bytes 368672 | tf_op jit(solution)/shard_map/projection_rows/ppermute | solution.py:30
  88.1 0.7 slice.13
  88.8 5.4 %collective-permute-start.8 = (bf16[128,720]{1,0:T(8,128)(2,1)}, bf16[128,720]{1,0:T(8,128)(2,1)}, u32[]{:S(2)}, u32[]{:S(2)}) collective-permute-start(bf16[128,720]{1,0:T(8,128)(2,1)} %slice.13), channel_id=1, source_target_pairs={{0,448},{64,0},{128,64},{192,128},{256,192},{320,256},{384,320},{4... | collective-permute-start | bytes 552968 | tf_op jit(solution)/shard_map/projection_rows/ppermute | solution.py:30
  94.2 0.0 collective-permute-done.5.refs_5_
  94.2 0.7 slice.12
  94.9 1.9 collective-permute-start.7
  96.9 0.1 stack.39.index_ref
  97.0 0.9 all-to-all-done
  97.9 0.1 collective-permute-done.8.refs_8_
  98.1 5.7 %collective-permute-done.7.refs_7_ = bf16[128,720]{1,0:T(8,128)(2,1)} collective-permute-done((bf16[128,720]{1,0:T(8,128)(2,1)}, bf16[128,720]{1,0:T(8,128)(2,1)}, u32[]{:S(2)}, u32[]{:S(2)}) %collective-permute-start.7) | collective-permute-done | bytes 184352 | tf_op jit(solution)/shard_map/projection_rows/ppermute | solution.py:30
  103.8 3.1 %stream.2 = (f32[128,720]{1,0:T(8,128)S(1)}, f32[128,720]{1,0:T(8,128)}) custom-call(s32[9]{0:T(128)S(1)} %stack.39.index_ref, bf16[2,8,128,256]{3,2,1,0:T(8,128)(2,1)S(1)} %bitcast.22, bf16[256,720]{1,0:T(8,128)(2,1)S(1)} %bitcast.25, bf16[256,720]{1,0:T(8,128)(2,1)S(1)} %collective-permute-done.1.refs_1_, ...), custom_call_target="tpu_custom_call" | custom-call | flops 800000000 | bytes 4000000 | tf_op jit(solution)/shard_map/stream/pallas_call | solution.py:35
  106.8 0.7 copy-done
  107.6 3.8 %collective-permute-start.9 = (f32[128,720]{1,0:T(8,128)}, f32[128,720]{1,0:T(8,128)S(1)}, u32[]{:S(2)}, u32[]{:S(2)}) collective-permute-start(f32[128,720]{1,0:T(8,128)} %get-tuple-element.12), channel_id=1, source_target_pairs={{0,4},{4,0},{1,5},{5,1},{2,6},{6,2},{3,7},{7,3},{8,12},{12,8},{9,1... | collective-permute-start | bytes 1105928 | tf_op jit(solution)/shard_map/stream/ppermute | solution.py:30
  111.4 1.1 copy.33.residual_ref
  112.5 0.5 collective-permute-done.9.got_ref
  112.9 1.0 copy-done.1
  113.9 1.1 stream.3
  115.1 3.7 %all-to-all-start.2 = ((bf16[4,128,768]{2,1,0:T(8,128)(2,1)}), bf16[4,128,768]{2,1,0:T(8,128)(2,1)S(1)}, u32[]{:S(2)}, u32[]{:S(2)}) async-start(bf16[4,128,768]{2,1,0:T(8,128)(2,1)} %get-tuple-element.14), calls=%async_computation.2 | async-start | bytes 1572864 | tf_op jit(solution)/shard_map/stream/all_to_all | solution.py:262
  118.7 0.0 copy-done.8
  118.7 0.1 copy.34
  118.8 0.2 reduce_window_sum.11
  119.0 0.1 copy.36
  119.2 20.4 %all-to-all-done.2.rows_ref = bf16[4,128,768]{2,1,0:T(8,128)(2,1)S(1)} async-done(((bf16[4,128,768]{2,1,0:T(8,128)(2,1)}), bf16[4,128,768]{2,1,0:T(8,128)(2,1)S(1)}, u32[]{:S(2)}, u32[]{:S(2)}) %all-to-all-start.2) | async-done | bytes 786464 | tf_op jit(solution)/shard_map/stream/all_to_all | solution.py:262
  139.6 0.9 dispatch.1
  140.5 34.8 %all_to_all.31 = bf16[64,72,128]{2,1,0:T(8,128)(2,1)S(1)} all-to-all(bf16[64,72,128]{2,1,0:T(8,128)(2,1)S(1)} %bitcast.21), channel_id=1, replica_groups=mesh['y'=8,'z'=8,'core'=2,'tp'=4] {'y','z'}, dimensions={0} | all-to-all | bytes 2359296 | tf_op jit(solution)/shard_map/dispatch/all_to_all | solution.py:288
  175.3 6.4 %collective-permute-start.10 = (bf16[64,72,128]{2,1,0:T(8,128)(2,1)S(1)}, bf16[64,72,128]{2,1,0:T(8,128)(2,1)S(1)}, u32[]{:S(2)}, u32[]{:S(2)}) collective-permute-start(bf16[64,72,128]{2,1,0:T(8,128)(2,1)S(1)} %all_to_all.31), channel_id=1, source_target_pairs={{0,4},{4,0},{1,5},{5,1},{2,6},{6,2},{3,7},{7,3},{8,12},{12,8},{9,1... | collective-permute-start | bytes 3538952 | tf_op jit(solution)/shard_map/dispatch/ppermute | solution.py:30
  181.7 0.0 all-gather.4.cloned.1.call-done
  181.7 18.1 %copy.40.weights_ref = bf16[4,2160,720]{2,1,0:T(8,128)(2,1)} copy(bf16[4,2160,720]{1,2,0:T(8,128)(2,1)} %all-gather.4.cloned.1.call-done) | data formatting | bytes 24883200 | tf_op jit(solution)/shard_map/expert_weights/all_gather | solution.py:208
  199.8 0.0 collective-permute-done.10
  199.8 9.3 %experts.1 = (bf16[4608,128]{1,0:T(8,128)(2,1)S(1)}, bf16[4608,128]{1,0:T(8,128)(2,1)S(1)}) custom-call(bf16[4608,128]{1,0:T(8,128)(2,1)S(1)} %bitcast.26, bf16[4608,128]{1,0:T(8,128)(2,1)S(1)} %bitcast.27, bf16[4,2160,720]{2,1,0:T(8,128)(2,1)} %copy.40.weights_ref), custom_call_target="tpu_custom_call" | custom-call | flops 5000000000 | bytes 15000000 | tf_op jit(solution)/shard_map/experts/pallas_call | solution.py:35
  209.1 1.9 collective-permute-start.11
  211.0 2.8 %collective-permute-done.11 = bf16[4608,128]{1,0:T(8,128)(2,1)S(1)} collective-permute-done((bf16[4608,128]{1,0:T(8,128)(2,1)S(1)}, bf16[4608,128]{1,0:T(8,128)(2,1)S(1)}, u32[]{:S(2)}, u32[]{:S(2)}) %collective-permute-start.11) | collective-permute-done | bytes 1179680 | tf_op jit(solution)/shard_map/experts/ppermute | solution.py:30
  213.8 1.4 add_convert_fusion
  215.2 6.7 %all-to-all-start.4 = ((bf16[64,72,128]{2,1,0:T(8,128)(2,1)}), bf16[64,72,128]{2,1,0:T(8,128)(2,1)S(1)}, u32[]{:S(2)}, u32[]{:S(2)}) async-start(bf16[64,72,128]{2,1,0:T(8,128)(2,1)} %bitcast.17), calls=%async_computation.4 | async-start | bytes 2359296 | tf_op jit(solution)/shard_map/combine/all_to_all | solution.py:310
  221.9 0.1 copy.41.mixing_ref
  222.0 30.0 %all-to-all-done.4 = bf16[64,72,128]{2,1,0:T(8,128)(2,1)S(1)} async-done(((bf16[64,72,128]{2,1,0:T(8,128)(2,1)}), bf16[64,72,128]{2,1,0:T(8,128)(2,1)S(1)}, u32[]{:S(2)}, u32[]{:S(2)}) %all-to-all-start.4) | async-done | bytes 1179680 | tf_op jit(solution)/shard_map/combine/all_to_all | solution.py:310
  252.1 0.8 combine.1
  252.9 12.3 %all_to_all.32 = bf16[4,128,768]{2,1,0:T(8,128)(2,1)S(1)} all-to-all(bf16[4,128,768]{2,1,0:T(8,128)(2,1)S(1)} %combine.1), channel_id=1, replica_groups=mesh['y'=8,'z'=8,'core'=2,'tp'=4] {'tp'}, dimensions={0} | all-to-all | bytes 1572864 | tf_op jit(solution)/shard_map/combine/all_to_all | solution.py:317
  265.2 0.1 convert_reduce_fusion
  265.4 0.8 copy.42
  (31 shorter events, 0.3 us)
Async XLA Ops:
  6.5 1.9 copy-start.4
  6.5 175.2 %all-gather.4.cloned.1.call-start = ((), (), s32[]{:S(2)}) async-start(), calls=%async_computation.6 | async-start | bytes 15667200 | tf_op jit(solution)/shard_map/expert_weights/all_gather | solution.py:208
  15.5 0.8 copy-start.5
  16.3 31.4 %copy-start.6 = (bf16[128,128]{1,0:T(8,128)(2,1)S(1)}, bf16[128,128]{1,0:T(8,128)(2,1)}, u32[]{:S(2)}) copy-start(bf16[128,128]{1,0:T(8,128)(2,1)} %param.14) | copy-start | bytes 98308
  16.3 31.4 %copy-start.7 = (bf16[128,128]{1,0:T(8,128)(2,1)S(1)}, bf16[128,128]{1,0:T(8,128)(2,1)}, u32[]{:S(2)}) copy-start(bf16[128,128]{1,0:T(8,128)(2,1)} %param.15) | copy-start | bytes 98308
  16.3 35.9 %copy-start.11 = (s32[128]{0:T(128)S(1)}, s32[128]{0:T(128)}, u32[]{:S(2)}) copy-start(s32[128]{0:T(128)} %param.17) | copy-start | bytes 1540
  16.3 43.1 %copy-start.2 = (bf16[128,1024]{1,0:T(8,128)(2,1)S(1)}, bf16[128,1024]{1,0:T(8,128)(2,1)}, u32[]{:S(2)}) copy-start(bf16[128,1024]{1,0:T(8,128)(2,1)} %q_ref.1) | copy-start | bytes 786436
  16.3 43.1 %copy-start.3 = (f32[16]{0:T(128)S(1)}, f32[16]{0:T(128)}, u32[]{:S(2)}) copy-start(f32[16]{0:T(128)} %sink_ref.1) | copy-start | bytes 196
  40.6 11.7 %collective-permute-start.2 = (bf16[256,720]{1,0:T(8,128)(2,1)S(1)}, bf16[256,720]{1,0:T(8,128)(2,1)S(1)}, u32[]{:S(2)}, u32[]{:S(2)}) collective-permute-start(bf16[256,720]{1,0:T(8,128)(2,1)S(1)} %bitcast.23), channel_id=1, source_target_pairs={{0,448},{64,0},{128,64},{192,128},{256,192},{320,256},{384,320},{4... | collective-permute-start | bytes 1105928 | tf_op jit(solution)/shard_map/projection_rows/ppermute | solution.py:30
  45.7 11.7 %collective-permute-start.1 = (bf16[256,720]{1,0:T(8,128)(2,1)S(1)}, bf16[256,720]{1,0:T(8,128)(2,1)S(1)}, u32[]{:S(2)}, u32[]{:S(2)}) collective-permute-start(bf16[256,720]{1,0:T(8,128)(2,1)S(1)} %bitcast.24), channel_id=1, source_target_pairs={{0,64},{64,128},{128,192},{192,256},{256,320},{320,384},{384,448},... | collective-permute-start | bytes 1105928 | tf_op jit(solution)/shard_map/projection_rows/ppermute | solution.py:30
  47.7 11.6 %collective-permute-start = (bf16[128,256]{1,0:T(8,128)(2,1)S(1)}, bf16[128,256]{1,0:T(8,128)(2,1)S(1)}, u32[]{:S(2)}, u32[]{:S(2)}) collective-permute-start(bf16[128,256]{1,0:T(8,128)(2,1)S(1)} %constant_dynamic-update-slice_fusion.own_ref), channel_id=1, source_target_pairs={{0,4},{4,8},{8,12},{12,16},{16,20},{20,24},{24,28},{28,32},{32,36}... | collective-permute-start | bytes 196616 | tf_op jit(solution)/shard_map/attention/ppermute | solution.py:228
  52.3 22.4 %collective-permute-start.4 = (bf16[256,720]{1,0:T(8,128)(2,1)S(1)}, bf16[256,720]{1,0:T(8,128)(2,1)S(1)}, u32[]{:S(2)}, u32[]{:S(2)}) collective-permute-start(bf16[256,720]{1,0:T(8,128)(2,1)S(1)} %collective-permute-done.2.refs_2_), channel_id=1, source_target_pairs={{0,448},{64,0},{128,64},{192,128},{256,192},{320,256},{384,320},{4... | collective-permute-start | bytes 1105928 | tf_op jit(solution)/shard_map/projection_rows/ppermute | solution.py:30
  57.4 22.2 %collective-permute-start.3 = (bf16[256,720]{1,0:T(8,128)(2,1)S(1)}, bf16[256,720]{1,0:T(8,128)(2,1)}, u32[]{:S(2)}, u32[]{:S(2)}) collective-permute-start(bf16[256,720]{1,0:T(8,128)(2,1)S(1)} %collective-permute-done.1.refs_1_), channel_id=1, source_target_pairs={{0,64},{64,128},{128,192},{192,256},{256,320},{320,384},{384,448},... | collective-permute-start | bytes 1105928 | tf_op jit(solution)/shard_map/projection_rows/ppermute | solution.py:30
  67.2 30.7 %all-to-all-start = ((bf16[8,2,128,256]{3,2,1,0:T(8,128)(2,1)}), bf16[8,2,128,256]{3,2,1,0:T(8,128)(2,1)S(1)}, u32[]{:S(2)}, u32[]{:S(2)}) async-start(bf16[8,2,128,256]{3,2,1,0:T(8,128)(2,1)} %bitcast.10), calls=%async_computation | async-start | bytes 2097152 | tf_op jit(solution)/shard_map/attention/all_to_all | solution.py:238
  74.7 13.4 %collective-permute-start.6 = (bf16[256,720]{1,0:T(8,128)(2,1)S(1)}, bf16[256,720]{1,0:T(8,128)(2,1)S(1)}, u32[]{:S(2)}, u32[]{:S(2)}) collective-permute-start(bf16[256,720]{1,0:T(8,128)(2,1)S(1)} %collective-permute-done.4.refs_4_), channel_id=1, source_target_pairs={{0,448},{64,0},{128,64},{192,128},{256,192},{320,256},{384,320},{4... | collective-permute-start | bytes 1105928 | tf_op jit(solution)/shard_map/projection_rows/ppermute | solution.py:30
  79.6 14.6 %collective-permute-start.5 = (bf16[256,720]{1,0:T(8,128)(2,1)}, bf16[256,720]{1,0:T(8,128)(2,1)S(1)}, u32[]{:S(2)}, u32[]{:S(2)}) collective-permute-start(bf16[256,720]{1,0:T(8,128)(2,1)} %collective-permute-done.3.refs_3_), channel_id=1, source_target_pairs={{0,64},{64,128},{128,192},{192,256},{256,320},{320,384},{384,448},... | collective-permute-start | bytes 1105928 | tf_op jit(solution)/shard_map/projection_rows/ppermute | solution.py:30
  88.8 9.3 %collective-permute-start.8 = (bf16[128,720]{1,0:T(8,128)(2,1)}, bf16[128,720]{1,0:T(8,128)(2,1)}, u32[]{:S(2)}, u32[]{:S(2)}) collective-permute-start(bf16[128,720]{1,0:T(8,128)(2,1)} %slice.13), channel_id=1, source_target_pairs={{0,448},{64,0},{128,64},{192,128},{256,192},{320,256},{384,320},{4... | collective-permute-start | bytes 552968 | tf_op jit(solution)/shard_map/projection_rows/ppermute | solution.py:30
  94.9 8.8 %collective-permute-start.7 = (bf16[128,720]{1,0:T(8,128)(2,1)}, bf16[128,720]{1,0:T(8,128)(2,1)}, u32[]{:S(2)}, u32[]{:S(2)}) collective-permute-start(bf16[128,720]{1,0:T(8,128)(2,1)} %slice.12), channel_id=1, source_target_pairs={{0,64},{64,128},{128,192},{192,256},{256,320},{320,384},{384,448},... | collective-permute-start | bytes 552968 | tf_op jit(solution)/shard_map/projection_rows/ppermute | solution.py:30
  103.8 7.6 %copy-start.9 = (f32[720]{0:T(1024)S(1)}, f32[720]{0:T(1024)}, u32[]{:S(2)}) copy-start(f32[720]{0:T(1024)} %param.20) | copy-start | bytes 8644
  106.8 0.7 copy-start
  107.6 5.3 %collective-permute-start.9 = (f32[128,720]{1,0:T(8,128)}, f32[128,720]{1,0:T(8,128)S(1)}, u32[]{:S(2)}, u32[]{:S(2)}) collective-permute-start(f32[128,720]{1,0:T(8,128)} %get-tuple-element.12), channel_id=1, source_target_pairs={{0,4},{4,0},{1,5},{5,1},{2,6},{6,2},{3,7},{7,3},{8,12},{12,8},{9,1... | collective-permute-start | bytes 1105928 | tf_op jit(solution)/shard_map/stream/ppermute | solution.py:30
  112.9 1.0 copy-start.1
  113.9 4.8 %copy-start.8 = (s32[128,4]{0,1:T(4,128)S(1)}, s32[128,4]{0,1:T(4,128)}, u32[]{:S(2)}) copy-start(s32[128,4]{0,1:T(4,128)} %param.21) | copy-start | bytes 6148
  115.1 24.5 %all-to-all-start.2 = ((bf16[4,128,768]{2,1,0:T(8,128)(2,1)}), bf16[4,128,768]{2,1,0:T(8,128)(2,1)S(1)}, u32[]{:S(2)}, u32[]{:S(2)}) async-start(bf16[4,128,768]{2,1,0:T(8,128)(2,1)} %get-tuple-element.14), calls=%async_computation.2 | async-start | bytes 1572864 | tf_op jit(solution)/shard_map/stream/all_to_all | solution.py:262
  175.3 24.5 %collective-permute-start.10 = (bf16[64,72,128]{2,1,0:T(8,128)(2,1)S(1)}, bf16[64,72,128]{2,1,0:T(8,128)(2,1)S(1)}, u32[]{:S(2)}, u32[]{:S(2)}) collective-permute-start(bf16[64,72,128]{2,1,0:T(8,128)(2,1)S(1)} %all_to_all.31), channel_id=1, source_target_pairs={{0,4},{4,0},{1,5},{5,1},{2,6},{6,2},{3,7},{7,3},{8,12},{12,8},{9,1... | collective-permute-start | bytes 3538952 | tf_op jit(solution)/shard_map/dispatch/ppermute | solution.py:30
  209.1 4.7 %collective-permute-start.11 = (bf16[4608,128]{1,0:T(8,128)(2,1)S(1)}, bf16[4608,128]{1,0:T(8,128)(2,1)S(1)}, u32[]{:S(2)}, u32[]{:S(2)}) collective-permute-start(bf16[4608,128]{1,0:T(8,128)(2,1)S(1)} %get-tuple-element.16), channel_id=1, source_target_pairs={{0,4},{4,0},{1,5},{5,1},{2,6},{6,2},{3,7},{7,3},{8,12},{12,8},{9,1... | collective-permute-start | bytes 3538952 | tf_op jit(solution)/shard_map/experts/ppermute | solution.py:30
  215.2 6.7 %copy-start.10 = (bf16[128,4]{0,1:T(4,128)(2,1)S(1)}, bf16[128,4]{0,1:T(4,128)(2,1)}, u32[]{:S(2)}) copy-start(bf16[128,4]{0,1:T(4,128)(2,1)} %param.22) | copy-start | bytes 3076
  215.2 36.9 %all-to-all-start.4 = ((bf16[64,72,128]{2,1,0:T(8,128)(2,1)}), bf16[64,72,128]{2,1,0:T(8,128)(2,1)S(1)}, u32[]{:S(2)}, u32[]{:S(2)}) async-start(bf16[64,72,128]{2,1,0:T(8,128)(2,1)} %bitcast.17), calls=%async_computation.4 | async-start | bytes 2359296 | tf_op jit(solution)/shard_map/combine/all_to_all | solution.py:310
Sparse Core Ops, SparseCore 0:
  15.6 148.6 all-gather.3

commit v2 on v1

--- a/solution.py
+++ b/solution.py
@@ -15,6 +15,7 @@
 QUARTER = 720
 PADDED = 768
 BLOCKS = 24
+FAR = QUARTER + 384
 CLASS_SLOTS = 3
 SLOTS = EXPERTS * CLASS_SLOTS
 EPSILON = 1e-05
@@ -23,6 +24,7 @@
 BF16 = jnp.bfloat16
 SEQ = ("y", "z", "core")
 CHIPS = ("y", "z")
+GATHERED = ("y", "core")
 
 
 def shifted(block, axis, distance):
@@ -30,7 +32,7 @@
     return lax.ppermute(block, axis, [(i, (i + distance) % size) for i in range(size)])
 
 
-def call(kernel, out_shape, args, scratch=(), spaces=None, flops=0, moved=0):
+def call(kernel, out_shape, args, scratch=(), spaces=None, flops=0, moved=0, limit=32):
     spaces = spaces or [pltpu.VMEM] * len(args)
     return pl.pallas_call(
         kernel,
@@ -39,7 +41,7 @@
         out_specs=jax.tree.map(lambda _: pl.BlockSpec(memory_space=pltpu.VMEM), out_shape),
         scratch_shapes=list(scratch),
         cost_estimate=pl.CostEstimate(flops=flops, bytes_accessed=moved, transcendentals=0),
-        compiler_params=pltpu.CompilerParams(vmem_limit_bytes=48 * 1024 * 1024),
+        compiler_params=pltpu.CompilerParams(vmem_limit_bytes=limit * 1024 * 1024),
     )(*args)
 
 
@@ -92,29 +94,16 @@
         for c in range(2):
             made = totals[c].astype(BF16)
             for t in range(TP):
-                out_ref[c, t, h] = made
-
-
-def projection_kernel(index_ref, heads_ref, *refs):
-    shards, (own_ref, other_ref, total) = refs[:9], refs[9:]
-    me = index_ref[8]
-    rows = own_ref.shape[0]
-    for half in range(2):
-        acc = jnp.zeros((rows, QUARTER), F32)
-        for n in range(7):
-            chunk = heads_ref[half, index_ref[n]]
-            acc += jnp.dot(chunk, shards[n][...], preferred_element_type=F32)
-        chunk = heads_ref[half, index_ref[7]]
-        depth = chunk.shape[1] // 2
-        acc += jnp.dot(chunk[:, :depth], shards[7][...], preferred_element_type=F32)
-        acc += jnp.dot(chunk[:, depth:], shards[8][...], preferred_element_type=F32)
-        total[half] = acc
-    own_ref[...] = total[me]
-    other_ref[...] = total[1 - me]
-
-
-def stream_kernel(residual_ref, own_ref, got_ref, gain_ref, stream_ref, rows_ref):
-    stream = residual_ref[...].astype(F32) + (own_ref[...] + got_ref[...])
+                out_ref[t, h, c] = made
+
+
+def projection_kernel(heads_ref, w_ref, residual_ref, gain_ref, stream_ref, rows_ref):
+    stream = residual_ref[...].astype(F32)
+    depth = GROUPS * HALF
+    for n in range(heads_ref.shape[0]):
+        stream += jnp.dot(
+            heads_ref[n], w_ref[n * depth : (n + 1) * depth, :], preferred_element_type=F32
+        )
     stream_ref[...] = stream
     squares = jnp.sum(stream * stream, axis=1, keepdims=True)
     scaled = (stream * gain_ref[...]).astype(BF16)
@@ -129,55 +118,78 @@
         rows_ref[t, :, QUARTER:] = extra
 
 
-def dispatch_kernel(rows_ref, routing_ref, out_ref, flat):
+def dispatch_kernel(order_ref, rows_ref, routing_ref, out_ref, flat):
     squares = jnp.zeros((rows_ref.shape[1], 1), F32)
     for t in range(TP):
         squares += jnp.sum(rows_ref[t, :, QUARTER:].astype(F32), axis=1, keepdims=True)
     scale = lax.rsqrt(squares / D + EPSILON)
     routing = routing_ref[...]
     for t in range(TP):
-        normed = (rows_ref[t].astype(F32) * scale).astype(BF16)
+        normed = (rows_ref[order_ref[t]].astype(F32) * scale).astype(BF16)
         picked = jnp.dot(routing, normed, preferred_element_type=F32)
         for b in range(6):
             flat[pl.ds(t * 6 + b, SLOTS, stride=BLOCKS), :] = picked[:, b * 128 : (b + 1) * 128]
     out_ref[...] = flat[...].astype(BF16)
 
 
-def expert_kernel(mine_ref, other_ref, weights_ref, to_mine_ref, to_other_ref, flat, rows, w, sem):
-    copies = [pltpu.make_async_copy(weights_ref.at[t], w.at[t], sem.at[t]) for t in range(TP)]
-    for copy in copies:
-        copy.start()
+def pack_kernel(gate_ref, up_ref, down_ref, out_ref):
+    for n, ref in enumerate((gate_ref, up_ref, down_ref)):
+        out_ref[n * QUARTER : (n + 1) * QUARTER, :QUARTER] = ref[...]
+    pad = jnp.zeros((out_ref.shape[0], PADDED - QUARTER), BF16)
+    out_ref[:, QUARTER:] = pad
+
+
+def expert_kernel(
+    mine_ref,
+    other_ref,
+    own_ref,
+    left_ref,
+    right_ref,
+    far_a_ref,
+    far_b_ref,
+    to_mine_ref,
+    to_other_ref,
+    flat,
+    rows,
+):
     for n, ref in enumerate((mine_ref, other_ref)):
         flat[...] = ref[...].astype(F32)
         for b in range(BLOCKS):
-            rows[n * SLOTS : (n + 1) * SLOTS, b * 128 : (b + 1) * 128] = flat[
+            lanes = slice(b % 6 * 128, b % 6 * 128 + 128)
+            rows[b // 6, n * SLOTS : (n + 1) * SLOTS, lanes] = flat[
                 pl.ds(b, SLOTS, stride=BLOCKS), :
             ].astype(BF16)
     gate = jnp.zeros((2 * SLOTS, QUARTER), F32)
     up = jnp.zeros((2 * SLOTS, QUARTER), F32)
-    for t in range(TP):
-        copies[t].wait()
-        part = rows[:, t * PADDED : t * PADDED + QUARTER]
-        gate += jnp.dot(part, w[t, :QUARTER, :], preferred_element_type=F32)
-        up += jnp.dot(part, w[t, QUARTER : 2 * QUARTER, :], preferred_element_type=F32)
+    near = (own_ref, left_ref, right_ref)
+    for n, ref in enumerate(near):
+        part = rows[n, :, :QUARTER]
+        gate += jnp.dot(part, ref[:QUARTER, :QUARTER], preferred_element_type=F32)
+        up += jnp.dot(part, ref[QUARTER : 2 * QUARTER, :QUARTER], preferred_element_type=F32)
+    split = FAR - QUARTER
+    gate += jnp.dot(rows[3, :, :QUARTER], far_a_ref[:QUARTER, :QUARTER], preferred_element_type=F32)
+    up += jnp.dot(rows[3, :, :split], far_a_ref[QUARTER:, :QUARTER], preferred_element_type=F32)
+    up += jnp.dot(
+        rows[3, :, split:QUARTER], far_b_ref[: QUARTER - split, :QUARTER], preferred_element_type=F32
+    )
     active = (gate / (1.0 + jnp.exp(-gate)) * up).astype(BF16)
+    down = [ref[2 * QUARTER :, :] for ref in near] + [far_b_ref[QUARTER - split :, :]]
     for n, ref in enumerate((to_mine_ref, to_other_ref)):
         part = active[n * SLOTS : (n + 1) * SLOTS]
         for t in range(TP):
-            made = jnp.dot(part, w[t, 2 * QUARTER :, :], preferred_element_type=F32)
-            made = jnp.concatenate([made, jnp.zeros((SLOTS, PADDED - QUARTER), F32)], axis=1)
+            made = jnp.dot(part, down[t], preferred_element_type=F32)
             for b in range(6):
                 flat[pl.ds(t * 6 + b, SLOTS, stride=BLOCKS), :] = made[:, b * 128 : (b + 1) * 128]
         ref[...] = flat[...].astype(BF16)
 
 
-def combine_kernel(back_ref, mixing_ref, out_ref, flat):
+def combine_kernel(order_ref, back_ref, mixing_ref, out_ref, flat):
     flat[...] = back_ref[...].astype(F32)
     mixing = mixing_ref[...]
     for t in range(TP):
         for b in range(6):
             part = flat[pl.ds(t * 6 + b, SLOTS, stride=BLOCKS), :].astype(BF16)
-            out_ref[t, :, b * 128 : (b + 1) * 128] = jnp.dot(
+            out_ref[order_ref[t], :, b * 128 : (b + 1) * 128] = jnp.dot(
                 mixing, part, preferred_element_type=F32
             ).astype(BF16)
 
@@ -198,30 +210,27 @@
     w_down,
 ):
     count = queries.shape[0]
-    y, core, tp = lax.axis_index("y"), lax.axis_index("core"), lax.axis_index("tp")
+    tp = lax.axis_index("tp")
     seq_index = lax.axis_index(SEQ)
     seq_size = lax.axis_size("y") * lax.axis_size("z") * lax.axis_size("core")
-    y_size, z_size = lax.axis_size("y"), lax.axis_size("z")
+    z_size = lax.axis_size("z")
+    order = jnp.stack([tp, (tp + 3) % TP, (tp + 1) % TP, (tp + 2) % TP]).astype(jnp.int32)
 
     with jax.named_scope("expert_weights"):
-        blocks = jnp.concatenate([w_gate, w_up, w_down], axis=0)
-        weights = lax.all_gather(blocks, "tp", axis=0, tiled=False)
+        packed = call(
+            pack_kernel,
+            jax.ShapeDtypeStruct((3 * QUARTER, PADDED), BF16),
+            (w_gate, w_up, w_down),
+            limit=16,
+        )
+        packed, w_out, keys = lax.optimization_barrier((packed, w_out, keys))
+        left, right = shifted(packed, "tp", 1), shifted(packed, "tp", -1)
 
     with jax.named_scope("projection_rows"):
         spread = jnp.broadcast_to(w_out[None], (z_size,) + w_out.shape)
         column = lax.all_to_all(spread, "z", 0, 0, tiled=True)
         column = column.reshape(z_size * w_out.shape[0], QUARTER)
-        half = column.shape[0] // 2
-        ahead, behind, pieces = column, column, [column]
-        for _ in range(y_size // 2 - 1):
-            ahead, behind = shifted(ahead, "y", 1), shifted(behind, "y", -1)
-            pieces += [ahead, behind]
-        pieces += [shifted(ahead[:half], "y", 1), shifted(behind[half:], "y", -1)]
-        sources = [y]
-        for k in range(1, y_size // 2):
-            sources += [(y - k) % y_size, (y + k) % y_size]
-        sources.append((y + y_size // 2) % y_size)
-        index = jnp.stack([jnp.asarray(v, jnp.int32) for v in sources + [core]])
+        w_all = lax.all_gather(column, GATHERED, axis=0, tiled=True)
 
     with jax.named_scope("attention"):
         pair = jnp.concatenate([keys, values], axis=1)
@@ -229,37 +238,34 @@
         start = (session_start - seq_index * count + WINDOW)[:, None]
         heads = call(
             attention_kernel,
-            jax.ShapeDtypeStruct((2, TP, 2, count, GROUPS * HALF), BF16),
+            jax.ShapeDtypeStruct((TP, 2, 2, count, GROUPS * HALF), BF16),
             (queries, pair, before, start, sinks),
             spaces=[pltpu.VMEM] * 4 + [pltpu.SMEM],
             flops=2_000_000_000,
             moved=2_000_000,
-        )
-        heads = lax.all_to_all(
-            heads.reshape(2 * TP, 2, count, GROUPS * HALF), ("core", "tp"), 0, 0, tiled=True
-        )
-        heads = heads.reshape(2, TP * 2, count, GROUPS * HALF)
+            limit=24,
+        )
+        heads = lax.all_to_all(heads, "tp", 0, 0, tiled=True)
+        heads = heads.reshape(TP * 4, count, GROUPS * HALF)
 
     with jax.named_scope("stream"):
-        own, other = call(
+        stream, scaled = call(
             projection_kernel,
-            [jax.ShapeDtypeStruct((count, QUARTER), F32)] * 2,
-            (index, heads, *pieces),
-            scratch=[pltpu.VMEM((2, count, QUARTER), F32)],
-            spaces=[pltpu.SMEM] + [pltpu.VMEM] * 10,
-            flops=800_000_000,
-            moved=4_000_000,
-        )
-        got = shifted(other, "core", 1)
-        stream, scaled = call(
-            stream_kernel,
             [
                 jax.ShapeDtypeStruct((count, QUARTER), F32),
                 jax.ShapeDtypeStruct((TP, count, PADDED), BF16),
             ],
-            (residual, own, got, norm_gain[None, :]),
+            (heads, w_all, residual, norm_gain[None, :]),
+            flops=800_000_000,
+            moved=8_000_000,
+            limit=24,
         )
         scaled = lax.all_to_all(scaled, "tp", 0, 0, tiled=True)
+        scaled, left, right = lax.optimization_barrier((scaled, left, right))
+
+    with jax.named_scope("expert_weights"):
+        far_a = shifted(left[:FAR], "tp", 1)
+        far_b = shifted(right[FAR:], "tp", -1)
 
     with jax.named_scope("routing"):
         present = expert_ids[:, :, None] == jnp.arange(EXPERTS, dtype=jnp.int32)[None, None, :]
@@ -284,7 +290,7 @@
     block = (EXPERTS, CLASS_SLOTS * BLOCKS, 128)
     flat_shape = jax.ShapeDtypeStruct((SLOTS * BLOCKS, 128), BF16)
     with jax.named_scope("dispatch"):
-        sending = call(dispatch_kernel, flat_shape, (scaled, routing), scratch=[flat_scratch])
+        sending = call(dispatch_kernel, flat_shape, (order, scaled, routing), scratch=[flat_scratch], spaces=[pltpu.SMEM] + [pltpu.VMEM] * 2, limit=16)
         arrived = lax.all_to_all(sending.reshape(block), CHIPS, 0, 0, tiled=True)
         partner = shifted(arrived, "core", 1)
 
@@ -292,16 +298,19 @@
         to_mine, to_other = call(
             expert_kernel,
             [flat_shape] * 2,
-            (arrived.reshape(flat_shape.shape), partner.reshape(flat_shape.shape), weights),
-            scratch=[
-                flat_scratch,
-                pltpu.VMEM((2 * SLOTS, TP * PADDED), BF16),
-                pltpu.VMEM((TP, 3 * QUARTER, QUARTER), BF16),
-                pltpu.SemaphoreType.DMA((TP,)),
-            ],
-            spaces=[pltpu.VMEM] * 2 + [pl.ANY],
+            (
+                arrived.reshape(flat_shape.shape),
+                partner.reshape(flat_shape.shape),
+                packed,
+                left,
+                right,
+                far_a,
+                far_b,
+            ),
+            scratch=[flat_scratch, pltpu.VMEM((TP, 2 * SLOTS, PADDED), BF16)],
             flops=5_000_000_000,
             moved=15_000_000,
+            limit=40,
         )
         received = shifted(to_other, "core", 1)
         both = (to_mine.astype(F32) + received.astype(F32)).astype(BF16)
@@ -311,8 +320,10 @@
         mixed = call(
             combine_kernel,
             jax.ShapeDtypeStruct((TP, count, PADDED), BF16),
-            (back.reshape(flat_shape.shape), mixing),
+            (order, back.reshape(flat_shape.shape), mixing),
             scratch=[flat_scratch],
+            spaces=[pltpu.SMEM] + [pltpu.VMEM] * 2,
+            limit=16,
         )
         mixed = lax.all_to_all(mixed, "tp", 0, 0, tiled=True)
         moe = jnp.sum(mixed[:, :, :QUARTER].astype(F32), axis=0)

time: 277 us -> 289 us (1.043)
  waiting for transfers between devices: 67.1 us -> 125 us
  blocking collectives: 71.5 us -> 37.4 us
  local copies, waits for them, and re-layouts: 33.3 us -> 13.4 us
  Pallas kernels: 23 us -> 26.9 us
    all_to_all x1 -> x2, waiting for transfers between devices: 0.92 us -> 77.2 us  [the longest x1 62.4 us: shards(): heads = lax.all_to_all(heads, 'tp', 0, 0, tiled=True)]
    all_to_all x1 -> x0, blocking collectives: 34.8 us -> none  [shards(): arrived = lax.all_to_all(sending.reshape(block), CHIPS, 0, 0, tiled=True)]
    all_gather x1 -> x0, local copies, waits for them, and re-layouts: 18.1 us -> none  [shards(): weights = lax.all_gather(blocks, 'tp', axis=0, tiled=False)]
    all_to_all x1, waiting for transfers between devices: 20.4 us -> 7.72 us  [shards(): scaled = lax.all_to_all(scaled, 'tp', 0, 0, tiled=True)]
    ppermute x11 -> x6, starting transfers between devices: 40.2 us -> 28.9 us  [shifted(): lax.ppermute(block, axis, [(i, (i + distance) % size) for i in range(size)])]
    all_to_all x1 -> x2, starting transfers between devices: 7.52 us -> 14.9 us  [the longest x1 11.3 us: shards(): arrived = lax.all_to_all(sending.reshape(block), CHIPS, 0, 0, tiled=True)]
    ppermute x11 -> x6, waiting for transfers between devices: 15.7 us -> 9.57 us  [shifted(): lax.ppermute(block, axis, [(i, (i + distance) % size) for i in range(size)])]
    all_to_all x1, starting transfers between devices: 6.66 us -> 12.3 us  [shards(): back = lax.all_to_all(both.reshape(block), CHIPS, 0, 0, tiled=True)]
  transfers between devices with their start and end apart: 16 -> 12, of which waited for: 8 -> 7; matrix products, arithmetic and copies ran while one was open for 8% -> 2% of each run, Pallas kernels for 5% -> 3%
where the time goes in v2:
time: 289 us; the launch traced here: 283 us
  waiting for transfers between devices  125 us (43%)
  starting transfers between devices  65.1 us (23%)
  blocking collectives  37.4 us (13%)
  Pallas kernels  26.9 us (9%)
  between operations  13.7 us (5%)
  local copies, waits for them, and re-layouts  13.4 us (5%)
    all_to_all x1, waiting for transfers between devices, shards(): heads = lax.all_to_all(heads, 'tp', 0, 0, tiled=True)  62.4 us
    all_to_all x1, waiting for transfers between devices, shards(): back = lax.all_to_all(both.reshape(block), CHIPS, 0, 0, tiled=True)  29.4 us
    ppermute x6, starting transfers between devices, shifted(): lax.ppermute(block, axis, [(i, (i + distance) % size) for i in range(size)])  28.9 us
    pallas_call x6, Pallas kernels, call(): pl.pallas_call(kernel, out_shape=out_shape, in_specs=[pl.BlockSpec(memory...  26.9 us
    all_to_all x1, blocking collectives, shards(): column = lax.all_to_all(spread, 'z', 0, 0, tiled=True)  24.4 us
    all_to_all x1, waiting for transfers between devices, shards(): arrived = lax.all_to_all(sending.reshape(block), CHIPS, 0, 0, tiled=True)  14.8 us
    all_to_all x1, blocking collectives, shards(): mixed = lax.all_to_all(mixed, 'tp', 0, 0, tiled=True)  13 us
    all_to_all x1, starting transfers between devices, shards(): back = lax.all_to_all(both.reshape(block), CHIPS, 0, 0, tiled=True)  12.3 us
  transfers between devices with their start and end apart: 12, of which 7 were waited for; matrix products, arithmetic and copies ran while one was open for 2% of the time, Pallas kernels for 3%

profile of v2, /device:TPU:1, one launch (start us, length us, event | category | flops | bytes accessed | tf_op | source)
XLA Modules:
  0.0 283.5 jit_solution(18408747834870279066)
XLA Ops:
  6.5 0.0 all-gather.2.cloned.1.call-start
  6.5 0.0 copy-start.1
  6.5 1.2 copy-done.1
  7.8 0.0 copy-start.2
  7.8 1.2 copy-done.2
  9.0 0.0 copy-start.3
  9.0 1.2 copy-done.3
  10.3 0.0 copy-start.7
  10.3 2.1 expert_weights.1.own_ref
  12.3 0.0 copy-done.7
  12.4 0.0 copy-start.4
  12.4 0.0 copy-start.5
  12.4 24.4 %all_to_all.30 = bf16[8,32,720]{2,1,0:T(8,128)(2,1)} all-to-all(bf16[8,32,720]{2,1,0:T(8,128)(2,1)S(1)} %broadcast_in_dim.47), channel_id=1, replica_groups=mesh['y'=8,'z'=8,'core'=2,'tp'=4] {'z'}, dimensions={0} | all-to-all | bytes 737280 | tf_op jit(solution)/shard_map/projection_rows/all_to_all | solution.py:231
  36.8 0.0 all-gather.2.cloned.1.call-update
  36.9 3.1 %collective-permute-start.1 = (bf16[2160,768]{1,0:T(8,128)(2,1)}, bf16[2160,768]{1,0:T(8,128)(2,1)}, u32[]{:S(2)}, u32[]{:S(2)}) collective-permute-start(bf16[2160,768]{1,0:T(8,128)(2,1)} %expert_weights.1.own_ref), channel_id=1, source_target_pairs={{0,1},{1,2},{2,3},{3,0},{4,5},{5,6},{6,7},{7,4},{8,9},{9,10},{10,1... | collective-permute-start | bytes 9953288 | tf_op jit(solution)/shard_map/expert_weights/ppermute | solution.py:32
  40.0 3.4 %collective-permute-start.2 = (bf16[2160,768]{1,0:T(8,128)(2,1)}, bf16[2160,768]{1,0:T(8,128)(2,1)}, u32[]{:S(2)}, u32[]{:S(2)}) collective-permute-start(bf16[2160,768]{1,0:T(8,128)(2,1)} %expert_weights.1.own_ref), channel_id=1, source_target_pairs={{0,3},{1,0},{2,1},{3,2},{4,7},{5,4},{6,5},{7,6},{8,11},{9,8},{10,9... | collective-permute-start | bytes 9953288 | tf_op jit(solution)/shard_map/expert_weights/ppermute | solution.py:32
  43.4 0.0 copy-done.8
  43.4 0.0 copy-done.9
  43.4 4.8 %collective-permute-start = (bf16[128,256]{1,0:T(8,128)(2,1)S(1)}, bf16[128,256]{1,0:T(8,128)(2,1)S(1)}, u32[]{:S(2)}, u32[]{:S(2)}) collective-permute-start(bf16[128,256]{1,0:T(8,128)(2,1)S(1)} %constant_dynamic-update-slice_fusion.own_ref), channel_id=1, source_target_pairs={{0,4},{4,8},{8,12},{12,16},{16,20},{20,24},{24,28},{28,32},{32,36}... | collective-permute-start | bytes 196616 | tf_op jit(solution)/shard_map/attention/ppermute | solution.py:237
  48.2 0.0 copy-done.13
  48.2 0.1 copy.21.start_ref
  48.3 1.2 collective-permute-done.before_ref
  49.5 0.0 copy-done.4
  49.5 0.0 copy-done.5
  49.5 7.8 %attention.1 = bf16[4,2,2,128,256]{4,3,2,1,0:T(8,128)(2,1)} custom-call(bf16[128,1024]{1,0:T(8,128)(2,1)S(1)} %copy-done.4, bf16[128,256]{1,0:T(8,128)(2,1)S(1)} %constant_dynamic-update-slice_fusion.own_ref, bf16[128,256]{1,0:T(8,128)(2,1)S(1)} %collective-permute-done.before_ref, s32[128,1]{1,0:T(8,128)S(1)} %copy.21.start_ref, f32[16]{0:T(128)S(1)} %copy-done.5), custom_call_target="tpu_custom_call" | custom-call | flops 2000000000 | bytes 2000000 | tf_op jit(solution)/shard_map/attention/pallas_call | solution.py:37
  57.3 3.6 %all-to-all-start = ((bf16[4,2,2,128,256]{4,3,2,1,0:T(8,128)(2,1)}), bf16[4,2,2,128,256]{4,3,2,1,0:T(8,128)(2,1)S(1)}, u32[]{:S(2)}, u32[]{:S(2)}) async-start(bf16[4,2,2,128,256]{4,3,2,1,0:T(8,128)(2,1)} %attention.1), calls=%async_computation | async-start | bytes 2097152 | tf_op jit(solution)/shard_map/attention/all_to_all | solution.py:248
  61.0 0.0 copy-done.6
  61.0 0.1 copy.22.residual_ref
  61.1 0.0 copy-done.11
  61.1 62.4 %all-to-all-done = bf16[4,2,2,128,256]{4,3,2,1,0:T(8,128)(2,1)S(1)} async-done(((bf16[4,2,2,128,256]{4,3,2,1,0:T(8,128)(2,1)}), bf16[4,2,2,128,256]{4,3,2,1,0:T(8,128)(2,1)S(1)}, u32[]{:S(2)}, u32[]{:S(2)}) %all-to-all-start) | async-done | bytes 1048608 | tf_op jit(solution)/shard_map/attention/all_to_all | solution.py:248
  123.6 2.8 copy-done
  126.3 2.1 stream.1
  128.4 4.2 %all-to-all-start.2 = ((bf16[4,128,768]{2,1,0:T(8,128)(2,1)}), bf16[4,128,768]{2,1,0:T(8,128)(2,1)S(1)}, u32[]{:S(2)}, u32[]{:S(2)}) async-start(bf16[4,128,768]{2,1,0:T(8,128)(2,1)} %get-tuple-element.18), calls=%async_computation.2 | async-start | bytes 1572864 | tf_op jit(solution)/shard_map/stream/all_to_all | solution.py:263
  132.6 0.0 copy-done.10
  132.6 0.1 copy.23
  132.7 0.2 reduce_window_sum.11
  132.9 0.1 copy.25
  133.0 0.1 pad_add_fusion.order_ref
  133.2 0.0 collective-permute-done.1.left_ref
  133.2 0.0 collective-permute-done.2.right_ref
  133.2 7.7 %all-to-all-done.2.rows_ref = bf16[4,128,768]{2,1,0:T(8,128)(2,1)S(1)} async-done(((bf16[4,128,768]{2,1,0:T(8,128)(2,1)}), bf16[4,128,768]{2,1,0:T(8,128)(2,1)S(1)}, u32[]{:S(2)}, u32[]{:S(2)}) %all-to-all-start.2) | async-done | bytes 786464 | tf_op jit(solution)/shard_map/stream/all_to_all | solution.py:263
  140.9 2.5 dispatch.1
  143.4 11.3 %all-to-all-start.3 = ((bf16[64,72,128]{2,1,0:T(8,128)(2,1)}), bf16[64,72,128]{2,1,0:T(8,128)(2,1)S(1)}, u32[]{:S(2)}, u32[]{:S(2)}) async-start(bf16[64,72,128]{2,1,0:T(8,128)(2,1)} %bitcast.7), calls=%async_computation.3 | async-start | bytes 2359296 | tf_op jit(solution)/shard_map/dispatch/all_to_all | solution.py:294
  154.7 2.8 slice.9
  157.4 2.2 collective-permute-start.4
  159.6 2.7 slice.10
  162.3 4.3 %collective-permute-start.5 = (bf16[1056,768]{1,0:T(8,128)(2,1)}, bf16[1056,768]{1,0:T(8,128)(2,1)}, u32[]{:S(2)}, u32[]{:S(2)}) collective-permute-start(bf16[1056,768]{1,0:T(8,128)(2,1)} %slice.10), channel_id=1, source_target_pairs={{0,3},{1,0},{2,1},{3,2},{4,7},{5,4},{6,5},{7,6},{8,11},{9,8},{10,9... | collective-permute-start | bytes 4866056 | tf_op jit(solution)/shard_map/expert_weights/ppermute | solution.py:32
  166.6 14.8 %all-to-all-done.3 = bf16[64,72,128]{2,1,0:T(8,128)(2,1)S(1)} async-done(((bf16[64,72,128]{2,1,0:T(8,128)(2,1)}), bf16[64,72,128]{2,1,0:T(8,128)(2,1)S(1)}, u32[]{:S(2)}, u32[]{:S(2)}) %all-to-all-start.3) | async-done | bytes 1179680 | tf_op jit(solution)/shard_map/dispatch/all_to_all | solution.py:294
  181.4 8.6 %collective-permute-start.3 = (bf16[64,72,128]{2,1,0:T(8,128)(2,1)S(1)}, bf16[64,72,128]{2,1,0:T(8,128)(2,1)S(1)}, u32[]{:S(2)}, u32[]{:S(2)}) collective-permute-start(bf16[64,72,128]{2,1,0:T(8,128)(2,1)S(1)} %all-to-all-done.3), channel_id=1, source_target_pairs={{0,4},{4,0},{1,5},{5,1},{2,6},{6,2},{3,7},{7,3},{8,12},{12,8},{9,1... | collective-permute-start | bytes 3538952 | tf_op jit(solution)/shard_map/dispatch/ppermute | solution.py:32
  190.0 7.1 %collective-permute-done.5.far_b_ref = bf16[1056,768]{1,0:T(8,128)(2,1)} collective-permute-done((bf16[1056,768]{1,0:T(8,128)(2,1)}, bf16[1056,768]{1,0:T(8,128)(2,1)}, u32[]{:S(2)}, u32[]{:S(2)}) %collective-permute-start.5) | collective-permute-done | bytes 1622048 | tf_op jit(solution)/shard_map/expert_weights/ppermute | solution.py:32
  197.1 0.0 collective-permute-done.4.far_a_ref
  197.1 0.0 collective-permute-done.3
  197.2 11.2 %experts.1 = (bf16[4608,128]{1,0:T(8,128)(2,1)S(1)}, bf16[4608,128]{1,0:T(8,128)(2,1)S(1)}) custom-call(bf16[4608,128]{1,0:T(8,128)(2,1)S(1)} %bitcast.15, bf16[4608,128]{1,0:T(8,128)(2,1)S(1)} %bitcast.16, bf16[2160,768]{1,0:T(8,128)(2,1)} %expert_weights.1.own_ref, bf16[2160,768]{1,0:T(8,128)(2,1)} %collective-permute-done.1.left_ref, ...), custom_call_target="tpu_custom_call" | custom-call | flops 5000000000 | bytes 15000000 | tf_op jit(solution)/shard_map/experts/pallas_call | solution.py:37
  208.3 7.4 %collective-permute-start.6 = (bf16[4608,128]{1,0:T(8,128)(2,1)S(1)}, bf16[4608,128]{1,0:T(8,128)(2,1)S(1)}, u32[]{:S(2)}, u32[]{:S(2)}) collective-permute-start(bf16[4608,128]{1,0:T(8,128)(2,1)S(1)} %get-tuple-element.24), channel_id=1, source_target_pairs={{0,4},{4,0},{1,5},{5,1},{2,6},{6,2},{3,7},{7,3},{8,12},{12,8},{9,1... | collective-permute-start | bytes 3538952 | tf_op jit(solution)/shard_map/experts/ppermute | solution.py:32
  215.7 2.5 collective-permute-done.6
  218.1 1.3 add_convert_fusion
  219.5 12.3 %all-to-all-start.4 = ((bf16[64,72,128]{2,1,0:T(8,128)(2,1)}), bf16[64,72,128]{2,1,0:T(8,128)(2,1)S(1)}, u32[]{:S(2)}, u32[]{:S(2)}) async-start(bf16[64,72,128]{2,1,0:T(8,128)(2,1)} %bitcast.10), calls=%async_computation.4 | async-start | bytes 2359296 | tf_op jit(solution)/shard_map/combine/all_to_all | solution.py:319
  231.7 0.0 copy-done.12
  231.8 0.1 copy.26.mixing_ref
  231.9 29.4 %all-to-all-done.4 = bf16[64,72,128]{2,1,0:T(8,128)(2,1)S(1)} async-done(((bf16[64,72,128]{2,1,0:T(8,128)(2,1)}), bf16[64,72,128]{2,1,0:T(8,128)(2,1)S(1)}, u32[]{:S(2)}, u32[]{:S(2)}) %all-to-all-start.4) | async-done | bytes 1179680 | tf_op jit(solution)/shard_map/combine/all_to_all | solution.py:319
  261.3 1.3 combine.1
  262.7 13.0 %all_to_all.31 = bf16[4,128,768]{2,1,0:T(8,128)(2,1)S(1)} all-to-all(bf16[4,128,768]{2,1,0:T(8,128)(2,1)S(1)} %combine.1), channel_id=1, replica_groups=mesh['y'=8,'z'=8,'core'=2,'tp'=4] {'tp'}, dimensions={0} | all-to-all | bytes 1572864 | tf_op jit(solution)/shard_map/combine/all_to_all | solution.py:328
  275.7 0.1 convert_reduce_fusion
  275.8 0.8 copy.27
  (21 shorter events, 0.3 us)
Async XLA Ops:
  6.5 117.0 %all-gather.2.cloned.1.call-start = ((), (), s32[]{:S(2)}) async-start(), calls=%async_computation.6 | async-start | bytes 6684672 | tf_op jit(solution)/shard_map/projection_rows/all_gather | solution.py:233
  6.5 1.2 copy-start.1
  7.8 1.2 copy-start.2
  9.0 1.2 copy-start.3
  10.3 2.1 copy-start.7
  12.3 31.0 %copy-start.8 = (bf16[128,128]{1,0:T(8,128)(2,1)S(1)}, bf16[128,128]{1,0:T(8,128)(2,1)}, u32[]{:S(2)}) copy-start(bf16[128,128]{1,0:T(8,128)(2,1)} %param.14) | copy-start | bytes 98308
  12.3 31.0 %copy-start.9 = (bf16[128,128]{1,0:T(8,128)(2,1)S(1)}, bf16[128,128]{1,0:T(8,128)(2,1)}, u32[]{:S(2)}) copy-start(bf16[128,128]{1,0:T(8,128)(2,1)} %param.15) | copy-start | bytes 98308
  12.3 35.9 %copy-start.13 = (s32[128]{0:T(128)S(1)}, s32[128]{0:T(128)}, u32[]{:S(2)}) copy-start(s32[128]{0:T(128)} %param.17) | copy-start | bytes 1540
  12.4 37.1 %copy-start.4 = (bf16[128,1024]{1,0:T(8,128)(2,1)S(1)}, bf16[128,1024]{1,0:T(8,128)(2,1)}, u32[]{:S(2)}) copy-start(bf16[128,1024]{1,0:T(8,128)(2,1)} %q_ref.1) | copy-start | bytes 786436
  12.4 37.1 %copy-start.5 = (f32[16]{0:T(128)S(1)}, f32[16]{0:T(128)}, u32[]{:S(2)}) copy-start(f32[16]{0:T(128)} %sink_ref.1) | copy-start | bytes 196
  36.9 96.3 %collective-permute-start.1 = (bf16[2160,768]{1,0:T(8,128)(2,1)}, bf16[2160,768]{1,0:T(8,128)(2,1)}, u32[]{:S(2)}, u32[]{:S(2)}) collective-permute-start(bf16[2160,768]{1,0:T(8,128)(2,1)} %expert_weights.1.own_ref), channel_id=1, source_target_pairs={{0,1},{1,2},{2,3},{3,0},{4,5},{5,6},{6,7},{7,4},{8,9},{9,10},{10,1... | collective-permute-start | bytes 9953288 | tf_op jit(solution)/shard_map/expert_weights/ppermute | solution.py:32
  40.0 93.2 %collective-permute-start.2 = (bf16[2160,768]{1,0:T(8,128)(2,1)}, bf16[2160,768]{1,0:T(8,128)(2,1)}, u32[]{:S(2)}, u32[]{:S(2)}) collective-permute-start(bf16[2160,768]{1,0:T(8,128)(2,1)} %expert_weights.1.own_ref), channel_id=1, source_target_pairs={{0,3},{1,0},{2,1},{3,2},{4,7},{5,4},{6,5},{7,6},{8,11},{9,8},{10,9... | collective-permute-start | bytes 9953288 | tf_op jit(solution)/shard_map/expert_weights/ppermute | solution.py:32
  43.4 6.1 %collective-permute-start = (bf16[128,256]{1,0:T(8,128)(2,1)S(1)}, bf16[128,256]{1,0:T(8,128)(2,1)S(1)}, u32[]{:S(2)}, u32[]{:S(2)}) collective-permute-start(bf16[128,256]{1,0:T(8,128)(2,1)S(1)} %constant_dynamic-update-slice_fusion.own_ref), channel_id=1, source_target_pairs={{0,4},{4,8},{8,12},{12,16},{16,20},{20,24},{24,28},{28,32},{32,36}... | collective-permute-start | bytes 196616 | tf_op jit(solution)/shard_map/attention/ppermute | solution.py:237
  57.3 3.7 %copy-start.6 = (bf16[128,720]{0,1:T(8,128)(2,1)S(1)}, bf16[128,720]{0,1:T(8,128)(2,1)}, u32[]{:S(2)}) copy-start(bf16[128,720]{0,1:T(8,128)(2,1)} %param.18) | copy-start | bytes 552964
  57.3 3.8 %copy-start.11 = (f32[720]{0:T(1024)S(1)}, f32[720]{0:T(1024)}, u32[]{:S(2)}) copy-start(f32[720]{0:T(1024)} %param.20) | copy-start | bytes 8644
  57.3 66.2 %all-to-all-start = ((bf16[4,2,2,128,256]{4,3,2,1,0:T(8,128)(2,1)}), bf16[4,2,2,128,256]{4,3,2,1,0:T(8,128)(2,1)S(1)}, u32[]{:S(2)}, u32[]{:S(2)}) async-start(bf16[4,2,2,128,256]{4,3,2,1,0:T(8,128)(2,1)} %attention.1), calls=%async_computation | async-start | bytes 2097152 | tf_op jit(solution)/shard_map/attention/all_to_all | solution.py:248
  123.6 2.8 copy-start
  128.4 4.2 %copy-start.10 = (s32[128,4]{0,1:T(4,128)S(1)}, s32[128,4]{0,1:T(4,128)}, u32[]{:S(2)}) copy-start(s32[128,4]{0,1:T(4,128)} %param.21) | copy-start | bytes 6148
  128.4 12.5 %all-to-all-start.2 = ((bf16[4,128,768]{2,1,0:T(8,128)(2,1)}), bf16[4,128,768]{2,1,0:T(8,128)(2,1)S(1)}, u32[]{:S(2)}, u32[]{:S(2)}) async-start(bf16[4,128,768]{2,1,0:T(8,128)(2,1)} %get-tuple-element.18), calls=%async_computation.2 | async-start | bytes 1572864 | tf_op jit(solution)/shard_map/stream/all_to_all | solution.py:263
  143.4 38.1 %all-to-all-start.3 = ((bf16[64,72,128]{2,1,0:T(8,128)(2,1)}), bf16[64,72,128]{2,1,0:T(8,128)(2,1)S(1)}, u32[]{:S(2)}, u32[]{:S(2)}) async-start(bf16[64,72,128]{2,1,0:T(8,128)(2,1)} %bitcast.7), calls=%async_computation.3 | async-start | bytes 2359296 | tf_op jit(solution)/shard_map/dispatch/all_to_all | solution.py:294
  157.4 39.7 %collective-permute-start.4 = (bf16[1104,768]{1,0:T(8,128)(2,1)}, bf16[1104,768]{1,0:T(8,128)(2,1)S(1)}, u32[]{:S(2)}, u32[]{:S(2)}) collective-permute-start(bf16[1104,768]{1,0:T(8,128)(2,1)} %slice.9), channel_id=1, source_target_pairs={{0,1},{1,2},{2,3},{3,0},{4,5},{5,6},{6,7},{7,4},{8,9},{9,10},{10,1... | collective-permute-start | bytes 5087240 | tf_op jit(solution)/shard_map/expert_weights/ppermute | solution.py:32
  162.3 34.8 %collective-permute-start.5 = (bf16[1056,768]{1,0:T(8,128)(2,1)}, bf16[1056,768]{1,0:T(8,128)(2,1)}, u32[]{:S(2)}, u32[]{:S(2)}) collective-permute-start(bf16[1056,768]{1,0:T(8,128)(2,1)} %slice.10), channel_id=1, source_target_pairs={{0,3},{1,0},{2,1},{3,2},{4,7},{5,4},{6,5},{7,6},{8,11},{9,8},{10,9... | collective-permute-start | bytes 4866056 | tf_op jit(solution)/shard_map/expert_weights/ppermute | solution.py:32
  181.4 15.7 %collective-permute-start.3 = (bf16[64,72,128]{2,1,0:T(8,128)(2,1)S(1)}, bf16[64,72,128]{2,1,0:T(8,128)(2,1)S(1)}, u32[]{:S(2)}, u32[]{:S(2)}) collective-permute-start(bf16[64,72,128]{2,1,0:T(8,128)(2,1)S(1)} %all-to-all-done.3), channel_id=1, source_target_pairs={{0,4},{4,0},{1,5},{5,1},{2,6},{6,2},{3,7},{7,3},{8,12},{12,8},{9,1... | collective-permute-start | bytes 3538952 | tf_op jit(solution)/shard_map/dispatch/ppermute | solution.py:32
  208.3 9.8 %collective-permute-start.6 = (bf16[4608,128]{1,0:T(8,128)(2,1)S(1)}, bf16[4608,128]{1,0:T(8,128)(2,1)S(1)}, u32[]{:S(2)}, u32[]{:S(2)}) collective-permute-start(bf16[4608,128]{1,0:T(8,128)(2,1)S(1)} %get-tuple-element.24), channel_id=1, source_target_pairs={{0,4},{4,0},{1,5},{5,1},{2,6},{6,2},{3,7},{7,3},{8,12},{12,8},{9,1... | collective-permute-start | bytes 3538952 | tf_op jit(solution)/shard_map/experts/ppermute | solution.py:32
  219.5 12.3 %copy-start.12 = (bf16[128,4]{0,1:T(4,128)(2,1)S(1)}, bf16[128,4]{0,1:T(4,128)(2,1)}, u32[]{:S(2)}) copy-start(bf16[128,4]{0,1:T(4,128)(2,1)} %param.22) | copy-start | bytes 3076
  219.5 41.9 %all-to-all-start.4 = ((bf16[64,72,128]{2,1,0:T(8,128)(2,1)}), bf16[64,72,128]{2,1,0:T(8,128)(2,1)S(1)}, u32[]{:S(2)}, u32[]{:S(2)}) async-start(bf16[64,72,128]{2,1,0:T(8,128)(2,1)} %bitcast.10), calls=%async_computation.4 | async-start | bytes 2359296 | tf_op jit(solution)/shard_map/combine/all_to_all | solution.py:319
Sparse Core Ops, SparseCore 0:
  37.0 46.7 all-gather.1

commit v3 on v1

--- a/solution.py
+++ b/solution.py
@@ -30,16 +30,16 @@
     return lax.ppermute(block, axis, [(i, (i + distance) % size) for i in range(size)])
 
 
-def call(kernel, out_shape, args, scratch=(), spaces=None, flops=0, moved=0):
+def call(kernel, out_shape, args, scratch=(), spaces=None, flops=0, moved=0, limit=32, made=pltpu.VMEM):
     spaces = spaces or [pltpu.VMEM] * len(args)
     return pl.pallas_call(
         kernel,
         out_shape=out_shape,
         in_specs=[pl.BlockSpec(memory_space=s) for s in spaces],
-        out_specs=jax.tree.map(lambda _: pl.BlockSpec(memory_space=pltpu.VMEM), out_shape),
+        out_specs=jax.tree.map(lambda _: pl.BlockSpec(memory_space=made), out_shape),
         scratch_shapes=list(scratch),
         cost_estimate=pl.CostEstimate(flops=flops, bytes_accessed=moved, transcendentals=0),
-        compiler_params=pltpu.CompilerParams(vmem_limit_bytes=48 * 1024 * 1024),
+        compiler_params=pltpu.CompilerParams(vmem_limit_bytes=limit * 1024 * 1024),
     )(*args)
 
 
@@ -129,55 +129,94 @@
         rows_ref[t, :, QUARTER:] = extra
 
 
-def dispatch_kernel(rows_ref, routing_ref, out_ref, flat):
+def dispatch_kernel(order_ref, rows_ref, routing_ref, out_ref, flat):
     squares = jnp.zeros((rows_ref.shape[1], 1), F32)
     for t in range(TP):
         squares += jnp.sum(rows_ref[t, :, QUARTER:].astype(F32), axis=1, keepdims=True)
     scale = lax.rsqrt(squares / D + EPSILON)
     routing = routing_ref[...]
     for t in range(TP):
-        normed = (rows_ref[t].astype(F32) * scale).astype(BF16)
+        normed = (rows_ref[order_ref[t]].astype(F32) * scale).astype(BF16)
         picked = jnp.dot(routing, normed, preferred_element_type=F32)
         for b in range(6):
             flat[pl.ds(t * 6 + b, SLOTS, stride=BLOCKS), :] = picked[:, b * 128 : (b + 1) * 128]
     out_ref[...] = flat[...].astype(BF16)
 
 
-def expert_kernel(mine_ref, other_ref, weights_ref, to_mine_ref, to_other_ref, flat, rows, w, sem):
-    copies = [pltpu.make_async_copy(weights_ref.at[t], w.at[t], sem.at[t]) for t in range(TP)]
+def pack_kernel(gate_ref, up_ref, out_ref, held, in_sems, out_sems):
+    span = QUARTER // 3
+    arriving, leaving = [], []
+    for n, ref in enumerate((gate_ref, up_ref)):
+        for k in range(3):
+            rows = pl.ds(k * span, span)
+            arriving.append(
+                pltpu.make_async_copy(ref.at[rows], held.at[n, rows], in_sems.at[3 * n + k])
+            )
+            leaving.append(
+                pltpu.make_async_copy(
+                    held.at[n, rows], out_ref.at[n, rows], out_sems.at[3 * n + k]
+                )
+            )
+    for copy in arriving:
+        copy.start()
+    for before, after in zip(arriving, leaving):
+        before.wait()
+        after.start()
+    for copy in leaving:
+        copy.wait()
+
+
+def expert_kernel(order_ref, mine_ref, other_ref, *refs):
+    sources, (to_mine_ref, to_other_ref, flat, rows, w, sems) = refs[:6], refs[6:]
+    half = QUARTER // 2
+    copies = []
+    for n in range(2):
+        for k in range(TP):
+            copies.append((sources[0].at[order_ref[k], n], w.at[n * TP + k]))
+    for k in range(3):
+        copies.append((sources[1 + k], w.at[2 * TP + k]))
+    copies.append((sources[4], w.at[2 * TP + 3, pl.ds(0, half)]))
+    copies.append((sources[5], w.at[2 * TP + 3, pl.ds(half, half)]))
+    copies = [
+        pltpu.make_async_copy(src, dst, sems.at[n]) for n, (src, dst) in enumerate(copies)
+    ]
     for copy in copies:
         copy.start()
     for n, ref in enumerate((mine_ref, other_ref)):
         flat[...] = ref[...].astype(F32)
         for b in range(BLOCKS):
-            rows[n * SLOTS : (n + 1) * SLOTS, b * 128 : (b + 1) * 128] = flat[
+            lanes = slice(b % 6 * 128, b % 6 * 128 + 128)
+            rows[b // 6, n * SLOTS : (n + 1) * SLOTS, lanes] = flat[
                 pl.ds(b, SLOTS, stride=BLOCKS), :
             ].astype(BF16)
-    gate = jnp.zeros((2 * SLOTS, QUARTER), F32)
-    up = jnp.zeros((2 * SLOTS, QUARTER), F32)
-    for t in range(TP):
-        copies[t].wait()
-        part = rows[:, t * PADDED : t * PADDED + QUARTER]
-        gate += jnp.dot(part, w[t, :QUARTER, :], preferred_element_type=F32)
-        up += jnp.dot(part, w[t, QUARTER : 2 * QUARTER, :], preferred_element_type=F32)
+    sums = []
+    for n in range(2):
+        total = jnp.zeros((2 * SLOTS, QUARTER), F32)
+        for t in range(TP):
+            copies[TP * n + t].wait()
+            total += jnp.dot(rows[t, :, :QUARTER], w[n * TP + t], preferred_element_type=F32)
+        sums.append(total)
+    gate, up = sums
     active = (gate / (1.0 + jnp.exp(-gate)) * up).astype(BF16)
+    for copy in copies[2 * TP :]:
+        copy.wait()
     for n, ref in enumerate((to_mine_ref, to_other_ref)):
         part = active[n * SLOTS : (n + 1) * SLOTS]
         for t in range(TP):
-            made = jnp.dot(part, w[t, 2 * QUARTER :, :], preferred_element_type=F32)
+            made = jnp.dot(part, w[2 * TP + t], preferred_element_type=F32)
             made = jnp.concatenate([made, jnp.zeros((SLOTS, PADDED - QUARTER), F32)], axis=1)
             for b in range(6):
                 flat[pl.ds(t * 6 + b, SLOTS, stride=BLOCKS), :] = made[:, b * 128 : (b + 1) * 128]
         ref[...] = flat[...].astype(BF16)
 
 
-def combine_kernel(back_ref, mixing_ref, out_ref, flat):
+def combine_kernel(order_ref, back_ref, mixing_ref, out_ref, flat):
     flat[...] = back_ref[...].astype(F32)
     mixing = mixing_ref[...]
     for t in range(TP):
         for b in range(6):
             part = flat[pl.ds(t * 6 + b, SLOTS, stride=BLOCKS), :].astype(BF16)
-            out_ref[t, :, b * 128 : (b + 1) * 128] = jnp.dot(
+            out_ref[order_ref[t], :, b * 128 : (b + 1) * 128] = jnp.dot(
                 mixing, part, preferred_element_type=F32
             ).astype(BF16)
 
@@ -203,14 +242,46 @@
     seq_size = lax.axis_size("y") * lax.axis_size("z") * lax.axis_size("core")
     y_size, z_size = lax.axis_size("y"), lax.axis_size("z")
 
+    order = jnp.stack([tp, (tp + 3) % TP, (tp + 1) % TP, (tp + 2) % TP]).astype(jnp.int32)
+
     with jax.named_scope("expert_weights"):
-        blocks = jnp.concatenate([w_gate, w_up, w_down], axis=0)
-        weights = lax.all_gather(blocks, "tp", axis=0, tiled=False)
+        packed = call(
+            pack_kernel,
+            jax.ShapeDtypeStruct((2, QUARTER, QUARTER), BF16),
+            (w_gate, w_up),
+            scratch=[
+                pltpu.VMEM((2, QUARTER, QUARTER), BF16),
+                pltpu.SemaphoreType.DMA((6,)),
+                pltpu.SemaphoreType.DMA((6,)),
+            ],
+            spaces=[pltpu.HBM] * 2,
+            made=pltpu.HBM,
+            limit=60,
+        )
+        gate_up = lax.all_gather(packed, "tp", axis=0, tiled=False)
+        packed, w_out, keys = lax.optimization_barrier((packed, w_out, keys))
 
     with jax.named_scope("projection_rows"):
         spread = jnp.broadcast_to(w_out[None], (z_size,) + w_out.shape)
         column = lax.all_to_all(spread, "z", 0, 0, tiled=True)
         column = column.reshape(z_size * w_out.shape[0], QUARTER)
+
+    with jax.named_scope("attention"):
+        pair = jnp.concatenate([keys, values], axis=1)
+        before = lax.ppermute(pair, SEQ, [(i, i + 1) for i in range(seq_size - 1)])
+        start = (session_start - seq_index * count + WINDOW)[:, None]
+        heads = call(
+            attention_kernel,
+            jax.ShapeDtypeStruct((2, TP, 2, count, GROUPS * HALF), BF16),
+            (queries, pair, before, start, sinks),
+            spaces=[pltpu.VMEM] * 4 + [pltpu.SMEM],
+            flops=2_000_000_000,
+            moved=2_000_000,
+            limit=24,
+        )
+        column, heads = lax.optimization_barrier((column, heads))
+
+    with jax.named_scope("projection_rows"):
         half = column.shape[0] // 2
         ahead, behind, pieces = column, column, [column]
         for _ in range(y_size // 2 - 1):
@@ -224,17 +295,6 @@
         index = jnp.stack([jnp.asarray(v, jnp.int32) for v in sources + [core]])
 
     with jax.named_scope("attention"):
-        pair = jnp.concatenate([keys, values], axis=1)
-        before = lax.ppermute(pair, SEQ, [(i, i + 1) for i in range(seq_size - 1)])
-        start = (session_start - seq_index * count + WINDOW)[:, None]
-        heads = call(
-            attention_kernel,
-            jax.ShapeDtypeStruct((2, TP, 2, count, GROUPS * HALF), BF16),
-            (queries, pair, before, start, sinks),
-            spaces=[pltpu.VMEM] * 4 + [pltpu.SMEM],
-            flops=2_000_000_000,
-            moved=2_000_000,
-        )
         heads = lax.all_to_all(
             heads.reshape(2 * TP, 2, count, GROUPS * HALF), ("core", "tp"), 0, 0, tiled=True
         )
@@ -260,6 +320,12 @@
             (residual, own, got, norm_gain[None, :]),
         )
         scaled = lax.all_to_all(scaled, "tp", 0, 0, tiled=True)
+        scaled, w_down = lax.optimization_barrier((scaled, w_down))
+
+    with jax.named_scope("expert_weights"):
+        left, right = shifted(w_down, "tp", 1), shifted(w_down, "tp", -1)
+        part = QUARTER // 2
+        far = [shifted(left[:part], "tp", 1), shifted(right[part:], "tp", -1)]
 
     with jax.named_scope("routing"):
         present = expert_ids[:, :, None] == jnp.arange(EXPERTS, dtype=jnp.int32)[None, None, :]
@@ -284,24 +350,35 @@
     block = (EXPERTS, CLASS_SLOTS * BLOCKS, 128)
     flat_shape = jax.ShapeDtypeStruct((SLOTS * BLOCKS, 128), BF16)
     with jax.named_scope("dispatch"):
-        sending = call(dispatch_kernel, flat_shape, (scaled, routing), scratch=[flat_scratch])
+        sending = call(dispatch_kernel, flat_shape, (order, scaled, routing), scratch=[flat_scratch], spaces=[pltpu.SMEM] + [pltpu.VMEM] * 2, limit=16)
         arrived = lax.all_to_all(sending.reshape(block), CHIPS, 0, 0, tiled=True)
+        arrived, left, right, far = lax.optimization_barrier((arrived, left, right, far))
         partner = shifted(arrived, "core", 1)
 
     with jax.named_scope("experts"):
         to_mine, to_other = call(
             expert_kernel,
             [flat_shape] * 2,
-            (arrived.reshape(flat_shape.shape), partner.reshape(flat_shape.shape), weights),
+            (
+                order,
+                arrived.reshape(flat_shape.shape),
+                partner.reshape(flat_shape.shape),
+                gate_up,
+                w_down,
+                left,
+                right,
+                *far,
+            ),
             scratch=[
                 flat_scratch,
-                pltpu.VMEM((2 * SLOTS, TP * PADDED), BF16),
-                pltpu.VMEM((TP, 3 * QUARTER, QUARTER), BF16),
-                pltpu.SemaphoreType.DMA((TP,)),
+                pltpu.VMEM((TP, 2 * SLOTS, PADDED), BF16),
+                pltpu.VMEM((3 * TP, QUARTER, QUARTER), BF16),
+                pltpu.SemaphoreType.DMA((13,)),
             ],
-            spaces=[pltpu.VMEM] * 2 + [pl.ANY],
+            spaces=[pltpu.SMEM] + [pltpu.VMEM] * 2 + [pltpu.HBM] * 6,
             flops=5_000_000_000,
             moved=15_000_000,
+            limit=58,
         )
         received = shifted(to_other, "core", 1)
         both = (to_mine.astype(F32) + received.astype(F32)).astype(BF16)
@@ -311,8 +388,10 @@
         mixed = call(
             combine_kernel,
             jax.ShapeDtypeStruct((TP, count, PADDED), BF16),
-            (back.reshape(flat_shape.shape), mixing),
+            (order, back.reshape(flat_shape.shape), mixing),
             scratch=[flat_scratch],
+            spaces=[pltpu.SMEM] + [pltpu.VMEM] * 2,
+            limit=16,
         )
         mixed = lax.all_to_all(mixed, "tp", 0, 0, tiled=True)
         moe = jnp.sum(mixed[:, :, :QUARTER].astype(F32), axis=0)

time: 277 us -> 284 us (1.025)
  blocking collectives: 71.5 us -> 13.1 us
  starting transfers between devices: 62.5 us -> 105 us
  waiting for transfers between devices: 67.1 us -> 103 us
  local copies, waits for them, and re-layouts: 33.3 us -> 7.97 us
  Pallas kernels: 23 us -> 32.7 us
    all_to_all x2 -> x0, blocking collectives: 59.1 us -> none  [the longest x1 34.8 us: shards(): arrived = lax.all_to_all(sending.reshape(block), CHIPS, 0, 0, tiled=True)]
    ppermute x11 -> x15, waiting for transfers between devices: 15.7 us -> 46.8 us  [shifted(): lax.ppermute(block, axis, [(i, (i + distance) % size) for i in range(size)])]
    all_to_all x0 -> x2, starting transfers between devices: none -> 25.4 us  [the longest x1 14.5 us: shards(): arrived = lax.all_to_all(sending.reshape(block), CHIPS, 0, 0, tiled=True)]
    all_gather x1 -> x0, local copies, waits for them, and re-layouts: 18.1 us -> none  [shards(): weights = lax.all_gather(blocks, 'tp', axis=0, tiled=False)]
    ppermute x11 -> x15, starting transfers between devices: 40.2 us -> 52.4 us  [shifted(): lax.ppermute(block, axis, [(i, (i + distance) % size) for i in range(size)])]
    pallas_call x6 -> x7, Pallas kernels: 23 us -> 32.7 us  [call(): pl.pallas_call(kernel, out_shape=out_shape, in_specs=[pl.BlockSpec(memory...]
    all_to_all x1, starting transfers between devices: 6.66 us -> 12 us  [shards(): back = lax.all_to_all(both.reshape(block), CHIPS, 0, 0, tiled=True)]
    concatenate x1 -> x0, local copies, waits for them, and re-layouts: 4.44 us -> none  [shards(): blocks = jnp.concatenate([w_gate, w_up, w_down], axis=0)]
  transfers between devices with their start and end apart: 16 -> 22, of which waited for: 8 -> 12; matrix products, arithmetic and copies ran while one was open for 8% -> 2% of each run, Pallas kernels for 5% -> 5%
where the time goes in v3:
time: 284 us; the launch traced here: 279 us
  starting transfers between devices  105 us (37%)
  waiting for transfers between devices  103 us (36%)
  Pallas kernels  32.7 us (12%)
  between operations  13.9 us (5%)
  blocking collectives  13.1 us (5%)
  local copies, waits for them, and re-layouts  7.97 us (3%)
  other arithmetic  3.18 us (1%)
    ppermute x15, starting transfers between devices, shifted(): lax.ppermute(block, axis, [(i, (i + distance) % size) for i in range(size)])  52.4 us
    ppermute x15, waiting for transfers between devices, shifted(): lax.ppermute(block, axis, [(i, (i + distance) % size) for i in range(size)])  46.8 us
    pallas_call x7, Pallas kernels, call(): pl.pallas_call(kernel, out_shape=out_shape, in_specs=[pl.BlockSpec(memory...  32.7 us
    all_to_all x1, waiting for transfers between devices, shards(): back = lax.all_to_all(both.reshape(block), CHIPS, 0, 0, tiled=True)  29.4 us
    all_to_all x1, waiting for transfers between devices, shards(): scaled = lax.all_to_all(scaled, 'tp', 0, 0, tiled=True)  20.3 us
    all_to_all x1, starting transfers between devices, shards(): arrived = lax.all_to_all(sending.reshape(block), CHIPS, 0, 0, tiled=True)  14.5 us
    all_to_all x1, blocking collectives, shards(): mixed = lax.all_to_all(mixed, 'tp', 0, 0, tiled=True)  13.1 us
    all_to_all x1, starting transfers between devices, shards(): back = lax.all_to_all(both.reshape(block), CHIPS, 0, 0, tiled=True)  12 us
  transfers between devices with their start and end apart: 22, of which 12 were waited for; matrix products, arithmetic and copies ran while one was open for 2% of the time, Pallas kernels for 5%

profile of v3, /device:TPU:1, one launch (start us, length us, event | category | flops | bytes accessed | tf_op | source)
XLA Modules:
  0.0 278.7 jit_solution(2027600098175463773)
XLA Ops:
  6.5 2.4 expert_weights.1
  9.0 0.0 copy-start.9
  9.0 0.0 copy-start.10
  9.0 0.0 all-gather.3.cloned.1.call-update
  9.0 0.8 copy-done.9
  9.8 0.8 broadcast_in_dim.46
  10.6 10.9 %all-to-all-start = ((bf16[8,32,720]{2,1,0:T(8,128)(2,1)}), bf16[8,32,720]{2,1,0:T(8,128)(2,1)S(1)}, u32[]{:S(2)}, u32[]{:S(2)}) async-start(bf16[8,32,720]{2,1,0:T(8,128)(2,1)} %broadcast_in_dim.46), calls=%async_computation | async-start | bytes 786432 | tf_op jit(solution)/shard_map/projection_rows/all_to_all | solution.py:266
  21.5 4.5 %collective-permute-start = (bf16[128,256]{1,0:T(8,128)(2,1)S(1)}, bf16[128,256]{1,0:T(8,128)(2,1)S(1)}, u32[]{:S(2)}, u32[]{:S(2)}) collective-permute-start(bf16[128,256]{1,0:T(8,128)(2,1)S(1)} %constant_dynamic-update-slice_fusion.own_ref), channel_id=1, source_target_pairs={{0,4},{4,8},{8,12},{12,16},{16,20},{20,24},{24,28},{28,32},{32,36}... | collective-permute-start | bytes 196616 | tf_op jit(solution)/shard_map/attention/ppermute | solution.py:271
  26.0 0.1 copy.28.start_ref
  26.1 3.5 %collective-permute-done.before_ref = bf16[128,256]{1,0:T(8,128)(2,1)S(1)} collective-permute-done((bf16[128,256]{1,0:T(8,128)(2,1)S(1)}, bf16[128,256]{1,0:T(8,128)(2,1)S(1)}, u32[]{:S(2)}, u32[]{:S(2)}) %collective-permute-start) | collective-permute-done | bytes 65568 | tf_op jit(solution)/shard_map/attention/ppermute | solution.py:271
  29.7 7.8 %attention.1 = bf16[2,4,2,128,256]{4,3,2,1,0:T(8,128)(2,1)} custom-call(bf16[128,1024]{1,0:T(8,128)(2,1)S(1)} %copy-done.4, bf16[128,256]{1,0:T(8,128)(2,1)S(1)} %constant_dynamic-update-slice_fusion.own_ref, bf16[128,256]{1,0:T(8,128)(2,1)S(1)} %collective-permute-done.before_ref, s32[128,1]{1,0:T(8,128)S(1)} %copy.28.start_ref, f32[16]{0:T(128)S(1)} %copy-done.5), custom_call_target="tpu_custom_call" | custom-call | flops 2000000000 | bytes 2000000 | tf_op jit(solution)/shard_map/attention/pallas_call | solution.py:35
  37.5 2.2 collective-permute-start.1
  39.7 4.3 %collective-permute-start.2 = (bf16[256,720]{1,0:T(8,128)(2,1)S(1)}, bf16[256,720]{1,0:T(8,128)(2,1)S(1)}, u32[]{:S(2)}, u32[]{:S(2)}) collective-permute-start(bf16[256,720]{1,0:T(8,128)(2,1)S(1)} %bitcast.27), channel_id=1, source_target_pairs={{0,448},{64,0},{128,64},{192,128},{256,192},{320,256},{384,320},{4... | collective-permute-start | bytes 1105928 | tf_op jit(solution)/shard_map/projection_rows/ppermute | solution.py:30
  44.0 6.4 %collective-permute-done.1.refs_1_ = bf16[256,720]{1,0:T(8,128)(2,1)S(1)} collective-permute-done((bf16[256,720]{1,0:T(8,128)(2,1)S(1)}, bf16[256,720]{1,0:T(8,128)(2,1)S(1)}, u32[]{:S(2)}, u32[]{:S(2)}) %collective-permute-start.1) | collective-permute-done | bytes 368672 | tf_op jit(solution)/shard_map/projection_rows/ppermute | solution.py:30
  50.4 1.9 collective-permute-start.3
  52.3 4.6 %collective-permute-start.4 = (bf16[256,720]{1,0:T(8,128)(2,1)S(1)}, bf16[256,720]{1,0:T(8,128)(2,1)}, u32[]{:S(2)}, u32[]{:S(2)}) collective-permute-start(bf16[256,720]{1,0:T(8,128)(2,1)S(1)} %collective-permute-done.2.refs_2_), channel_id=1, source_target_pairs={{0,448},{64,0},{128,64},{192,128},{256,192},{320,256},{384,320},{4... | collective-permute-start | bytes 1105928 | tf_op jit(solution)/shard_map/projection_rows/ppermute | solution.py:30
  56.9 6.7 %all-to-all-start.1 = ((bf16[8,2,128,256]{3,2,1,0:T(8,128)(2,1)}), bf16[8,2,128,256]{3,2,1,0:T(8,128)(2,1)S(1)}, u32[]{:S(2)}, u32[]{:S(2)}) async-start(bf16[8,2,128,256]{3,2,1,0:T(8,128)(2,1)} %bitcast.11), calls=%async_computation.1 | async-start | bytes 2097152 | tf_op jit(solution)/shard_map/attention/all_to_all | solution.py:298
  63.5 0.0 collective-permute-done.3.refs_3_
  63.5 1.9 collective-permute-start.5
  65.5 4.6 %collective-permute-start.6 = (bf16[256,720]{1,0:T(8,128)(2,1)}, bf16[256,720]{1,0:T(8,128)(2,1)S(1)}, u32[]{:S(2)}, u32[]{:S(2)}) collective-permute-start(bf16[256,720]{1,0:T(8,128)(2,1)} %collective-permute-done.4.refs_4_), channel_id=1, source_target_pairs={{0,448},{64,0},{128,64},{192,128},{256,192},{320,256},{384,320},{4... | collective-permute-start | bytes 1105928 | tf_op jit(solution)/shard_map/projection_rows/ppermute | solution.py:30
  70.0 5.8 %collective-permute-done.5.refs_5_ = bf16[256,720]{1,0:T(8,128)(2,1)S(1)} collective-permute-done((bf16[256,720]{1,0:T(8,128)(2,1)S(1)}, bf16[256,720]{1,0:T(8,128)(2,1)S(1)}, u32[]{:S(2)}, u32[]{:S(2)}) %collective-permute-start.5) | collective-permute-done | bytes 368672 | tf_op jit(solution)/shard_map/projection_rows/ppermute | solution.py:30
  75.9 0.7 slice.20
  76.6 1.9 collective-permute-start.7
  78.5 0.0 collective-permute-done.6.refs_6_
  78.5 0.7 slice.21
  79.2 4.6 %collective-permute-start.8 = (bf16[128,720]{1,0:T(8,128)(2,1)}, bf16[128,720]{1,0:T(8,128)(2,1)}, u32[]{:S(2)}, u32[]{:S(2)}) collective-permute-start(bf16[128,720]{1,0:T(8,128)(2,1)} %slice.21), channel_id=1, source_target_pairs={{0,448},{64,0},{128,64},{192,128},{256,192},{320,256},{384,320},{4... | collective-permute-start | bytes 552968 | tf_op jit(solution)/shard_map/projection_rows/ppermute | solution.py:30
  83.8 0.1 stack.54.index_ref
  83.9 2.8 all-to-all-done.1
  86.7 3.0 %stream.2 = (f32[128,720]{1,0:T(8,128)S(1)}, f32[128,720]{1,0:T(8,128)}) custom-call(s32[9]{0:T(128)S(1)} %stack.54.index_ref, bf16[2,8,128,256]{3,2,1,0:T(8,128)(2,1)S(1)} %bitcast.25, bf16[256,720]{1,0:T(8,128)(2,1)S(1)} %bitcast.28, bf16[256,720]{1,0:T(8,128)(2,1)S(1)} %collective-permute-done.1.refs_1_, ...), custom_call_target="tpu_custom_call" | custom-call | flops 800000000 | bytes 4000000 | tf_op jit(solution)/shard_map/stream/pallas_call | solution.py:35
  89.8 0.7 copy-done
  90.5 5.3 %collective-permute-start.9 = (f32[128,720]{1,0:T(8,128)}, f32[128,720]{1,0:T(8,128)S(1)}, u32[]{:S(2)}, u32[]{:S(2)}) collective-permute-start(f32[128,720]{1,0:T(8,128)} %get-tuple-element.27), channel_id=1, source_target_pairs={{0,4},{4,0},{1,5},{5,1},{2,6},{6,2},{3,7},{7,3},{8,12},{12,8},{9,1... | collective-permute-start | bytes 1105928 | tf_op jit(solution)/shard_map/stream/ppermute | solution.py:30
  95.8 1.1 copy.29.residual_ref
  96.9 0.4 collective-permute-done.9.got_ref
  97.3 1.0 copy-done.1
  98.3 1.1 stream.3
  99.5 4.1 %all-to-all-start.2 = ((bf16[4,128,768]{2,1,0:T(8,128)(2,1)}), bf16[4,128,768]{2,1,0:T(8,128)(2,1)S(1)}, u32[]{:S(2)}, u32[]{:S(2)}) async-start(bf16[4,128,768]{2,1,0:T(8,128)(2,1)} %get-tuple-element.29), calls=%async_computation.2 | async-start | bytes 1572864 | tf_op jit(solution)/shard_map/stream/all_to_all | solution.py:322
  103.7 0.1 copy.30
  103.8 0.2 reduce_window_sum.11
  104.0 0.1 copy.32
  104.0 0.1 pad_add_fusion.order_ref
  104.2 20.3 %all-to-all-done.2.rows_ref = bf16[4,128,768]{2,1,0:T(8,128)(2,1)S(1)} async-done(((bf16[4,128,768]{2,1,0:T(8,128)(2,1)}), bf16[4,128,768]{2,1,0:T(8,128)(2,1)S(1)}, u32[]{:S(2)}, u32[]{:S(2)}) %all-to-all-start.2) | async-done | bytes 786464 | tf_op jit(solution)/shard_map/stream/all_to_all | solution.py:322
  124.5 2.5 dispatch.1
  127.0 14.5 %all-to-all-start.3 = ((bf16[64,72,128]{2,1,0:T(8,128)(2,1)}), bf16[64,72,128]{2,1,0:T(8,128)(2,1)S(1)}, u32[]{:S(2)}, u32[]{:S(2)}) async-start(bf16[64,72,128]{2,1,0:T(8,128)(2,1)} %bitcast.17), calls=%async_computation.3 | async-start | bytes 2359296 | tf_op jit(solution)/shard_map/dispatch/all_to_all | solution.py:354
  141.5 2.2 collective-permute-start.10
  143.7 4.3 %collective-permute-start.11 = (bf16[720,720]{1,0:T(8,128)(2,1)}, bf16[720,720]{1,0:T(8,128)(2,1)S(1)}, u32[]{:S(2)}, u32[]{:S(2)}) collective-permute-start(bf16[720,720]{1,0:T(8,128)(2,1)} %refs_1_), channel_id=1, source_target_pairs={{0,3},{1,0},{2,1},{3,2},{4,7},{5,4},{6,5},{7,6},{8,11},{9,8},{10,9... | collective-permute-start | bytes 3110408 | tf_op jit(solution)/shard_map/expert_weights/ppermute | solution.py:30
  148.0 21.0 %collective-permute-done.10.refs_2_ = bf16[720,720]{1,0:T(8,128)(2,1)S(1)} collective-permute-done((bf16[720,720]{1,0:T(8,128)(2,1)}, bf16[720,720]{1,0:T(8,128)(2,1)S(1)}, u32[]{:S(2)}, u32[]{:S(2)}) %collective-permute-start.10) | collective-permute-done | bytes 1036832 | tf_op jit(solution)/shard_map/expert_weights/ppermute | solution.py:30
  169.0 1.9 collective-permute-start.12
  171.0 4.6 %collective-permute-start.13 = (bf16[360,720]{1,0:T(8,128)(2,1)S(1)}, bf16[360,720]{1,0:T(8,128)(2,1)}, u32[]{:S(2)}, u32[]{:S(2)}) collective-permute-start(bf16[360,720]{1,0:T(8,128)(2,1)S(1)} %slice.23), channel_id=1, source_target_pairs={{0,3},{1,0},{2,1},{3,2},{4,7},{5,4},{6,5},{7,6},{8,11},{9,8},{10,9... | collective-permute-start | bytes 1555208 | tf_op jit(solution)/shard_map/expert_weights/ppermute | solution.py:30
  175.6 7.9 %collective-permute-done.12.refs_4_ = bf16[360,720]{1,0:T(8,128)(2,1)S(1)} collective-permute-done((bf16[360,720]{1,0:T(8,128)(2,1)S(1)}, bf16[360,720]{1,0:T(8,128)(2,1)S(1)}, u32[]{:S(2)}, u32[]{:S(2)}) %collective-permute-start.12) | collective-permute-done | bytes 518432 | tf_op jit(solution)/shard_map/expert_weights/ppermute | solution.py:30
  183.5 0.8 copy-done.15
  184.3 0.2 collective-permute-done.13.refs_5_
  184.4 5.9 %collective-permute-start.14 = (bf16[64,72,128]{2,1,0:T(8,128)(2,1)S(1)}, bf16[64,72,128]{2,1,0:T(8,128)(2,1)}, u32[]{:S(2)}, u32[]{:S(2)}) collective-permute-start(bf16[64,72,128]{2,1,0:T(8,128)(2,1)S(1)} %all-to-all-done.3), channel_id=1, source_target_pairs={{0,4},{4,0},{1,5},{5,1},{2,6},{6,2},{3,7},{7,3},{8,12},{12,8},{9,1... | collective-permute-start | bytes 3538952 | tf_op jit(solution)/shard_map/dispatch/ppermute | solution.py:30
  190.4 2.4 collective-permute-done.14
  192.8 14.4 %experts.1 = (bf16[4608,128]{1,0:T(8,128)(2,1)}, bf16[4608,128]{1,0:T(8,128)(2,1)}) custom-call(s32[4]{0:T(128)} %copy-done.2, bf16[4608,128]{1,0:T(8,128)(2,1)} %bitcast.29, bf16[4608,128]{1,0:T(8,128)(2,1)} %bitcast.19.other_ref, bf16[4,2,720,720]{3,2,1,0:T(8,128)(2,1)} %bitcast.30, bf16[720,720]{1,0:T(8,128)(2,1)} %refs_1_, bf16[720,720]{1,0:T(8,128)(2,1)} %copy-done.7, ...), custom_call_target="tpu_custom_call" | custom-call | flops 5000000000 | bytes 15000000 | tf_op jit(solution)/shard_map/experts/pallas_call | solution.py:35
  207.2 2.3 collective-permute-start.15
  209.5 2.7 collective-permute-done.15
  212.2 2.6 add_convert_fusion
  214.8 12.0 %all-to-all-start.4 = ((bf16[64,72,128]{2,1,0:T(8,128)(2,1)}), bf16[64,72,128]{2,1,0:T(8,128)(2,1)S(1)}, u32[]{:S(2)}, u32[]{:S(2)}) async-start(bf16[64,72,128]{2,1,0:T(8,128)(2,1)} %bitcast.21), calls=%async_computation.4 | async-start | bytes 2359296 | tf_op jit(solution)/shard_map/combine/all_to_all | solution.py:387
  226.8 0.1 copy.33.mixing_ref
  226.9 29.4 %all-to-all-done.4 = bf16[64,72,128]{2,1,0:T(8,128)(2,1)S(1)} async-done(((bf16[64,72,128]{2,1,0:T(8,128)(2,1)}), bf16[64,72,128]{2,1,0:T(8,128)(2,1)S(1)}, u32[]{:S(2)}, u32[]{:S(2)}) %all-to-all-start.4) | async-done | bytes 1179680 | tf_op jit(solution)/shard_map/combine/all_to_all | solution.py:387
  256.4 1.3 combine.1
  257.8 13.1 %all_to_all.30 = bf16[4,128,768]{2,1,0:T(8,128)(2,1)S(1)} all-to-all(bf16[4,128,768]{2,1,0:T(8,128)(2,1)S(1)} %combine.1), channel_id=1, replica_groups=mesh['y'=8,'z'=8,'core'=2,'tp'=4] {'tp'}, dimensions={0} | all-to-all | bytes 1572864 | tf_op jit(solution)/shard_map/combine/all_to_all | solution.py:396
  270.9 0.1 convert_reduce_fusion
  271.0 0.8 copy.34
  (50 shorter events, 0.4 us)
Async XLA Ops:
  6.5 186.2 %all-gather.3.cloned.1.call-start = ((), (), s32[]{:S(2)}) async-start(), calls=%async_computation.6 | async-start | bytes 11059200 | tf_op jit(solution)/shard_map/expert_weights/all_gather | solution.py:261
  9.0 0.8 copy-start.9
  9.0 12.5 %copy-start.10 = (bf16[128,128]{1,0:T(8,128)(2,1)S(1)}, bf16[128,128]{1,0:T(8,128)(2,1)}, u32[]{:S(2)}) copy-start(bf16[128,128]{1,0:T(8,128)(2,1)} %param.14) | copy-start | bytes 98308
  9.8 11.7 %copy-start.11 = (bf16[128,128]{1,0:T(8,128)(2,1)S(1)}, bf16[128,128]{1,0:T(8,128)(2,1)}, u32[]{:S(2)}) copy-start(bf16[128,128]{1,0:T(8,128)(2,1)} %param.15) | copy-start | bytes 98308
  9.8 16.2 %copy-start.16 = (s32[128]{0:T(128)S(1)}, s32[128]{0:T(128)}, u32[]{:S(2)}) copy-start(s32[128]{0:T(128)} %param.17) | copy-start | bytes 1540
  9.8 19.9 %copy-start.4 = (bf16[128,1024]{1,0:T(8,128)(2,1)S(1)}, bf16[128,1024]{1,0:T(8,128)(2,1)}, u32[]{:S(2)}) copy-start(bf16[128,1024]{1,0:T(8,128)(2,1)} %q_ref.1) | copy-start | bytes 786436
  9.8 19.9 %copy-start.5 = (f32[16]{0:T(128)S(1)}, f32[16]{0:T(128)}, u32[]{:S(2)}) copy-start(f32[16]{0:T(128)} %sink_ref.1) | copy-start | bytes 196
  10.6 26.9 %all-to-all-start = ((bf16[8,32,720]{2,1,0:T(8,128)(2,1)}), bf16[8,32,720]{2,1,0:T(8,128)(2,1)S(1)}, u32[]{:S(2)}, u32[]{:S(2)}) async-start(bf16[8,32,720]{2,1,0:T(8,128)(2,1)} %broadcast_in_dim.46), calls=%async_computation | async-start | bytes 786432 | tf_op jit(solution)/shard_map/projection_rows/all_to_all | solution.py:266
  21.5 8.2 %collective-permute-start = (bf16[128,256]{1,0:T(8,128)(2,1)S(1)}, bf16[128,256]{1,0:T(8,128)(2,1)S(1)}, u32[]{:S(2)}, u32[]{:S(2)}) collective-permute-start(bf16[128,256]{1,0:T(8,128)(2,1)S(1)} %constant_dynamic-update-slice_fusion.own_ref), channel_id=1, source_target_pairs={{0,4},{4,8},{8,12},{12,16},{16,20},{20,24},{24,28},{28,32},{32,36}... | collective-permute-start | bytes 196616 | tf_op jit(solution)/shard_map/attention/ppermute | solution.py:271
  37.5 12.9 %collective-permute-start.1 = (bf16[256,720]{1,0:T(8,128)(2,1)S(1)}, bf16[256,720]{1,0:T(8,128)(2,1)S(1)}, u32[]{:S(2)}, u32[]{:S(2)}) collective-permute-start(bf16[256,720]{1,0:T(8,128)(2,1)S(1)} %bitcast.26), channel_id=1, source_target_pairs={{0,64},{64,128},{128,192},{192,256},{256,320},{320,384},{384,448},... | collective-permute-start | bytes 1105928 | tf_op jit(solution)/shard_map/projection_rows/ppermute | solution.py:30
  39.7 12.6 %collective-permute-start.2 = (bf16[256,720]{1,0:T(8,128)(2,1)S(1)}, bf16[256,720]{1,0:T(8,128)(2,1)S(1)}, u32[]{:S(2)}, u32[]{:S(2)}) collective-permute-start(bf16[256,720]{1,0:T(8,128)(2,1)S(1)} %bitcast.27), channel_id=1, source_target_pairs={{0,448},{64,0},{128,64},{192,128},{256,192},{320,256},{384,320},{4... | collective-permute-start | bytes 1105928 | tf_op jit(solution)/shard_map/projection_rows/ppermute | solution.py:30
  50.4 13.2 %collective-permute-start.3 = (bf16[256,720]{1,0:T(8,128)(2,1)S(1)}, bf16[256,720]{1,0:T(8,128)(2,1)S(1)}, u32[]{:S(2)}, u32[]{:S(2)}) collective-permute-start(bf16[256,720]{1,0:T(8,128)(2,1)S(1)} %collective-permute-done.1.refs_1_), channel_id=1, source_target_pairs={{0,64},{64,128},{128,192},{192,256},{256,320},{320,384},{384,448},... | collective-permute-start | bytes 1105928 | tf_op jit(solution)/shard_map/projection_rows/ppermute | solution.py:30
  52.3 13.2 %collective-permute-start.4 = (bf16[256,720]{1,0:T(8,128)(2,1)S(1)}, bf16[256,720]{1,0:T(8,128)(2,1)}, u32[]{:S(2)}, u32[]{:S(2)}) collective-permute-start(bf16[256,720]{1,0:T(8,128)(2,1)S(1)} %collective-permute-done.2.refs_2_), channel_id=1, source_target_pairs={{0,448},{64,0},{128,64},{192,128},{256,192},{320,256},{384,320},{4... | collective-permute-start | bytes 1105928 | tf_op jit(solution)/shard_map/projection_rows/ppermute | solution.py:30
  56.9 29.9 %all-to-all-start.1 = ((bf16[8,2,128,256]{3,2,1,0:T(8,128)(2,1)}), bf16[8,2,128,256]{3,2,1,0:T(8,128)(2,1)S(1)}, u32[]{:S(2)}, u32[]{:S(2)}) async-start(bf16[8,2,128,256]{3,2,1,0:T(8,128)(2,1)} %bitcast.11), calls=%async_computation.1 | async-start | bytes 2097152 | tf_op jit(solution)/shard_map/attention/all_to_all | solution.py:298
  63.5 12.4 %collective-permute-start.5 = (bf16[256,720]{1,0:T(8,128)(2,1)S(1)}, bf16[256,720]{1,0:T(8,128)(2,1)S(1)}, u32[]{:S(2)}, u32[]{:S(2)}) collective-permute-start(bf16[256,720]{1,0:T(8,128)(2,1)S(1)} %collective-permute-done.3.refs_3_), channel_id=1, source_target_pairs={{0,64},{64,128},{128,192},{192,256},{256,320},{320,384},{384,448},... | collective-permute-start | bytes 1105928 | tf_op jit(solution)/shard_map/projection_rows/ppermute | solution.py:30
  65.5 13.0 %collective-permute-start.6 = (bf16[256,720]{1,0:T(8,128)(2,1)}, bf16[256,720]{1,0:T(8,128)(2,1)S(1)}, u32[]{:S(2)}, u32[]{:S(2)}) collective-permute-start(bf16[256,720]{1,0:T(8,128)(2,1)} %collective-permute-done.4.refs_4_), channel_id=1, source_target_pairs={{0,448},{64,0},{128,64},{192,128},{256,192},{320,256},{384,320},{4... | collective-permute-start | bytes 1105928 | tf_op jit(solution)/shard_map/projection_rows/ppermute | solution.py:30
  76.6 10.1 %collective-permute-start.7 = (bf16[128,720]{1,0:T(8,128)(2,1)}, bf16[128,720]{1,0:T(8,128)(2,1)}, u32[]{:S(2)}, u32[]{:S(2)}) collective-permute-start(bf16[128,720]{1,0:T(8,128)(2,1)} %slice.20), channel_id=1, source_target_pairs={{0,64},{64,128},{128,192},{192,256},{256,320},{320,384},{384,448},... | collective-permute-start | bytes 552968 | tf_op jit(solution)/shard_map/projection_rows/ppermute | solution.py:30
  79.2 7.5 %collective-permute-start.8 = (bf16[128,720]{1,0:T(8,128)(2,1)}, bf16[128,720]{1,0:T(8,128)(2,1)}, u32[]{:S(2)}, u32[]{:S(2)}) collective-permute-start(bf16[128,720]{1,0:T(8,128)(2,1)} %slice.21), channel_id=1, source_target_pairs={{0,448},{64,0},{128,64},{192,128},{256,192},{320,256},{384,320},{4... | collective-permute-start | bytes 552968 | tf_op jit(solution)/shard_map/projection_rows/ppermute | solution.py:30
  86.7 10.1 %copy-start.13 = (f32[720]{0:T(1024)S(1)}, f32[720]{0:T(1024)}, u32[]{:S(2)}) copy-start(f32[720]{0:T(1024)} %param.20) | copy-start | bytes 8644
  89.8 0.7 copy-start
  90.5 6.8 %collective-permute-start.9 = (f32[128,720]{1,0:T(8,128)}, f32[128,720]{1,0:T(8,128)S(1)}, u32[]{:S(2)}, u32[]{:S(2)}) collective-permute-start(f32[128,720]{1,0:T(8,128)} %get-tuple-element.27), channel_id=1, source_target_pairs={{0,4},{4,0},{1,5},{5,1},{2,6},{6,2},{3,7},{7,3},{8,12},{12,8},{9,1... | collective-permute-start | bytes 1105928 | tf_op jit(solution)/shard_map/stream/ppermute | solution.py:30
  97.3 1.0 copy-start.1
  98.3 5.3 %copy-start.12 = (s32[128,4]{0,1:T(4,128)S(1)}, s32[128,4]{0,1:T(4,128)}, u32[]{:S(2)}) copy-start(s32[128,4]{0,1:T(4,128)} %param.21) | copy-start | bytes 6148
  99.5 25.0 %all-to-all-start.2 = ((bf16[4,128,768]{2,1,0:T(8,128)(2,1)}), bf16[4,128,768]{2,1,0:T(8,128)(2,1)S(1)}, u32[]{:S(2)}, u32[]{:S(2)}) async-start(bf16[4,128,768]{2,1,0:T(8,128)(2,1)} %get-tuple-element.29), calls=%async_computation.2 | async-start | bytes 1572864 | tf_op jit(solution)/shard_map/stream/all_to_all | solution.py:322
  104.1 22.8 %copy-start.2 = (s32[4]{0:T(128)}, s32[4]{0:T(128)S(1)}, u32[]{:S(2)}) copy-start(s32[4]{0:T(128)S(1)} %pad_add_fusion.order_ref) | copy-start | bytes 52
  127.0 57.5 %all-to-all-start.3 = ((bf16[64,72,128]{2,1,0:T(8,128)(2,1)}), bf16[64,72,128]{2,1,0:T(8,128)(2,1)S(1)}, u32[]{:S(2)}, u32[]{:S(2)}) async-start(bf16[64,72,128]{2,1,0:T(8,128)(2,1)} %bitcast.17), calls=%async_computation.3 | async-start | bytes 2359296 | tf_op jit(solution)/shard_map/dispatch/all_to_all | solution.py:354
  141.5 27.5 %collective-permute-start.10 = (bf16[720,720]{1,0:T(8,128)(2,1)}, bf16[720,720]{1,0:T(8,128)(2,1)S(1)}, u32[]{:S(2)}, u32[]{:S(2)}) collective-permute-start(bf16[720,720]{1,0:T(8,128)(2,1)} %refs_1_), channel_id=1, source_target_pairs={{0,1},{1,2},{2,3},{3,0},{4,5},{5,6},{6,7},{7,4},{8,9},{9,10},{10,1... | collective-permute-start | bytes 3110408 | tf_op jit(solution)/shard_map/expert_weights/ppermute | solution.py:30
  143.7 27.2 %collective-permute-start.11 = (bf16[720,720]{1,0:T(8,128)(2,1)}, bf16[720,720]{1,0:T(8,128)(2,1)S(1)}, u32[]{:S(2)}, u32[]{:S(2)}) collective-permute-start(bf16[720,720]{1,0:T(8,128)(2,1)} %refs_1_), channel_id=1, source_target_pairs={{0,3},{1,0},{2,1},{3,2},{4,7},{5,4},{6,5},{7,6},{8,11},{9,8},{10,9... | collective-permute-start | bytes 3110408 | tf_op jit(solution)/shard_map/expert_weights/ppermute | solution.py:30
  168.9 23.8 %copy-start.7 = (bf16[720,720]{1,0:T(8,128)(2,1)}, bf16[720,720]{1,0:T(8,128)(2,1)S(1)}, u32[]{:S(2)}) copy-start(bf16[720,720]{1,0:T(8,128)(2,1)S(1)} %collective-permute-done.10.refs_2_) | copy-start | bytes 3110404
  169.0 14.5 %collective-permute-start.12 = (bf16[360,720]{1,0:T(8,128)(2,1)S(1)}, bf16[360,720]{1,0:T(8,128)(2,1)S(1)}, u32[]{:S(2)}, u32[]{:S(2)}) collective-permute-start(bf16[360,720]{1,0:T(8,128)(2,1)S(1)} %slice.22), channel_id=1, source_target_pairs={{0,1},{1,2},{2,3},{3,0},{4,5},{5,6},{6,7},{7,4},{8,9},{9,10},{10,1... | collective-permute-start | bytes 1555208 | tf_op jit(solution)/shard_map/expert_weights/ppermute | solution.py:30
  170.9 12.5 %copy-start.8 = (bf16[720,720]{1,0:T(8,128)(2,1)}, bf16[720,720]{1,0:T(8,128)(2,1)S(1)}, u32[]{:S(2)}) copy-start(bf16[720,720]{1,0:T(8,128)(2,1)S(1)} %collective-permute-done.11.refs_3_) | copy-start | bytes 3110404
  171.0 13.5 %collective-permute-start.13 = (bf16[360,720]{1,0:T(8,128)(2,1)S(1)}, bf16[360,720]{1,0:T(8,128)(2,1)}, u32[]{:S(2)}, u32[]{:S(2)}) collective-permute-start(bf16[360,720]{1,0:T(8,128)(2,1)S(1)} %slice.23), channel_id=1, source_target_pairs={{0,3},{1,0},{2,1},{3,2},{4,7},{5,4},{6,5},{7,6},{8,11},{9,8},{10,9... | collective-permute-start | bytes 1555208 | tf_op jit(solution)/shard_map/expert_weights/ppermute | solution.py:30
  183.5 0.8 copy-start.15
  184.4 8.4 %copy-start.6 = (bf16[64,72,128]{2,1,0:T(8,128)(2,1)}, bf16[64,72,128]{2,1,0:T(8,128)(2,1)S(1)}, u32[]{:S(2)}) copy-start(bf16[64,72,128]{2,1,0:T(8,128)(2,1)S(1)} %all-to-all-done.3) | copy-start | bytes 3538948
  184.4 8.3 %collective-permute-start.14 = (bf16[64,72,128]{2,1,0:T(8,128)(2,1)S(1)}, bf16[64,72,128]{2,1,0:T(8,128)(2,1)}, u32[]{:S(2)}, u32[]{:S(2)}) collective-permute-start(bf16[64,72,128]{2,1,0:T(8,128)(2,1)S(1)} %all-to-all-done.3), channel_id=1, source_target_pairs={{0,4},{4,0},{1,5},{5,1},{2,6},{6,2},{3,7},{7,3},{8,12},{12,8},{9,1... | collective-permute-start | bytes 3538952 | tf_op jit(solution)/shard_map/dispatch/ppermute | solution.py:30
  207.2 5.0 %collective-permute-start.15 = (bf16[4608,128]{1,0:T(8,128)(2,1)}, bf16[4608,128]{1,0:T(8,128)(2,1)S(1)}, u32[]{:S(2)}, u32[]{:S(2)}) collective-permute-start(bf16[4608,128]{1,0:T(8,128)(2,1)} %get-tuple-element.38), channel_id=1, source_target_pairs={{0,4},{4,0},{1,5},{5,1},{2,6},{6,2},{3,7},{7,3},{8,12},{12,8},{9,1... | collective-permute-start | bytes 3538952 | tf_op jit(solution)/shard_map/experts/ppermute | solution.py:30
  214.8 12.0 %copy-start.14 = (bf16[128,4]{0,1:T(4,128)(2,1)S(1)}, bf16[128,4]{0,1:T(4,128)(2,1)}, u32[]{:S(2)}) copy-start(bf16[128,4]{0,1:T(4,128)(2,1)} %param.22) | copy-start | bytes 3076
  214.8 41.6 %copy-start.3 = (s32[4]{0:T(128)S(1)}, s32[4]{0:T(128)}, u32[]{:S(2)}) copy-start(s32[4]{0:T(128)} %copy-done.2) | copy-start | bytes 52
  214.8 41.6 %all-to-all-start.4 = ((bf16[64,72,128]{2,1,0:T(8,128)(2,1)}), bf16[64,72,128]{2,1,0:T(8,128)(2,1)S(1)}, u32[]{:S(2)}, u32[]{:S(2)}) async-start(bf16[64,72,128]{2,1,0:T(8,128)(2,1)} %bitcast.21), calls=%async_computation.4 | async-start | bytes 2359296 | tf_op jit(solution)/shard_map/combine/all_to_all | solution.py:387
Sparse Core Ops, SparseCore 0:
  9.5 117.4 all-gather.2

commit v4 on v3

--- a/solution.py
+++ b/solution.py
@@ -14,7 +14,8 @@
 TP = 4
 QUARTER = 720
 PADDED = 768
-BLOCKS = 24
+CHUNK = 18
+TARGETS = EXPERTS * TP
 CLASS_SLOTS = 3
 SLOTS = EXPERTS * CLASS_SLOTS
 EPSILON = 1e-05
@@ -22,7 +23,7 @@
 F32 = jnp.float32
 BF16 = jnp.bfloat16
 SEQ = ("y", "z", "core")
-CHIPS = ("y", "z")
+PLANE = ("y", "z", "tp")
 
 
 def shifted(block, axis, distance):
@@ -124,29 +125,24 @@
     low = squares - high - middle
     extra = jnp.where(lane == 0, high, jnp.where(lane == 1, middle, jnp.where(lane == 2, low, 0.0)))
     extra = extra.astype(BF16)
-    for t in range(TP):
-        rows_ref[t, :, :QUARTER] = scaled
-        rows_ref[t, :, QUARTER:] = extra
-
-
-def dispatch_kernel(order_ref, rows_ref, routing_ref, out_ref, flat):
-    squares = jnp.zeros((rows_ref.shape[1], 1), F32)
-    for t in range(TP):
-        squares += jnp.sum(rows_ref[t, :, QUARTER:].astype(F32), axis=1, keepdims=True)
-    scale = lax.rsqrt(squares / D + EPSILON)
-    routing = routing_ref[...]
-    for t in range(TP):
-        normed = (rows_ref[order_ref[t]].astype(F32) * scale).astype(BF16)
-        picked = jnp.dot(routing, normed, preferred_element_type=F32)
+    rows_ref[:, :QUARTER] = scaled
+    rows_ref[:, QUARTER:] = extra
+
+
+def dispatch_kernel(rows_ref, routing_ref, out_ref, flat):
+    picked = jnp.dot(routing_ref[...], rows_ref[...], preferred_element_type=F32)
+    for k in range(CLASS_SLOTS):
         for b in range(6):
-            flat[pl.ds(t * 6 + b, SLOTS, stride=BLOCKS), :] = picked[:, b * 128 : (b + 1) * 128]
+            flat[pl.ds(k * 6 + b, TARGETS, stride=CHUNK), :] = picked[
+                k * TARGETS : (k + 1) * TARGETS, b * 128 : (b + 1) * 128
+            ]
     out_ref[...] = flat[...].astype(BF16)
 
 
-def pack_kernel(gate_ref, up_ref, out_ref, held, in_sems, out_sems):
+def pack_kernel(gate_ref, up_ref, down_ref, out_ref, held, in_sems, out_sems):
     span = QUARTER // 3
     arriving, leaving = [], []
-    for n, ref in enumerate((gate_ref, up_ref)):
+    for n, ref in enumerate((gate_ref, up_ref, down_ref)):
         for k in range(3):
             rows = pl.ds(k * span, span)
             arriving.append(
@@ -166,36 +162,39 @@
         copy.wait()
 
 
-def expert_kernel(order_ref, mine_ref, other_ref, *refs):
-    sources, (to_mine_ref, to_other_ref, flat, rows, w, sems) = refs[:6], refs[6:]
-    half = QUARTER // 2
+def expert_kernel(
+    mine_ref, other_ref, weights_ref, to_mine_ref, to_other_ref, flat, rows, w, sems
+):
     copies = []
-    for n in range(2):
-        for k in range(TP):
-            copies.append((sources[0].at[order_ref[k], n], w.at[n * TP + k]))
-    for k in range(3):
-        copies.append((sources[1 + k], w.at[2 * TP + k]))
-    copies.append((sources[4], w.at[2 * TP + 3, pl.ds(0, half)]))
-    copies.append((sources[5], w.at[2 * TP + 3, pl.ds(half, half)]))
-    copies = [
-        pltpu.make_async_copy(src, dst, sems.at[n]) for n, (src, dst) in enumerate(copies)
-    ]
-    for copy in copies:
-        copy.start()
+    for n in range(3):
+        for t in range(TP):
+            copies.append(
+                pltpu.make_async_copy(weights_ref.at[t, n], w.at[n * TP + t], sems.at[n * TP + t])
+            )
+            copies[-1].start()
+    squares = []
     for n, ref in enumerate((mine_ref, other_ref)):
         flat[...] = ref[...].astype(F32)
-        for b in range(BLOCKS):
-            lanes = slice(b % 6 * 128, b % 6 * 128 + 128)
-            rows[b // 6, n * SLOTS : (n + 1) * SLOTS, lanes] = flat[
-                pl.ds(b, SLOTS, stride=BLOCKS), :
-            ].astype(BF16)
+        for k in range(CLASS_SLOTS):
+            part = slice(n * SLOTS + k * EXPERTS, n * SLOTS + (k + 1) * EXPERTS)
+            total = jnp.zeros((EXPERTS, 1), F32)
+            for t in range(TP):
+                for b in range(6):
+                    piece = flat[pl.ds(t * CHUNK + k * 6 + b, EXPERTS, stride=TP * CHUNK), :]
+                    rows[t, part, b * 128 : (b + 1) * 128] = piece.astype(BF16)
+                lane = lax.broadcasted_iota(jnp.int32, piece.shape, 1)
+                total += jnp.sum(
+                    jnp.where(lane >= QUARTER - 5 * 128, piece, 0.0), axis=1, keepdims=True
+                )
+            squares.append(total)
+    scale = lax.rsqrt(jnp.concatenate(squares, axis=0) / D + EPSILON)
     sums = []
     for n in range(2):
         total = jnp.zeros((2 * SLOTS, QUARTER), F32)
         for t in range(TP):
             copies[TP * n + t].wait()
             total += jnp.dot(rows[t, :, :QUARTER], w[n * TP + t], preferred_element_type=F32)
-        sums.append(total)
+        sums.append(total * scale)
     gate, up = sums
     active = (gate / (1.0 + jnp.exp(-gate)) * up).astype(BF16)
     for copy in copies[2 * TP :]:
@@ -205,20 +204,26 @@
         for t in range(TP):
             made = jnp.dot(part, w[2 * TP + t], preferred_element_type=F32)
             made = jnp.concatenate([made, jnp.zeros((SLOTS, PADDED - QUARTER), F32)], axis=1)
-            for b in range(6):
-                flat[pl.ds(t * 6 + b, SLOTS, stride=BLOCKS), :] = made[:, b * 128 : (b + 1) * 128]
+            for k in range(CLASS_SLOTS):
+                for b in range(6):
+                    flat[pl.ds(t * CHUNK + k * 6 + b, EXPERTS, stride=TP * CHUNK), :] = made[
+                        k * EXPERTS : (k + 1) * EXPERTS, b * 128 : (b + 1) * 128
+                    ]
         ref[...] = flat[...].astype(BF16)
 
 
-def combine_kernel(order_ref, back_ref, mixing_ref, out_ref, flat):
+def combine_kernel(back_ref, mixing_ref, stream_ref, out_ref, flat):
     flat[...] = back_ref[...].astype(F32)
-    mixing = mixing_ref[...]
-    for t in range(TP):
-        for b in range(6):
-            part = flat[pl.ds(t * 6 + b, SLOTS, stride=BLOCKS), :].astype(BF16)
-            out_ref[order_ref[t], :, b * 128 : (b + 1) * 128] = jnp.dot(
-                mixing, part, preferred_element_type=F32
-            ).astype(BF16)
+    for b in range(6):
+        total = jnp.zeros((out_ref.shape[0], 128), F32)
+        for k in range(CLASS_SLOTS):
+            part = flat[pl.ds(k * 6 + b, TARGETS, stride=CHUNK), :].astype(BF16)
+            total += jnp.dot(
+                mixing_ref[:, k * TARGETS : (k + 1) * TARGETS], part, preferred_element_type=F32
+            )
+        width = min(128, QUARTER - b * 128)
+        lanes = slice(b * 128, b * 128 + width)
+        out_ref[:, lanes] = (stream_ref[:, lanes] + total[:, :width]).astype(BF16)
 
 
 def shards(
@@ -242,23 +247,21 @@
     seq_size = lax.axis_size("y") * lax.axis_size("z") * lax.axis_size("core")
     y_size, z_size = lax.axis_size("y"), lax.axis_size("z")
 
-    order = jnp.stack([tp, (tp + 3) % TP, (tp + 1) % TP, (tp + 2) % TP]).astype(jnp.int32)
-
     with jax.named_scope("expert_weights"):
         packed = call(
             pack_kernel,
-            jax.ShapeDtypeStruct((2, QUARTER, QUARTER), BF16),
-            (w_gate, w_up),
+            jax.ShapeDtypeStruct((3, QUARTER, QUARTER), BF16),
+            (w_gate, w_up, w_down),
             scratch=[
-                pltpu.VMEM((2, QUARTER, QUARTER), BF16),
-                pltpu.SemaphoreType.DMA((6,)),
-                pltpu.SemaphoreType.DMA((6,)),
+                pltpu.VMEM((3, QUARTER, QUARTER), BF16),
+                pltpu.SemaphoreType.DMA((9,)),
+                pltpu.SemaphoreType.DMA((9,)),
             ],
-            spaces=[pltpu.HBM] * 2,
+            spaces=[pltpu.HBM] * 3,
             made=pltpu.HBM,
             limit=60,
         )
-        gate_up = lax.all_gather(packed, "tp", axis=0, tiled=False)
+        weights = lax.all_gather(packed, "tp", axis=0, tiled=False)
         packed, w_out, keys = lax.optimization_barrier((packed, w_out, keys))
 
     with jax.named_scope("projection_rows"):
@@ -315,27 +318,18 @@
             stream_kernel,
             [
                 jax.ShapeDtypeStruct((count, QUARTER), F32),
-                jax.ShapeDtypeStruct((TP, count, PADDED), BF16),
+                jax.ShapeDtypeStruct((count, PADDED), BF16),
             ],
             (residual, own, got, norm_gain[None, :]),
         )
-        scaled = lax.all_to_all(scaled, "tp", 0, 0, tiled=True)
-        scaled, w_down = lax.optimization_barrier((scaled, w_down))
-
-    with jax.named_scope("expert_weights"):
-        left, right = shifted(w_down, "tp", 1), shifted(w_down, "tp", -1)
-        part = QUARTER // 2
-        far = [shifted(left[:part], "tp", 1), shifted(right[part:], "tp", -1)]
 
     with jax.named_scope("routing"):
         present = expert_ids[:, :, None] == jnp.arange(EXPERTS, dtype=jnp.int32)[None, None, :]
         per_row = jnp.sum(present.astype(jnp.int32), axis=1)
         earlier = jnp.cumsum(per_row, axis=0) - per_row
         position = jnp.sum(jnp.where(present, earlier[:, None, :], 0), axis=2)
-        target = jnp.where(
-            position % TP == tp, expert_ids * CLASS_SLOTS + position // TP, -1
-        )
-        slots = jnp.arange(SLOTS, dtype=jnp.int32)
+        target = (position // TP) * TARGETS + expert_ids * TP + position % TP
+        slots = jnp.arange(CLASS_SLOTS * TARGETS, dtype=jnp.int32)
         routing = jnp.sum((slots[:, None, None] == target[None]).astype(BF16), axis=2)
         mixing = jnp.sum(
             jnp.where(
@@ -346,56 +340,48 @@
             axis=2,
         )
 
-    flat_scratch = pltpu.VMEM((SLOTS * BLOCKS, 128), F32)
-    block = (EXPERTS, CLASS_SLOTS * BLOCKS, 128)
-    flat_shape = jax.ShapeDtypeStruct((SLOTS * BLOCKS, 128), BF16)
+    flat_scratch = pltpu.VMEM((TARGETS * CHUNK, 128), F32)
+    flat_shape = jax.ShapeDtypeStruct((TARGETS * CHUNK, 128), BF16)
+
+    def exchanged(block):
+        block = block.reshape(TARGETS, CHUNK // 2, 2, 128)
+        return lax.all_to_all(block, PLANE, 0, 0, tiled=True).reshape(flat_shape.shape)
+
     with jax.named_scope("dispatch"):
-        sending = call(dispatch_kernel, flat_shape, (order, scaled, routing), scratch=[flat_scratch], spaces=[pltpu.SMEM] + [pltpu.VMEM] * 2, limit=16)
-        arrived = lax.all_to_all(sending.reshape(block), CHIPS, 0, 0, tiled=True)
-        arrived, left, right, far = lax.optimization_barrier((arrived, left, right, far))
+        sending = call(
+            dispatch_kernel, flat_shape, (scaled, routing), scratch=[flat_scratch], limit=16
+        )
+        arrived = exchanged(sending)
         partner = shifted(arrived, "core", 1)
 
     with jax.named_scope("experts"):
         to_mine, to_other = call(
             expert_kernel,
             [flat_shape] * 2,
-            (
-                order,
-                arrived.reshape(flat_shape.shape),
-                partner.reshape(flat_shape.shape),
-                gate_up,
-                w_down,
-                left,
-                right,
-                *far,
-            ),
+            (arrived, partner, weights),
             scratch=[
                 flat_scratch,
                 pltpu.VMEM((TP, 2 * SLOTS, PADDED), BF16),
                 pltpu.VMEM((3 * TP, QUARTER, QUARTER), BF16),
-                pltpu.SemaphoreType.DMA((13,)),
+                pltpu.SemaphoreType.DMA((3 * TP,)),
             ],
-            spaces=[pltpu.SMEM] + [pltpu.VMEM] * 2 + [pltpu.HBM] * 6,
+            spaces=[pltpu.VMEM] * 2 + [pltpu.HBM],
             flops=5_000_000_000,
             moved=15_000_000,
-            limit=58,
+            limit=48,
         )
         received = shifted(to_other, "core", 1)
         both = (to_mine.astype(F32) + received.astype(F32)).astype(BF16)
 
     with jax.named_scope("combine"):
-        back = lax.all_to_all(both.reshape(block), CHIPS, 0, 0, tiled=True)
-        mixed = call(
+        back = exchanged(both)
+        return call(
             combine_kernel,
-            jax.ShapeDtypeStruct((TP, count, PADDED), BF16),
-            (order, back.reshape(flat_shape.shape), mixing),
+            jax.ShapeDtypeStruct((count, QUARTER), BF16),
+            (back, mixing, stream),
             scratch=[flat_scratch],
-            spaces=[pltpu.SMEM] + [pltpu.VMEM] * 2,
             limit=16,
         )
-        mixed = lax.all_to_all(mixed, "tp", 0, 0, tiled=True)
-        moe = jnp.sum(mixed[:, :, :QUARTER].astype(F32), axis=0)
-        return (stream + moe).astype(BF16)
 
 
 def solution(mesh):

time: 284 us -> 248 us (0.87); the launches traced: 279 us -> 246 us
  waiting for transfers between devices: 103 us -> 65.2 us
  blocking collectives: 13.1 us -> 49.8 us
  starting transfers between devices: 105 us -> 79.3 us
  Pallas kernels: 32.7 us -> 27.9 us
    all_to_all x1, blocking collectives: 13.1 us -> 49.8 us  [exchanged(): lax.all_to_all(block, PLANE, 0, 0, tiled=True).reshape(flat_shape.shape)]
    ppermute x15 -> x11, waiting for transfers between devices: 46.8 us -> 21.3 us  [shifted(): lax.ppermute(block, axis, [(i, (i + distance) % size) for i in range(size)])]
    all_to_all x3 -> x1, waiting for transfers between devices: 49.7 us -> 31.1 us  [exchanged(): lax.all_to_all(block, PLANE, 0, 0, tiled=True).reshape(flat_shape.shape)]
    ppermute x15 -> x11, starting transfers between devices: 52.4 us -> 38 us  [shifted(): lax.ppermute(block, axis, [(i, (i + distance) % size) for i in range(size)])]
    all_to_all x3 -> x1, starting transfers between devices: 30.6 us -> 18.9 us  [exchanged(): lax.all_to_all(block, PLANE, 0, 0, tiled=True).reshape(flat_shape.shape)]
    all_gather x1, waiting for transfers between devices: 0.01 us -> 9.26 us  [shards(): weights = lax.all_gather(packed, 'tp', axis=0, tiled=False)]
    pallas_call x7, Pallas kernels: 32.7 us -> 27.9 us  [call(): pl.pallas_call(kernel, out_shape=out_shape, in_specs=[pl.BlockSpec(memory...]
  transfers between devices with their start and end apart: 22 -> 16, of which waited for: 12 -> 9; matrix products, arithmetic and copies ran while one was open for 2% -> 2% of each run, Pallas kernels for 5% -> 5%
where the time goes in v4:
time: 248 us; the launch traced here: 246 us
  starting transfers between devices  79.3 us (32%)
  waiting for transfers between devices  65.2 us (26%)
  blocking collectives  49.8 us (20%)
  Pallas kernels  27.9 us (11%)
  between operations  13.8 us (6%)
  local copies, waits for them, and re-layouts  7.79 us (3%)
  other arithmetic  2.64 us (1%)
    all_to_all x1, blocking collectives, exchanged(): lax.all_to_all(block, PLANE, 0, 0, tiled=True).reshape(flat_shape.shape)  49.8 us
    ppermute x11, starting transfers between devices, shifted(): lax.ppermute(block, axis, [(i, (i + distance) % size) for i in range(size)])  38 us
    all_to_all x1, waiting for transfers between devices, exchanged(): lax.all_to_all(block, PLANE, 0, 0, tiled=True).reshape(flat_shape.shape)  31.1 us
    pallas_call x7, Pallas kernels, call(): pl.pallas_call(kernel, out_shape=out_shape, in_specs=[pl.BlockSpec(memory...  27.9 us
    ppermute x11, waiting for transfers between devices, shifted(): lax.ppermute(block, axis, [(i, (i + distance) % size) for i in range(size)])  21.3 us
    all_to_all x1, starting transfers between devices, exchanged(): lax.all_to_all(block, PLANE, 0, 0, tiled=True).reshape(flat_shape.shape)  18.9 us
    all_to_all x1, starting transfers between devices, shards(): column = lax.all_to_all(spread, 'z', 0, 0, tiled=True)  10.9 us
    all_gather x1, waiting for transfers between devices, shards(): weights = lax.all_gather(packed, 'tp', axis=0, tiled=False)  9.26 us
  transfers between devices with their start and end apart: 16, of which 9 were waited for; matrix products, arithmetic and copies ran while one was open for 2% of the time, Pallas kernels for 5%

profile of v4, /device:TPU:1, one launch (start us, length us, event | category | flops | bytes accessed | tf_op | source)
XLA Modules:
  0.0 246.5 jit_solution(14129734888019914009)
XLA Ops:
  6.5 0.0 all-gather.3.cloned.1.call-start
  6.5 2.8 %expert_weights.1 = bf16[3,720,720]{2,1,0:T(8,128)(2,1)} custom-call(bf16[720,720]{1,0:T(8,128)(2,1)} %gate_ref.1, bf16[720,720]{1,0:T(8,128)(2,1)} %up_ref.1, bf16[720,720]{1,0:T(8,128)(2,1)} %down_ref.1), custom_call_target="tpu_custom_call" | custom-call | tf_op jit(solution)/shard_map/expert_weights/pallas_call | solution.py:36
  9.4 0.0 copy-start.4
  9.4 0.0 all-gather.3.cloned.1.call-update
  9.4 0.8 copy-done.4
  10.2 0.0 copy-start.3
  10.2 0.8 broadcast_in_dim.44
  11.0 10.9 %all-to-all-start = ((bf16[8,32,720]{2,1,0:T(8,128)(2,1)}), bf16[8,32,720]{2,1,0:T(8,128)(2,1)S(1)}, u32[]{:S(2)}, u32[]{:S(2)}) async-start(bf16[8,32,720]{2,1,0:T(8,128)(2,1)} %broadcast_in_dim.44), calls=%async_computation | async-start | bytes 786432 | tf_op jit(solution)/shard_map/projection_rows/all_to_all | solution.py:269
  21.8 0.0 copy-done.5
  21.9 0.0 copy-done.6
  21.9 4.5 %collective-permute-start = (bf16[128,256]{1,0:T(8,128)(2,1)S(1)}, bf16[128,256]{1,0:T(8,128)(2,1)S(1)}, u32[]{:S(2)}, u32[]{:S(2)}) collective-permute-start(bf16[128,256]{1,0:T(8,128)(2,1)S(1)} %constant_dynamic-update-slice_fusion.own_ref), channel_id=1, source_target_pairs={{0,4},{4,8},{8,12},{12,16},{16,20},{20,24},{24,28},{28,32},{32,36}... | collective-permute-start | bytes 196616 | tf_op jit(solution)/shard_map/attention/ppermute | solution.py:274
  26.4 0.1 copy.28.start_ref
  26.5 3.5 %collective-permute-done.before_ref = bf16[128,256]{1,0:T(8,128)(2,1)S(1)} collective-permute-done((bf16[128,256]{1,0:T(8,128)(2,1)S(1)}, bf16[128,256]{1,0:T(8,128)(2,1)S(1)}, u32[]{:S(2)}, u32[]{:S(2)}) %collective-permute-start) | collective-permute-done | bytes 65568 | tf_op jit(solution)/shard_map/attention/ppermute | solution.py:274
  30.1 0.0 copy-done.3
  30.1 7.8 %attention.1 = bf16[2,4,2,128,256]{4,3,2,1,0:T(8,128)(2,1)} custom-call(bf16[128,1024]{1,0:T(8,128)(2,1)S(1)} %copy-done.2, bf16[128,256]{1,0:T(8,128)(2,1)S(1)} %constant_dynamic-update-slice_fusion.own_ref, bf16[128,256]{1,0:T(8,128)(2,1)S(1)} %collective-permute-done.before_ref, s32[128,1]{1,0:T(8,128)S(1)} %copy.28.start_ref, f32[16]{0:T(128)S(1)} %copy-done.3), custom_call_target="tpu_custom_call" | custom-call | flops 2000000000 | bytes 2000000 | tf_op jit(solution)/shard_map/attention/pallas_call | solution.py:36
  37.9 0.0 all-to-all-done
  37.9 4.1 %collective-permute-start.2 = (bf16[256,720]{1,0:T(8,128)(2,1)S(1)}, bf16[256,720]{1,0:T(8,128)(2,1)S(1)}, u32[]{:S(2)}, u32[]{:S(2)}) collective-permute-start(bf16[256,720]{1,0:T(8,128)(2,1)S(1)} %bitcast.22), channel_id=1, source_target_pairs={{0,448},{64,0},{128,64},{192,128},{256,192},{320,256},{384,320},{4... | collective-permute-start | bytes 1105928 | tf_op jit(solution)/shard_map/projection_rows/ppermute | solution.py:31
  42.0 1.9 collective-permute-start.1
  43.9 6.4 %collective-permute-done.2.refs_2_ = bf16[256,720]{1,0:T(8,128)(2,1)S(1)} collective-permute-done((bf16[256,720]{1,0:T(8,128)(2,1)S(1)}, bf16[256,720]{1,0:T(8,128)(2,1)S(1)}, u32[]{:S(2)}, u32[]{:S(2)}) %collective-permute-start.2) | collective-permute-done | bytes 368672 | tf_op jit(solution)/shard_map/projection_rows/ppermute | solution.py:31
  50.3 3.8 %collective-permute-start.4 = (bf16[256,720]{1,0:T(8,128)(2,1)S(1)}, bf16[256,720]{1,0:T(8,128)(2,1)S(1)}, u32[]{:S(2)}, u32[]{:S(2)}) collective-permute-start(bf16[256,720]{1,0:T(8,128)(2,1)S(1)} %collective-permute-done.2.refs_2_), channel_id=1, source_target_pairs={{0,448},{64,0},{128,64},{192,128},{256,192},{320,256},{384,320},{4... | collective-permute-start | bytes 1105928 | tf_op jit(solution)/shard_map/projection_rows/ppermute | solution.py:31
  54.1 0.0 collective-permute-done.1.refs_1_
  54.1 1.9 collective-permute-start.3
  56.1 0.0 copy-start.7
  56.1 7.1 %all-to-all-start.1 = ((bf16[8,2,128,256]{3,2,1,0:T(8,128)(2,1)}), bf16[8,2,128,256]{3,2,1,0:T(8,128)(2,1)S(1)}, u32[]{:S(2)}, u32[]{:S(2)}) async-start(bf16[8,2,128,256]{3,2,1,0:T(8,128)(2,1)} %bitcast.11), calls=%async_computation.1 | async-start | bytes 2097152 | tf_op jit(solution)/shard_map/attention/all_to_all | solution.py:301
  63.2 0.0 collective-permute-done.4.refs_4_
  63.2 4.8 %collective-permute-start.6 = (bf16[256,720]{1,0:T(8,128)(2,1)S(1)}, bf16[256,720]{1,0:T(8,128)(2,1)S(1)}, u32[]{:S(2)}, u32[]{:S(2)}) collective-permute-start(bf16[256,720]{1,0:T(8,128)(2,1)S(1)} %collective-permute-done.4.refs_4_), channel_id=1, source_target_pairs={{0,448},{64,0},{128,64},{192,128},{256,192},{320,256},{384,320},{4... | collective-permute-start | bytes 1105928 | tf_op jit(solution)/shard_map/projection_rows/ppermute | solution.py:31
  68.0 0.0 collective-permute-done.3.refs_3_
  68.0 1.9 collective-permute-start.5
  70.0 5.7 %collective-permute-done.6.refs_6_ = bf16[256,720]{1,0:T(8,128)(2,1)S(1)} collective-permute-done((bf16[256,720]{1,0:T(8,128)(2,1)S(1)}, bf16[256,720]{1,0:T(8,128)(2,1)S(1)}, u32[]{:S(2)}, u32[]{:S(2)}) %collective-permute-start.6) | collective-permute-done | bytes 368672 | tf_op jit(solution)/shard_map/projection_rows/ppermute | solution.py:31
  75.7 0.7 slice.9
  76.4 5.4 %collective-permute-start.8 = (bf16[128,720]{1,0:T(8,128)(2,1)}, bf16[128,720]{1,0:T(8,128)(2,1)}, u32[]{:S(2)}, u32[]{:S(2)}) collective-permute-start(bf16[128,720]{1,0:T(8,128)(2,1)} %slice.9), channel_id=1, source_target_pairs={{0,448},{64,0},{128,64},{192,128},{256,192},{320,256},{384,320},{4... | collective-permute-start | bytes 552968 | tf_op jit(solution)/shard_map/projection_rows/ppermute | solution.py:31
  81.8 0.0 collective-permute-done.5.refs_5_
  81.8 0.7 slice.8
  82.5 1.9 collective-permute-start.7
  84.5 0.1 copy.30
  84.6 0.2 reduce_window_sum.11
  84.8 0.6 sub.33
  85.4 0.9 copy.32
  86.4 0.1 stack.39.index_ref
  86.5 0.0 all-to-all-done.1
  86.5 0.0 collective-permute-done.8.refs_8_
  86.5 4.2 %collective-permute-done.7.refs_7_ = bf16[128,720]{1,0:T(8,128)(2,1)} collective-permute-done((bf16[128,720]{1,0:T(8,128)(2,1)}, bf16[128,720]{1,0:T(8,128)(2,1)}, u32[]{:S(2)}, u32[]{:S(2)}) %collective-permute-start.7) | collective-permute-done | bytes 184352 | tf_op jit(solution)/shard_map/projection_rows/ppermute | solution.py:31
  90.7 3.0 %stream.2 = (f32[128,720]{1,0:T(8,128)S(1)}, f32[128,720]{1,0:T(8,128)}) custom-call(s32[9]{0:T(128)S(1)} %stack.39.index_ref, bf16[2,8,128,256]{3,2,1,0:T(8,128)(2,1)S(1)} %bitcast.21, bf16[256,720]{1,0:T(8,128)(2,1)S(1)} %bitcast.24, bf16[256,720]{1,0:T(8,128)(2,1)S(1)} %collective-permute-done.1.refs_1_, ...), custom_call_target="tpu_custom_call" | custom-call | flops 800000000 | bytes 4000000 | tf_op jit(solution)/shard_map/stream/pallas_call | solution.py:36
  93.8 0.7 copy-done
  94.5 4.5 %collective-permute-start.9 = (f32[128,720]{1,0:T(8,128)}, f32[128,720]{1,0:T(8,128)S(1)}, u32[]{:S(2)}, u32[]{:S(2)}) collective-permute-start(f32[128,720]{1,0:T(8,128)} %get-tuple-element.20), channel_id=1, source_target_pairs={{0,4},{4,0},{1,5},{5,1},{2,6},{6,2},{3,7},{7,3},{8,12},{12,8},{9,1... | collective-permute-start | bytes 1105928 | tf_op jit(solution)/shard_map/stream/ppermute | solution.py:31
  99.1 1.1 copy.29.residual_ref
  100.2 0.2 fusion.3.routing_ref
  100.4 0.2 collective-permute-done.9.got_ref
  100.6 1.0 copy-done.1
  101.6 0.2 stream.3
  101.8 0.5 dispatch.1
  102.4 49.8 %all_to_all.20 = bf16[256,9,2,128]{3,2,1,0:T(2,128)(2,1)S(1)} all-to-all(bf16[256,9,2,128]{3,2,1,0:T(2,128)(2,1)S(1)} %bitcast.19), channel_id=1, replica_groups=mesh['y'=8,'z'=8,'core'=2,'tp'=4] {'y','z','tp'}, dimensions={0} | all-to-all | bytes 2359296 | tf_op jit(solution)/shard_map/dispatch/all_to_all | solution.py:348
  152.2 5.0 %collective-permute-start.10 = (bf16[4608,128]{1,0:T(8,128)(2,1)S(1)}, bf16[4608,128]{1,0:T(8,128)(2,1)S(1)}, u32[]{:S(2)}, u32[]{:S(2)}) collective-permute-start(bf16[4608,128]{1,0:T(8,128)(2,1)S(1)} %bitcast.25), channel_id=1, source_target_pairs={{0,4},{4,0},{1,5},{5,1},{2,6},{6,2},{3,7},{7,3},{8,12},{12,8},{9,1... | collective-permute-start | bytes 3538952 | tf_op jit(solution)/shard_map/dispatch/ppermute | solution.py:31
  157.2 2.3 collective-permute-done.10.other_ref
  159.5 9.3 %all-gather.3.cloned.1.call-done = bf16[12,720,720]{2,1,0:T(8,128)(2,1)} async-done(((bf16[3,720,720]{2,1,0:T(8,128)(2,1)}), bf16[12,720,720]{2,1,0:T(8,128)(2,1)}) %all-gather.3.cloned.1.call-update) | async-done | bytes 12441616 | tf_op jit(solution)/shard_map/expert_weights/all_gather | solution.py:264
  168.7 12.9 %experts.1 = (bf16[4608,128]{1,0:T(8,128)(2,1)S(1)}, bf16[4608,128]{1,0:T(8,128)(2,1)S(1)}) custom-call(bf16[4608,128]{1,0:T(8,128)(2,1)S(1)} %bitcast.26, bf16[4608,128]{1,0:T(8,128)(2,1)S(1)} %collective-permute-done.10.other_ref, bf16[4,3,720,720]{3,2,1,0:T(8,128)(2,1)} %bitcast.27), custom_call_target="tpu_custom_call" | custom-call | flops 5000000000 | bytes 15000000 | tf_op jit(solution)/shard_map/experts/pallas_call | solution.py:36
  181.6 2.6 %collective-permute-start.11 = (bf16[4608,128]{1,0:T(8,128)(2,1)S(1)}, bf16[4608,128]{1,0:T(8,128)(2,1)S(1)}, u32[]{:S(2)}, u32[]{:S(2)}) collective-permute-start(bf16[4608,128]{1,0:T(8,128)(2,1)S(1)} %get-tuple-element.23), channel_id=1, source_target_pairs={{0,4},{4,0},{1,5},{5,1},{2,6},{6,2},{3,7},{7,3},{8,12},{12,8},{9,1... | collective-permute-start | bytes 3538952 | tf_op jit(solution)/shard_map/experts/ppermute | solution.py:31
  184.2 2.5 collective-permute-done.11
  186.7 1.4 add_convert_fusion
  188.0 18.9 %all-to-all-start.3 = ((bf16[256,9,2,128]{3,2,1,0:T(2,128)(2,1)}), bf16[256,9,2,128]{3,2,1,0:T(2,128)(2,1)S(1)}, u32[]{:S(2)}, u32[]{:S(2)}) async-start(bf16[256,9,2,128]{3,2,1,0:T(2,128)(2,1)} %bitcast.16), calls=%async_computation.3 | async-start | bytes 2359296 | tf_op jit(solution)/shard_map/combine/all_to_all | solution.py:348
  206.9 0.2 fusion.2.mixing_ref
  207.1 31.1 %all-to-all-done.3 = bf16[256,9,2,128]{3,2,1,0:T(2,128)(2,1)S(1)} async-done(((bf16[256,9,2,128]{3,2,1,0:T(2,128)(2,1)}), bf16[256,9,2,128]{3,2,1,0:T(2,128)(2,1)S(1)}, u32[]{:S(2)}, u32[]{:S(2)}) %all-to-all-start.3) | async-done | bytes 1179680 | tf_op jit(solution)/shard_map/combine/all_to_all | solution.py:348
  238.2 0.6 combine.1
  238.8 0.8 copy.33
  (20 shorter events, 0.1 us)
Async XLA Ops:
  6.5 162.2 %all-gather.3.cloned.1.call-start = ((), (), s32[]{:S(2)}) async-start(), calls=%async_computation.4 | async-start | bytes 16588800 | tf_op jit(solution)/shard_map/expert_weights/all_gather | solution.py:264
  9.4 0.8 copy-start.4
  10.2 11.7 %copy-start.5 = (bf16[128,128]{1,0:T(8,128)(2,1)S(1)}, bf16[128,128]{1,0:T(8,128)(2,1)}, u32[]{:S(2)}) copy-start(bf16[128,128]{1,0:T(8,128)(2,1)} %param.14) | copy-start | bytes 98308
  10.2 11.7 %copy-start.6 = (bf16[128,128]{1,0:T(8,128)(2,1)S(1)}, bf16[128,128]{1,0:T(8,128)(2,1)}, u32[]{:S(2)}) copy-start(bf16[128,128]{1,0:T(8,128)(2,1)} %param.15) | copy-start | bytes 98308
  10.2 16.2 %copy-start.10 = (s32[128]{0:T(128)S(1)}, s32[128]{0:T(128)}, u32[]{:S(2)}) copy-start(s32[128]{0:T(128)} %param.17) | copy-start | bytes 1540
  10.2 19.9 %copy-start.2 = (bf16[128,1024]{1,0:T(8,128)(2,1)S(1)}, bf16[128,1024]{1,0:T(8,128)(2,1)}, u32[]{:S(2)}) copy-start(bf16[128,1024]{1,0:T(8,128)(2,1)} %q_ref.1) | copy-start | bytes 786436
  10.2 19.9 %copy-start.3 = (f32[16]{0:T(128)S(1)}, f32[16]{0:T(128)}, u32[]{:S(2)}) copy-start(f32[16]{0:T(128)} %sink_ref.1) | copy-start | bytes 196
  11.0 26.9 %all-to-all-start = ((bf16[8,32,720]{2,1,0:T(8,128)(2,1)}), bf16[8,32,720]{2,1,0:T(8,128)(2,1)S(1)}, u32[]{:S(2)}, u32[]{:S(2)}) async-start(bf16[8,32,720]{2,1,0:T(8,128)(2,1)} %broadcast_in_dim.44), calls=%async_computation | async-start | bytes 786432 | tf_op jit(solution)/shard_map/projection_rows/all_to_all | solution.py:269
  21.9 8.2 %collective-permute-start = (bf16[128,256]{1,0:T(8,128)(2,1)S(1)}, bf16[128,256]{1,0:T(8,128)(2,1)S(1)}, u32[]{:S(2)}, u32[]{:S(2)}) collective-permute-start(bf16[128,256]{1,0:T(8,128)(2,1)S(1)} %constant_dynamic-update-slice_fusion.own_ref), channel_id=1, source_target_pairs={{0,4},{4,8},{8,12},{12,16},{16,20},{20,24},{24,28},{28,32},{32,36}... | collective-permute-start | bytes 196616 | tf_op jit(solution)/shard_map/attention/ppermute | solution.py:274
  37.9 12.4 %collective-permute-start.2 = (bf16[256,720]{1,0:T(8,128)(2,1)S(1)}, bf16[256,720]{1,0:T(8,128)(2,1)S(1)}, u32[]{:S(2)}, u32[]{:S(2)}) collective-permute-start(bf16[256,720]{1,0:T(8,128)(2,1)S(1)} %bitcast.22), channel_id=1, source_target_pairs={{0,448},{64,0},{128,64},{192,128},{256,192},{320,256},{384,320},{4... | collective-permute-start | bytes 1105928 | tf_op jit(solution)/shard_map/projection_rows/ppermute | solution.py:31
  42.0 12.1 %collective-permute-start.1 = (bf16[256,720]{1,0:T(8,128)(2,1)S(1)}, bf16[256,720]{1,0:T(8,128)(2,1)S(1)}, u32[]{:S(2)}, u32[]{:S(2)}) collective-permute-start(bf16[256,720]{1,0:T(8,128)(2,1)S(1)} %bitcast.23), channel_id=1, source_target_pairs={{0,64},{64,128},{128,192},{192,256},{256,320},{320,384},{384,448},... | collective-permute-start | bytes 1105928 | tf_op jit(solution)/shard_map/projection_rows/ppermute | solution.py:31
  50.3 12.8 %collective-permute-start.4 = (bf16[256,720]{1,0:T(8,128)(2,1)S(1)}, bf16[256,720]{1,0:T(8,128)(2,1)S(1)}, u32[]{:S(2)}, u32[]{:S(2)}) collective-permute-start(bf16[256,720]{1,0:T(8,128)(2,1)S(1)} %collective-permute-done.2.refs_2_), channel_id=1, source_target_pairs={{0,448},{64,0},{128,64},{192,128},{256,192},{320,256},{384,320},{4... | collective-permute-start | bytes 1105928 | tf_op jit(solution)/shard_map/projection_rows/ppermute | solution.py:31
  54.1 13.9 %collective-permute-start.3 = (bf16[256,720]{1,0:T(8,128)(2,1)S(1)}, bf16[256,720]{1,0:T(8,128)(2,1)}, u32[]{:S(2)}, u32[]{:S(2)}) collective-permute-start(bf16[256,720]{1,0:T(8,128)(2,1)S(1)} %collective-permute-done.1.refs_1_), channel_id=1, source_target_pairs={{0,64},{64,128},{128,192},{192,256},{256,320},{320,384},{384,448},... | collective-permute-start | bytes 1105928 | tf_op jit(solution)/shard_map/projection_rows/ppermute | solution.py:31
  56.1 28.4 %copy-start.7 = (s32[128,4]{0,1:T(4,128)S(1)}, s32[128,4]{0,1:T(4,128)}, u32[]{:S(2)}) copy-start(s32[128,4]{0,1:T(4,128)} %param.21) | copy-start | bytes 6148
  56.1 30.4 %all-to-all-start.1 = ((bf16[8,2,128,256]{3,2,1,0:T(8,128)(2,1)}), bf16[8,2,128,256]{3,2,1,0:T(8,128)(2,1)S(1)}, u32[]{:S(2)}, u32[]{:S(2)}) async-start(bf16[8,2,128,256]{3,2,1,0:T(8,128)(2,1)} %bitcast.11), calls=%async_computation.1 | async-start | bytes 2097152 | tf_op jit(solution)/shard_map/attention/all_to_all | solution.py:301
  63.2 12.5 %collective-permute-start.6 = (bf16[256,720]{1,0:T(8,128)(2,1)S(1)}, bf16[256,720]{1,0:T(8,128)(2,1)S(1)}, u32[]{:S(2)}, u32[]{:S(2)}) collective-permute-start(bf16[256,720]{1,0:T(8,128)(2,1)S(1)} %collective-permute-done.4.refs_4_), channel_id=1, source_target_pairs={{0,448},{64,0},{128,64},{192,128},{256,192},{320,256},{384,320},{4... | collective-permute-start | bytes 1105928 | tf_op jit(solution)/shard_map/projection_rows/ppermute | solution.py:31
  68.0 13.8 %collective-permute-start.5 = (bf16[256,720]{1,0:T(8,128)(2,1)}, bf16[256,720]{1,0:T(8,128)(2,1)S(1)}, u32[]{:S(2)}, u32[]{:S(2)}) collective-permute-start(bf16[256,720]{1,0:T(8,128)(2,1)} %collective-permute-done.3.refs_3_), channel_id=1, source_target_pairs={{0,64},{64,128},{128,192},{192,256},{256,320},{320,384},{384,448},... | collective-permute-start | bytes 1105928 | tf_op jit(solution)/shard_map/projection_rows/ppermute | solution.py:31
  76.4 10.1 %collective-permute-start.8 = (bf16[128,720]{1,0:T(8,128)(2,1)}, bf16[128,720]{1,0:T(8,128)(2,1)}, u32[]{:S(2)}, u32[]{:S(2)}) collective-permute-start(bf16[128,720]{1,0:T(8,128)(2,1)} %slice.9), channel_id=1, source_target_pairs={{0,448},{64,0},{128,64},{192,128},{256,192},{320,256},{384,320},{4... | collective-permute-start | bytes 552968 | tf_op jit(solution)/shard_map/projection_rows/ppermute | solution.py:31
  82.5 8.2 %collective-permute-start.7 = (bf16[128,720]{1,0:T(8,128)(2,1)}, bf16[128,720]{1,0:T(8,128)(2,1)}, u32[]{:S(2)}, u32[]{:S(2)}) collective-permute-start(bf16[128,720]{1,0:T(8,128)(2,1)} %slice.8), channel_id=1, source_target_pairs={{0,64},{64,128},{128,192},{192,256},{256,320},{320,384},{384,448},... | collective-permute-start | bytes 552968 | tf_op jit(solution)/shard_map/projection_rows/ppermute | solution.py:31
  90.7 8.4 %copy-start.8 = (f32[720]{0:T(1024)S(1)}, f32[720]{0:T(1024)}, u32[]{:S(2)}) copy-start(f32[720]{0:T(1024)} %param.20) | copy-start | bytes 8644
  93.8 0.7 copy-start
  94.5 6.1 %collective-permute-start.9 = (f32[128,720]{1,0:T(8,128)}, f32[128,720]{1,0:T(8,128)S(1)}, u32[]{:S(2)}, u32[]{:S(2)}) collective-permute-start(f32[128,720]{1,0:T(8,128)} %get-tuple-element.20), channel_id=1, source_target_pairs={{0,4},{4,0},{1,5},{5,1},{2,6},{6,2},{3,7},{7,3},{8,12},{12,8},{9,1... | collective-permute-start | bytes 1105928 | tf_op jit(solution)/shard_map/stream/ppermute | solution.py:31
  100.6 1.0 copy-start.1
  152.2 7.3 %collective-permute-start.10 = (bf16[4608,128]{1,0:T(8,128)(2,1)S(1)}, bf16[4608,128]{1,0:T(8,128)(2,1)S(1)}, u32[]{:S(2)}, u32[]{:S(2)}) collective-permute-start(bf16[4608,128]{1,0:T(8,128)(2,1)S(1)} %bitcast.25), channel_id=1, source_target_pairs={{0,4},{4,0},{1,5},{5,1},{2,6},{6,2},{3,7},{7,3},{8,12},{12,8},{9,1... | collective-permute-start | bytes 3538952 | tf_op jit(solution)/shard_map/dispatch/ppermute | solution.py:31
  181.6 5.0 %collective-permute-start.11 = (bf16[4608,128]{1,0:T(8,128)(2,1)S(1)}, bf16[4608,128]{1,0:T(8,128)(2,1)S(1)}, u32[]{:S(2)}, u32[]{:S(2)}) collective-permute-start(bf16[4608,128]{1,0:T(8,128)(2,1)S(1)} %get-tuple-element.23), channel_id=1, source_target_pairs={{0,4},{4,0},{1,5},{5,1},{2,6},{6,2},{3,7},{7,3},{8,12},{12,8},{9,1... | collective-permute-start | bytes 3538952 | tf_op jit(solution)/shard_map/experts/ppermute | solution.py:31
  188.0 18.9 %copy-start.9 = (bf16[128,4]{0,1:T(4,128)(2,1)S(1)}, bf16[128,4]{0,1:T(4,128)(2,1)}, u32[]{:S(2)}) copy-start(bf16[128,4]{0,1:T(4,128)(2,1)} %param.22) | copy-start | bytes 3076
  188.0 50.2 %all-to-all-start.3 = ((bf16[256,9,2,128]{3,2,1,0:T(2,128)(2,1)}), bf16[256,9,2,128]{3,2,1,0:T(2,128)(2,1)S(1)}, u32[]{:S(2)}, u32[]{:S(2)}) async-start(bf16[256,9,2,128]{3,2,1,0:T(2,128)(2,1)} %bitcast.16), calls=%async_computation.3 | async-start | bytes 2359296 | tf_op jit(solution)/shard_map/combine/all_to_all | solution.py:348
Sparse Core Ops, SparseCore 0:
  9.5 159.1 all-gather.2

commit v5 on v4

--- a/solution.py
+++ b/solution.py
@@ -14,6 +14,9 @@
 TP = 4
 QUARTER = 720
 PADDED = 768
+MAIN = 640
+TAIL = 80
+PACKED = 3 * MAIN + 2 * 128
 CHUNK = 18
 TARGETS = EXPERTS * TP
 CLASS_SLOTS = 3
@@ -139,39 +142,33 @@
     out_ref[...] = flat[...].astype(BF16)
 
 
-def pack_kernel(gate_ref, up_ref, down_ref, out_ref, held, in_sems, out_sems):
+def pack_kernel(gate_ref, up_ref, down_ref, out_ref, held, made, in_sems, out_sems):
+    refs = (gate_ref, up_ref, down_ref)
     span = QUARTER // 3
     arriving, leaving = [], []
-    for n, ref in enumerate((gate_ref, up_ref, down_ref)):
-        for k in range(3):
-            rows = pl.ds(k * span, span)
+    for k in range(3):
+        rows = pl.ds(k * span, span)
+        for n, ref in enumerate(refs):
             arriving.append(
-                pltpu.make_async_copy(ref.at[rows], held.at[n, rows], in_sems.at[3 * n + k])
+                pltpu.make_async_copy(ref.at[rows], held.at[n, rows], in_sems.at[3 * k + n])
             )
-            leaving.append(
-                pltpu.make_async_copy(
-                    held.at[n, rows], out_ref.at[n, rows], out_sems.at[3 * n + k]
-                )
-            )
-    for copy in arriving:
-        copy.start()
-    for before, after in zip(arriving, leaving):
-        before.wait()
-        after.start()
+            arriving[-1].start()
+        leaving.append(pltpu.make_async_copy(made.at[rows], out_ref.at[rows], out_sems.at[k]))
+    for k in range(3):
+        rows = slice(k * span, (k + 1) * span)
+        tails = []
+        for n in range(3):
+            arriving[3 * k + n].wait()
+            made[rows, n * MAIN : (n + 1) * MAIN] = held[n, rows, :MAIN]
+            tails.append(held[n, rows, MAIN:])
+        tails.append(jnp.zeros((span, 2 * 128 - 3 * TAIL), BF16))
+        made[rows, 3 * MAIN :] = jnp.concatenate(tails, axis=1)
+        leaving[k].start()
     for copy in leaving:
         copy.wait()
 
 
-def expert_kernel(
-    mine_ref, other_ref, weights_ref, to_mine_ref, to_other_ref, flat, rows, w, sems
-):
-    copies = []
-    for n in range(3):
-        for t in range(TP):
-            copies.append(
-                pltpu.make_async_copy(weights_ref.at[t, n], w.at[n * TP + t], sems.at[n * TP + t])
-            )
-            copies[-1].start()
+def rows_kernel(mine_ref, other_ref, rows_ref, scale_ref, flat):
     squares = []
     for n, ref in enumerate((mine_ref, other_ref)):
         flat[...] = ref[...].astype(F32)
@@ -181,34 +178,51 @@
             for t in range(TP):
                 for b in range(6):
                     piece = flat[pl.ds(t * CHUNK + k * 6 + b, EXPERTS, stride=TP * CHUNK), :]
-                    rows[t, part, b * 128 : (b + 1) * 128] = piece.astype(BF16)
+                    rows_ref[t, part, b * 128 : (b + 1) * 128] = piece.astype(BF16)
                 lane = lax.broadcasted_iota(jnp.int32, piece.shape, 1)
-                total += jnp.sum(
-                    jnp.where(lane >= QUARTER - 5 * 128, piece, 0.0), axis=1, keepdims=True
-                )
+                total += jnp.sum(jnp.where(lane >= TAIL, piece, 0.0), axis=1, keepdims=True)
             squares.append(total)
-    scale = lax.rsqrt(jnp.concatenate(squares, axis=0) / D + EPSILON)
-    sums = []
-    for n in range(2):
-        total = jnp.zeros((2 * SLOTS, QUARTER), F32)
-        for t in range(TP):
-            copies[TP * n + t].wait()
-            total += jnp.dot(rows[t, :, :QUARTER], w[n * TP + t], preferred_element_type=F32)
-        sums.append(total * scale)
-    gate, up = sums
+    scale_ref[...] = lax.rsqrt(jnp.concatenate(squares, axis=0) / D + EPSILON)
+
+
+def expert_kernel(
+    rows_ref, scale_ref, weights_ref, to_mine_ref, to_other_ref, flat, rows, w, sems
+):
+    copies = []
+    for t in range(TP):
+        copies.append(
+            (
+                pltpu.make_async_copy(rows_ref.at[t], rows.at[t], sems.at[2 * t]),
+                pltpu.make_async_copy(weights_ref.at[t], w.at[t], sems.at[2 * t + 1]),
+            )
+        )
+        for copy in copies[-1]:
+            copy.start()
+    sums = jnp.zeros((2 * SLOTS, 2 * MAIN), F32)
+    ends = jnp.zeros((2 * SLOTS, 2 * 128), F32)
+    for t in range(TP):
+        for copy in copies[t]:
+            copy.wait()
+        part = rows[t, :, :QUARTER]
+        sums += jnp.dot(part, w[t, :, : 2 * MAIN], preferred_element_type=F32)
+        ends += jnp.dot(part, w[t, :, 3 * MAIN :], preferred_element_type=F32)
+    scale = scale_ref[...]
+    gate = jnp.concatenate([sums[:, :MAIN], ends[:, :TAIL]], axis=1) * scale
+    up = jnp.concatenate([sums[:, MAIN:], ends[:, TAIL : 2 * TAIL]], axis=1) * scale
     active = (gate / (1.0 + jnp.exp(-gate)) * up).astype(BF16)
-    for copy in copies[2 * TP :]:
-        copy.wait()
     for n, ref in enumerate((to_mine_ref, to_other_ref)):
         part = active[n * SLOTS : (n + 1) * SLOTS]
         for t in range(TP):
-            made = jnp.dot(part, w[2 * TP + t], preferred_element_type=F32)
-            made = jnp.concatenate([made, jnp.zeros((SLOTS, PADDED - QUARTER), F32)], axis=1)
+            made = jnp.dot(part, w[t, :, 2 * MAIN : 3 * MAIN], preferred_element_type=F32)
+            last = jnp.dot(part, w[t, :, 3 * MAIN :], preferred_element_type=F32)
+            last = jnp.concatenate(
+                [last[:, 2 * TAIL : 3 * TAIL], jnp.zeros((SLOTS, 128 - TAIL), F32)], axis=1
+            )
             for k in range(CLASS_SLOTS):
+                group = slice(k * EXPERTS, (k + 1) * EXPERTS)
                 for b in range(6):
-                    flat[pl.ds(t * CHUNK + k * 6 + b, EXPERTS, stride=TP * CHUNK), :] = made[
-                        k * EXPERTS : (k + 1) * EXPERTS, b * 128 : (b + 1) * 128
-                    ]
+                    piece = made[group, b * 128 : (b + 1) * 128] if b < 5 else last[group]
+                    flat[pl.ds(t * CHUNK + k * 6 + b, EXPERTS, stride=TP * CHUNK), :] = piece
         ref[...] = flat[...].astype(BF16)
 
 
@@ -250,12 +264,13 @@
     with jax.named_scope("expert_weights"):
         packed = call(
             pack_kernel,
-            jax.ShapeDtypeStruct((3, QUARTER, QUARTER), BF16),
+            jax.ShapeDtypeStruct((QUARTER, PACKED), BF16),
             (w_gate, w_up, w_down),
             scratch=[
                 pltpu.VMEM((3, QUARTER, QUARTER), BF16),
+                pltpu.VMEM((QUARTER, PACKED), BF16),
                 pltpu.SemaphoreType.DMA((9,)),
-                pltpu.SemaphoreType.DMA((9,)),
+                pltpu.SemaphoreType.DMA((3,)),
             ],
             spaces=[pltpu.HBM] * 3,
             made=pltpu.HBM,
@@ -355,17 +370,27 @@
         partner = shifted(arrived, "core", 1)
 
     with jax.named_scope("experts"):
+        rows, scale = call(
+            rows_kernel,
+            [
+                jax.ShapeDtypeStruct((TP, 2 * SLOTS, PADDED), BF16),
+                jax.ShapeDtypeStruct((2 * SLOTS, 1), F32),
+            ],
+            (arrived, partner),
+            scratch=[flat_scratch],
+            limit=16,
+        )
         to_mine, to_other = call(
             expert_kernel,
             [flat_shape] * 2,
-            (arrived, partner, weights),
+            (rows, scale, weights),
             scratch=[
                 flat_scratch,
                 pltpu.VMEM((TP, 2 * SLOTS, PADDED), BF16),
-                pltpu.VMEM((3 * TP, QUARTER, QUARTER), BF16),
-                pltpu.SemaphoreType.DMA((3 * TP,)),
+                pltpu.VMEM((TP, QUARTER, PACKED), BF16),
+                pltpu.SemaphoreType.DMA((2 * TP,)),
             ],
-            spaces=[pltpu.VMEM] * 2 + [pltpu.HBM],
+            spaces=[pltpu.HBM, pltpu.VMEM, pltpu.HBM],
             flops=5_000_000_000,
             moved=15_000_000,
             limit=48,

time: 248 us -> 241 us (0.972)
  waiting for transfers between devices: 65.2 us -> 56.1 us
  local copies, waits for them, and re-layouts: 7.79 us -> 10.9 us
    all_gather x1, waiting for transfers between devices: 9.26 us -> 0.2 us  [shards(): weights = lax.all_gather(packed, 'tp', axis=0, tiled=False)]
    unnamed x24 -> x28, local copies, waits for them, and re-layouts: 3.61 us -> 6.71 us
    pallas_call x7 -> x8, Pallas kernels: 27.9 us -> 26.7 us  [call(): pl.pallas_call(kernel, out_shape=out_shape, in_specs=[pl.BlockSpec(memory...]
where the time goes in v5:
time: 241 us; the launch traced here: 239 us
  starting transfers between devices  79.3 us (33%)
  waiting for transfers between devices  56.1 us (23%)
  blocking collectives  49.8 us (21%)
  Pallas kernels  26.7 us (11%)
  between operations  13.9 us (6%)
  local copies, waits for them, and re-layouts  10.9 us (5%)
  other arithmetic  2.62 us (1%)
    all_to_all x1, blocking collectives, exchanged(): lax.all_to_all(block, PLANE, 0, 0, tiled=True).reshape(flat_shape.shape)  49.8 us
    ppermute x11, starting transfers between devices, shifted(): lax.ppermute(block, axis, [(i, (i + distance) % size) for i in range(size)])  38.1 us
    all_to_all x1, waiting for transfers between devices, exchanged(): lax.all_to_all(block, PLANE, 0, 0, tiled=True).reshape(flat_shape.shape)  31.1 us
    pallas_call x8, Pallas kernels, call(): pl.pallas_call(kernel, out_shape=out_shape, in_specs=[pl.BlockSpec(memory...  26.7 us
    ppermute x11, waiting for transfers between devices, shifted(): lax.ppermute(block, axis, [(i, (i + distance) % size) for i in range(size)])  21.3 us
    all_to_all x1, starting transfers between devices, exchanged(): lax.all_to_all(block, PLANE, 0, 0, tiled=True).reshape(flat_shape.shape)  18.8 us
    all_to_all x1, starting transfers between devices, shards(): column = lax.all_to_all(spread, 'z', 0, 0, tiled=True)  10.9 us
    all_to_all x1, starting transfers between devices, shards(): lax.all_to_all(heads.reshape(2 * TP, 2, count, GROUPS * HALF), ('core', '...  7.09 us
  transfers between devices with their start and end apart: 16, of which 9 were waited for; matrix products, arithmetic and copies ran while one was open for 2% of the time, Pallas kernels for 5%

profile of v5, /device:TPU:1, one launch (start us, length us, event | category | flops | bytes accessed | tf_op | source)
XLA Modules:
  0.0 239.3 jit_solution(360739813055513725)
XLA Ops:
  6.5 3.1 %expert_weights.1 = bf16[720,2176]{1,0:T(8,128)(2,1)} custom-call(bf16[720,720]{1,0:T(8,128)(2,1)} %gate_ref.1, bf16[720,720]{1,0:T(8,128)(2,1)} %up_ref.1, bf16[720,720]{1,0:T(8,128)(2,1)} %down_ref.1), custom_call_target="tpu_custom_call" | custom-call | tf_op jit(solution)/shard_map/expert_weights/pallas_call | solution.py:39
  9.6 0.0 copy-start.6
  9.6 0.0 all-gather.3.cloned.1.call-update
  9.7 0.8 copy-done.6
  10.4 0.0 copy-start.5
  10.4 0.8 broadcast_in_dim.44
  11.2 10.9 %all-to-all-start = ((bf16[8,32,720]{2,1,0:T(8,128)(2,1)}), bf16[8,32,720]{2,1,0:T(8,128)(2,1)S(1)}, u32[]{:S(2)}, u32[]{:S(2)}) async-start(bf16[8,32,720]{2,1,0:T(8,128)(2,1)} %broadcast_in_dim.44), calls=%async_computation | async-start | bytes 786432 | tf_op jit(solution)/shard_map/projection_rows/all_to_all | solution.py:284
  22.2 4.5 %collective-permute-start = (bf16[128,256]{1,0:T(8,128)(2,1)S(1)}, bf16[128,256]{1,0:T(8,128)(2,1)S(1)}, u32[]{:S(2)}, u32[]{:S(2)}) collective-permute-start(bf16[128,256]{1,0:T(8,128)(2,1)S(1)} %constant_dynamic-update-slice_fusion.own_ref), channel_id=1, source_target_pairs={{0,4},{4,8},{8,12},{12,16},{16,20},{20,24},{24,28},{28,32},{32,36}... | collective-permute-start | bytes 196616 | tf_op jit(solution)/shard_map/attention/ppermute | solution.py:289
  26.7 0.0 copy-done.12
  26.7 0.1 copy.21.start_ref
  26.8 3.5 %collective-permute-done.before_ref = bf16[128,256]{1,0:T(8,128)(2,1)S(1)} collective-permute-done((bf16[128,256]{1,0:T(8,128)(2,1)S(1)}, bf16[128,256]{1,0:T(8,128)(2,1)S(1)}, u32[]{:S(2)}, u32[]{:S(2)}) %collective-permute-start) | collective-permute-done | bytes 65568 | tf_op jit(solution)/shard_map/attention/ppermute | solution.py:289
  30.3 7.8 %attention.1 = bf16[2,4,2,128,256]{4,3,2,1,0:T(8,128)(2,1)} custom-call(bf16[128,1024]{1,0:T(8,128)(2,1)S(1)} %copy-done.4, bf16[128,256]{1,0:T(8,128)(2,1)S(1)} %constant_dynamic-update-slice_fusion.own_ref, bf16[128,256]{1,0:T(8,128)(2,1)S(1)} %collective-permute-done.before_ref, s32[128,1]{1,0:T(8,128)S(1)} %copy.21.start_ref, f32[16]{0:T(128)S(1)} %copy-done.5), custom_call_target="tpu_custom_call" | custom-call | flops 2000000000 | bytes 2000000 | tf_op jit(solution)/shard_map/attention/pallas_call | solution.py:39
  38.1 0.0 all-to-all-done
  38.1 4.1 %collective-permute-start.2 = (bf16[256,720]{1,0:T(8,128)(2,1)S(1)}, bf16[256,720]{1,0:T(8,128)(2,1)S(1)}, u32[]{:S(2)}, u32[]{:S(2)}) collective-permute-start(bf16[256,720]{1,0:T(8,128)(2,1)S(1)} %bitcast.24), channel_id=1, source_target_pairs={{0,448},{64,0},{128,64},{192,128},{256,192},{320,256},{384,320},{4... | collective-permute-start | bytes 1105928 | tf_op jit(solution)/shard_map/projection_rows/ppermute | solution.py:34
  42.3 1.9 collective-permute-start.1
  44.2 6.3 %collective-permute-done.2.refs_2_ = bf16[256,720]{1,0:T(8,128)(2,1)S(1)} collective-permute-done((bf16[256,720]{1,0:T(8,128)(2,1)S(1)}, bf16[256,720]{1,0:T(8,128)(2,1)S(1)}, u32[]{:S(2)}, u32[]{:S(2)}) %collective-permute-start.2) | collective-permute-done | bytes 368672 | tf_op jit(solution)/shard_map/projection_rows/ppermute | solution.py:34
  50.5 3.9 %collective-permute-start.4 = (bf16[256,720]{1,0:T(8,128)(2,1)S(1)}, bf16[256,720]{1,0:T(8,128)(2,1)S(1)}, u32[]{:S(2)}, u32[]{:S(2)}) collective-permute-start(bf16[256,720]{1,0:T(8,128)(2,1)S(1)} %collective-permute-done.2.refs_2_), channel_id=1, source_target_pairs={{0,448},{64,0},{128,64},{192,128},{256,192},{320,256},{384,320},{4... | collective-permute-start | bytes 1105928 | tf_op jit(solution)/shard_map/projection_rows/ppermute | solution.py:34
  54.4 0.0 collective-permute-done.1.refs_1_
  54.4 1.9 collective-permute-start.3
  56.3 0.0 copy-start.9
  56.3 7.1 %all-to-all-start.1 = ((bf16[8,2,128,256]{3,2,1,0:T(8,128)(2,1)}), bf16[8,2,128,256]{3,2,1,0:T(8,128)(2,1)S(1)}, u32[]{:S(2)}, u32[]{:S(2)}) async-start(bf16[8,2,128,256]{3,2,1,0:T(8,128)(2,1)} %bitcast.11), calls=%async_computation.1 | async-start | bytes 2097152 | tf_op jit(solution)/shard_map/attention/all_to_all | solution.py:316
  63.4 0.0 collective-permute-done.4.refs_4_
  63.4 4.8 %collective-permute-start.6 = (bf16[256,720]{1,0:T(8,128)(2,1)S(1)}, bf16[256,720]{1,0:T(8,128)(2,1)S(1)}, u32[]{:S(2)}, u32[]{:S(2)}) collective-permute-start(bf16[256,720]{1,0:T(8,128)(2,1)S(1)} %collective-permute-done.4.refs_4_), channel_id=1, source_target_pairs={{0,448},{64,0},{128,64},{192,128},{256,192},{320,256},{384,320},{4... | collective-permute-start | bytes 1105928 | tf_op jit(solution)/shard_map/projection_rows/ppermute | solution.py:34
  68.3 0.0 collective-permute-done.3.refs_3_
  68.3 1.9 collective-permute-start.5
  70.2 5.8 %collective-permute-done.6.refs_6_ = bf16[256,720]{1,0:T(8,128)(2,1)S(1)} collective-permute-done((bf16[256,720]{1,0:T(8,128)(2,1)S(1)}, bf16[256,720]{1,0:T(8,128)(2,1)S(1)}, u32[]{:S(2)}, u32[]{:S(2)}) %collective-permute-start.6) | collective-permute-done | bytes 368672 | tf_op jit(solution)/shard_map/projection_rows/ppermute | solution.py:34
  76.0 0.7 slice.9
  76.7 5.4 %collective-permute-start.8 = (bf16[128,720]{1,0:T(8,128)(2,1)}, bf16[128,720]{1,0:T(8,128)(2,1)}, u32[]{:S(2)}, u32[]{:S(2)}) collective-permute-start(bf16[128,720]{1,0:T(8,128)(2,1)} %slice.9), channel_id=1, source_target_pairs={{0,448},{64,0},{128,64},{192,128},{256,192},{320,256},{384,320},{4... | collective-permute-start | bytes 552968 | tf_op jit(solution)/shard_map/projection_rows/ppermute | solution.py:34
  82.1 0.0 collective-permute-done.5.refs_5_
  82.1 0.7 slice.8
  82.8 1.9 collective-permute-start.7
  84.9 0.1 copy.23
  85.0 0.2 reduce_window_sum.11
  85.1 0.6 sub.33
  85.8 0.9 copy.25
  86.7 0.1 stack.39.index_ref
  86.8 0.0 all-to-all-done.1
  86.8 0.0 collective-permute-done.8.refs_8_
  86.8 4.2 %collective-permute-done.7.refs_7_ = bf16[128,720]{1,0:T(8,128)(2,1)} collective-permute-done((bf16[128,720]{1,0:T(8,128)(2,1)}, bf16[128,720]{1,0:T(8,128)(2,1)}, u32[]{:S(2)}, u32[]{:S(2)}) %collective-permute-start.7) | collective-permute-done | bytes 184352 | tf_op jit(solution)/shard_map/projection_rows/ppermute | solution.py:34
  91.1 3.1 %stream.2 = (f32[128,720]{1,0:T(8,128)S(1)}, f32[128,720]{1,0:T(8,128)}) custom-call(s32[9]{0:T(128)S(1)} %stack.39.index_ref, bf16[2,8,128,256]{3,2,1,0:T(8,128)(2,1)S(1)} %bitcast.23, bf16[256,720]{1,0:T(8,128)(2,1)S(1)} %bitcast.26, bf16[256,720]{1,0:T(8,128)(2,1)S(1)} %collective-permute-done.1.refs_1_, ...), custom_call_target="tpu_custom_call" | custom-call | flops 800000000 | bytes 4000000 | tf_op jit(solution)/shard_map/stream/pallas_call | solution.py:39
  94.1 0.8 copy-done
  94.9 4.5 %collective-permute-start.9 = (f32[128,720]{1,0:T(8,128)}, f32[128,720]{1,0:T(8,128)S(1)}, u32[]{:S(2)}, u32[]{:S(2)}) collective-permute-start(f32[128,720]{1,0:T(8,128)} %get-tuple-element.22), channel_id=1, source_target_pairs={{0,4},{4,0},{1,5},{5,1},{2,6},{6,2},{3,7},{7,3},{8,12},{12,8},{9,1... | collective-permute-start | bytes 1105928 | tf_op jit(solution)/shard_map/stream/ppermute | solution.py:34
  99.5 1.1 copy.22.residual_ref
  100.6 0.2 fusion.3.routing_ref
  100.8 0.2 collective-permute-done.9.got_ref
  101.0 1.0 copy-done.1
  102.0 0.2 stream.3
  102.2 0.5 dispatch.1
  102.8 49.8 %all_to_all.20 = bf16[256,9,2,128]{3,2,1,0:T(2,128)(2,1)S(1)} all-to-all(bf16[256,9,2,128]{3,2,1,0:T(2,128)(2,1)S(1)} %bitcast.21), channel_id=1, replica_groups=mesh['y'=8,'z'=8,'core'=2,'tp'=4] {'y','z','tp'}, dimensions={0} | all-to-all | bytes 2359296 | tf_op jit(solution)/shard_map/dispatch/all_to_all | solution.py:363
  152.6 5.0 %collective-permute-start.10 = (bf16[4608,128]{1,0:T(8,128)(2,1)S(1)}, bf16[4608,128]{1,0:T(8,128)(2,1)S(1)}, u32[]{:S(2)}, u32[]{:S(2)}) collective-permute-start(bf16[4608,128]{1,0:T(8,128)(2,1)S(1)} %bitcast.19), channel_id=1, source_target_pairs={{0,4},{4,0},{1,5},{5,1},{2,6},{6,2},{3,7},{7,3},{8,12},{12,8},{9,1... | collective-permute-start | bytes 3538952 | tf_op jit(solution)/shard_map/dispatch/ppermute | solution.py:34
  157.6 2.3 collective-permute-done.10.other_ref
  159.9 1.3 experts.2
  161.2 1.4 copy-done.2
  162.6 0.2 all-gather.3.cloned.1.call-done
  162.8 1.7 copy-done.3
  164.5 10.0 %experts.3 = (bf16[4608,128]{1,0:T(8,128)(2,1)S(1)}, bf16[4608,128]{1,0:T(8,128)(2,1)S(1)}) custom-call(bf16[4,384,768]{2,1,0:T(8,128)(2,1)S(1)} %copy-done.3, f32[384,1]{1,0:T(8,128)S(1)} %get-tuple-element.25.scale_ref, bf16[4,720,2176]{2,1,0:T(8,128)(2,1)} %bitcast.27), custom_call_target="tpu_custom_call" | custom-call | flops 5000000000 | bytes 15000000 | tf_op jit(solution)/shard_map/experts/pallas_call | solution.py:39
  174.5 2.6 %collective-permute-start.11 = (bf16[4608,128]{1,0:T(8,128)(2,1)S(1)}, bf16[4608,128]{1,0:T(8,128)(2,1)S(1)}, u32[]{:S(2)}, u32[]{:S(2)}) collective-permute-start(bf16[4608,128]{1,0:T(8,128)(2,1)S(1)} %get-tuple-element.27), channel_id=1, source_target_pairs={{0,4},{4,0},{1,5},{5,1},{2,6},{6,2},{3,7},{7,3},{8,12},{12,8},{9,1... | collective-permute-start | bytes 3538952 | tf_op jit(solution)/shard_map/experts/ppermute | solution.py:34
  177.1 2.5 %collective-permute-done.11 = bf16[4608,128]{1,0:T(8,128)(2,1)S(1)} collective-permute-done((bf16[4608,128]{1,0:T(8,128)(2,1)S(1)}, bf16[4608,128]{1,0:T(8,128)(2,1)S(1)}, u32[]{:S(2)}, u32[]{:S(2)}) %collective-permute-start.11) | collective-permute-done | bytes 1179680 | tf_op jit(solution)/shard_map/experts/ppermute | solution.py:34
  179.5 1.3 add_convert_fusion
  180.9 18.8 %all-to-all-start.3 = ((bf16[256,9,2,128]{3,2,1,0:T(2,128)(2,1)}), bf16[256,9,2,128]{3,2,1,0:T(2,128)(2,1)S(1)}, u32[]{:S(2)}, u32[]{:S(2)}) async-start(bf16[256,9,2,128]{3,2,1,0:T(2,128)(2,1)} %bitcast.16), calls=%async_computation.3 | async-start | bytes 2359296 | tf_op jit(solution)/shard_map/combine/all_to_all | solution.py:363
  199.7 0.2 fusion.2.mixing_ref
  199.9 31.1 %all-to-all-done.3 = bf16[256,9,2,128]{3,2,1,0:T(2,128)(2,1)S(1)} async-done(((bf16[256,9,2,128]{3,2,1,0:T(2,128)(2,1)}), bf16[256,9,2,128]{3,2,1,0:T(2,128)(2,1)S(1)}, u32[]{:S(2)}, u32[]{:S(2)}) %all-to-all-start.3) | async-done | bytes 1179680 | tf_op jit(solution)/shard_map/combine/all_to_all | solution.py:363
  231.0 0.6 combine.1
  231.6 0.8 copy.26
  (25 shorter events, 0.1 us)
Async XLA Ops:
  6.5 156.3 %all-gather.3.cloned.1.call-start = ((), (), s32[]{:S(2)}) async-start(), calls=%async_computation.4 | async-start | bytes 15667200 | tf_op jit(solution)/shard_map/expert_weights/all_gather | solution.py:279
  9.6 0.8 copy-start.6
  10.4 11.7 %copy-start.7 = (bf16[128,128]{1,0:T(8,128)(2,1)S(1)}, bf16[128,128]{1,0:T(8,128)(2,1)}, u32[]{:S(2)}) copy-start(bf16[128,128]{1,0:T(8,128)(2,1)} %param.14) | copy-start | bytes 98308
  10.4 11.7 %copy-start.8 = (bf16[128,128]{1,0:T(8,128)(2,1)S(1)}, bf16[128,128]{1,0:T(8,128)(2,1)}, u32[]{:S(2)}) copy-start(bf16[128,128]{1,0:T(8,128)(2,1)} %param.15) | copy-start | bytes 98308
  10.4 16.2 %copy-start.12 = (s32[128]{0:T(128)S(1)}, s32[128]{0:T(128)}, u32[]{:S(2)}) copy-start(s32[128]{0:T(128)} %param.17) | copy-start | bytes 1540
  10.4 19.9 %copy-start.4 = (bf16[128,1024]{1,0:T(8,128)(2,1)S(1)}, bf16[128,1024]{1,0:T(8,128)(2,1)}, u32[]{:S(2)}) copy-start(bf16[128,1024]{1,0:T(8,128)(2,1)} %q_ref.1) | copy-start | bytes 786436
  10.4 19.9 %copy-start.5 = (f32[16]{0:T(128)S(1)}, f32[16]{0:T(128)}, u32[]{:S(2)}) copy-start(f32[16]{0:T(128)} %sink_ref.1) | copy-start | bytes 196
  11.2 26.9 %all-to-all-start = ((bf16[8,32,720]{2,1,0:T(8,128)(2,1)}), bf16[8,32,720]{2,1,0:T(8,128)(2,1)S(1)}, u32[]{:S(2)}, u32[]{:S(2)}) async-start(bf16[8,32,720]{2,1,0:T(8,128)(2,1)} %broadcast_in_dim.44), calls=%async_computation | async-start | bytes 786432 | tf_op jit(solution)/shard_map/projection_rows/all_to_all | solution.py:284
  22.2 8.2 %collective-permute-start = (bf16[128,256]{1,0:T(8,128)(2,1)S(1)}, bf16[128,256]{1,0:T(8,128)(2,1)S(1)}, u32[]{:S(2)}, u32[]{:S(2)}) collective-permute-start(bf16[128,256]{1,0:T(8,128)(2,1)S(1)} %constant_dynamic-update-slice_fusion.own_ref), channel_id=1, source_target_pairs={{0,4},{4,8},{8,12},{12,16},{16,20},{20,24},{24,28},{28,32},{32,36}... | collective-permute-start | bytes 196616 | tf_op jit(solution)/shard_map/attention/ppermute | solution.py:289
  38.1 12.4 %collective-permute-start.2 = (bf16[256,720]{1,0:T(8,128)(2,1)S(1)}, bf16[256,720]{1,0:T(8,128)(2,1)S(1)}, u32[]{:S(2)}, u32[]{:S(2)}) collective-permute-start(bf16[256,720]{1,0:T(8,128)(2,1)S(1)} %bitcast.24), channel_id=1, source_target_pairs={{0,448},{64,0},{128,64},{192,128},{256,192},{320,256},{384,320},{4... | collective-permute-start | bytes 1105928 | tf_op jit(solution)/shard_map/projection_rows/ppermute | solution.py:34
  42.3 12.1 %collective-permute-start.1 = (bf16[256,720]{1,0:T(8,128)(2,1)S(1)}, bf16[256,720]{1,0:T(8,128)(2,1)S(1)}, u32[]{:S(2)}, u32[]{:S(2)}) collective-permute-start(bf16[256,720]{1,0:T(8,128)(2,1)S(1)} %bitcast.25), channel_id=1, source_target_pairs={{0,64},{64,128},{128,192},{192,256},{256,320},{320,384},{384,448},... | collective-permute-start | bytes 1105928 | tf_op jit(solution)/shard_map/projection_rows/ppermute | solution.py:34
  50.5 12.9 %collective-permute-start.4 = (bf16[256,720]{1,0:T(8,128)(2,1)S(1)}, bf16[256,720]{1,0:T(8,128)(2,1)S(1)}, u32[]{:S(2)}, u32[]{:S(2)}) collective-permute-start(bf16[256,720]{1,0:T(8,128)(2,1)S(1)} %collective-permute-done.2.refs_2_), channel_id=1, source_target_pairs={{0,448},{64,0},{128,64},{192,128},{256,192},{320,256},{384,320},{4... | collective-permute-start | bytes 1105928 | tf_op jit(solution)/shard_map/projection_rows/ppermute | solution.py:34
  54.4 13.9 %collective-permute-start.3 = (bf16[256,720]{1,0:T(8,128)(2,1)S(1)}, bf16[256,720]{1,0:T(8,128)(2,1)}, u32[]{:S(2)}, u32[]{:S(2)}) collective-permute-start(bf16[256,720]{1,0:T(8,128)(2,1)S(1)} %collective-permute-done.1.refs_1_), channel_id=1, source_target_pairs={{0,64},{64,128},{128,192},{192,256},{256,320},{320,384},{384,448},... | collective-permute-start | bytes 1105928 | tf_op jit(solution)/shard_map/projection_rows/ppermute | solution.py:34
  56.3 28.5 %copy-start.9 = (s32[128,4]{0,1:T(4,128)S(1)}, s32[128,4]{0,1:T(4,128)}, u32[]{:S(2)}) copy-start(s32[128,4]{0,1:T(4,128)} %param.21) | copy-start | bytes 6148
  56.3 30.5 %all-to-all-start.1 = ((bf16[8,2,128,256]{3,2,1,0:T(8,128)(2,1)}), bf16[8,2,128,256]{3,2,1,0:T(8,128)(2,1)S(1)}, u32[]{:S(2)}, u32[]{:S(2)}) async-start(bf16[8,2,128,256]{3,2,1,0:T(8,128)(2,1)} %bitcast.11), calls=%async_computation.1 | async-start | bytes 2097152 | tf_op jit(solution)/shard_map/attention/all_to_all | solution.py:316
  63.4 12.5 %collective-permute-start.6 = (bf16[256,720]{1,0:T(8,128)(2,1)S(1)}, bf16[256,720]{1,0:T(8,128)(2,1)S(1)}, u32[]{:S(2)}, u32[]{:S(2)}) collective-permute-start(bf16[256,720]{1,0:T(8,128)(2,1)S(1)} %collective-permute-done.4.refs_4_), channel_id=1, source_target_pairs={{0,448},{64,0},{128,64},{192,128},{256,192},{320,256},{384,320},{4... | collective-permute-start | bytes 1105928 | tf_op jit(solution)/shard_map/projection_rows/ppermute | solution.py:34
  68.3 13.8 %collective-permute-start.5 = (bf16[256,720]{1,0:T(8,128)(2,1)}, bf16[256,720]{1,0:T(8,128)(2,1)S(1)}, u32[]{:S(2)}, u32[]{:S(2)}) collective-permute-start(bf16[256,720]{1,0:T(8,128)(2,1)} %collective-permute-done.3.refs_3_), channel_id=1, source_target_pairs={{0,64},{64,128},{128,192},{192,256},{256,320},{320,384},{384,448},... | collective-permute-start | bytes 1105928 | tf_op jit(solution)/shard_map/projection_rows/ppermute | solution.py:34
  76.7 10.1 %collective-permute-start.8 = (bf16[128,720]{1,0:T(8,128)(2,1)}, bf16[128,720]{1,0:T(8,128)(2,1)}, u32[]{:S(2)}, u32[]{:S(2)}) collective-permute-start(bf16[128,720]{1,0:T(8,128)(2,1)} %slice.9), channel_id=1, source_target_pairs={{0,448},{64,0},{128,64},{192,128},{256,192},{320,256},{384,320},{4... | collective-permute-start | bytes 552968 | tf_op jit(solution)/shard_map/projection_rows/ppermute | solution.py:34
  82.8 8.2 %collective-permute-start.7 = (bf16[128,720]{1,0:T(8,128)(2,1)}, bf16[128,720]{1,0:T(8,128)(2,1)}, u32[]{:S(2)}, u32[]{:S(2)}) collective-permute-start(bf16[128,720]{1,0:T(8,128)(2,1)} %slice.8), channel_id=1, source_target_pairs={{0,64},{64,128},{128,192},{192,256},{256,320},{320,384},{384,448},... | collective-permute-start | bytes 552968 | tf_op jit(solution)/shard_map/projection_rows/ppermute | solution.py:34
  91.1 8.4 %copy-start.10 = (f32[720]{0:T(1024)S(1)}, f32[720]{0:T(1024)}, u32[]{:S(2)}) copy-start(f32[720]{0:T(1024)} %param.20) | copy-start | bytes 8644
  94.1 0.8 copy-start
  94.9 6.1 %collective-permute-start.9 = (f32[128,720]{1,0:T(8,128)}, f32[128,720]{1,0:T(8,128)S(1)}, u32[]{:S(2)}, u32[]{:S(2)}) collective-permute-start(f32[128,720]{1,0:T(8,128)} %get-tuple-element.22), channel_id=1, source_target_pairs={{0,4},{4,0},{1,5},{5,1},{2,6},{6,2},{3,7},{7,3},{8,12},{12,8},{9,1... | collective-permute-start | bytes 1105928 | tf_op jit(solution)/shard_map/stream/ppermute | solution.py:34
  101.0 1.0 copy-start.1
  152.6 7.3 %collective-permute-start.10 = (bf16[4608,128]{1,0:T(8,128)(2,1)S(1)}, bf16[4608,128]{1,0:T(8,128)(2,1)S(1)}, u32[]{:S(2)}, u32[]{:S(2)}) collective-permute-start(bf16[4608,128]{1,0:T(8,128)(2,1)S(1)} %bitcast.19), channel_id=1, source_target_pairs={{0,4},{4,0},{1,5},{5,1},{2,6},{6,2},{3,7},{7,3},{8,12},{12,8},{9,1... | collective-permute-start | bytes 3538952 | tf_op jit(solution)/shard_map/dispatch/ppermute | solution.py:34
  161.2 1.4 copy-start.2
  162.8 1.7 copy-start.3
  174.5 5.0 %collective-permute-start.11 = (bf16[4608,128]{1,0:T(8,128)(2,1)S(1)}, bf16[4608,128]{1,0:T(8,128)(2,1)S(1)}, u32[]{:S(2)}, u32[]{:S(2)}) collective-permute-start(bf16[4608,128]{1,0:T(8,128)(2,1)S(1)} %get-tuple-element.27), channel_id=1, source_target_pairs={{0,4},{4,0},{1,5},{5,1},{2,6},{6,2},{3,7},{7,3},{8,12},{12,8},{9,1... | collective-permute-start | bytes 3538952 | tf_op jit(solution)/shard_map/experts/ppermute | solution.py:34
  180.9 18.8 %copy-start.11 = (bf16[128,4]{0,1:T(4,128)(2,1)S(1)}, bf16[128,4]{0,1:T(4,128)(2,1)}, u32[]{:S(2)}) copy-start(bf16[128,4]{0,1:T(4,128)(2,1)} %param.22) | copy-start | bytes 3076
  180.9 50.1 %all-to-all-start.3 = ((bf16[256,9,2,128]{3,2,1,0:T(2,128)(2,1)}), bf16[256,9,2,128]{3,2,1,0:T(2,128)(2,1)S(1)}, u32[]{:S(2)}, u32[]{:S(2)}) async-start(bf16[256,9,2,128]{3,2,1,0:T(2,128)(2,1)} %bitcast.16), calls=%async_computation.3 | async-start | bytes 2359296 | tf_op jit(solution)/shard_map/combine/all_to_all | solution.py:363
Sparse Core Ops, SparseCore 0:
  9.8 152.9 all-gather.2

commit v6 on v5

--- a/solution.py
+++ b/solution.py
@@ -100,21 +100,23 @@
 
 
 def projection_kernel(index_ref, heads_ref, *refs):
-    shards, (own_ref, other_ref, total) = refs[:9], refs[9:]
+    shards, (own_ref, other_ref, total, sems) = refs[:9], refs[9:]
     me = index_ref[8]
-    rows = own_ref.shape[0]
-    for half in range(2):
-        acc = jnp.zeros((rows, QUARTER), F32)
-        for n in range(7):
-            chunk = heads_ref[half, index_ref[n]]
-            acc += jnp.dot(chunk, shards[n][...], preferred_element_type=F32)
+    leaving = []
+    for n, (half, ref) in enumerate(((1 - me, other_ref), (me, own_ref))):
+        acc = jnp.zeros(total.shape[1:], F32)
+        for k in range(7):
+            chunk = heads_ref[half, index_ref[k]]
+            acc += jnp.dot(chunk, shards[k][...], preferred_element_type=F32)
         chunk = heads_ref[half, index_ref[7]]
         depth = chunk.shape[1] // 2
         acc += jnp.dot(chunk[:, :depth], shards[7][...], preferred_element_type=F32)
         acc += jnp.dot(chunk[:, depth:], shards[8][...], preferred_element_type=F32)
-        total[half] = acc
-    own_ref[...] = total[me]
-    other_ref[...] = total[1 - me]
+        total[n] = acc
+        leaving.append(pltpu.make_async_copy(total.at[n], ref, sems.at[n]))
+        leaving[n].start()
+    for copy in leaving:
+        copy.wait()
 
 
 def stream_kernel(residual_ref, own_ref, got_ref, gain_ref, stream_ref, rows_ref):
@@ -168,7 +170,12 @@
         copy.wait()
 
 
-def rows_kernel(mine_ref, other_ref, rows_ref, scale_ref, flat):
+def expert_kernel(
+    mine_ref, other_ref, weights_ref, to_mine_ref, to_other_ref, flat, rows, w, sems
+):
+    copies = [pltpu.make_async_copy(weights_ref.at[t], w.at[t], sems.at[t]) for t in range(TP)]
+    for copy in copies:
+        copy.start()
     squares = []
     for n, ref in enumerate((mine_ref, other_ref)):
         flat[...] = ref[...].astype(F32)
@@ -178,35 +185,18 @@
             for t in range(TP):
                 for b in range(6):
                     piece = flat[pl.ds(t * CHUNK + k * 6 + b, EXPERTS, stride=TP * CHUNK), :]
-                    rows_ref[t, part, b * 128 : (b + 1) * 128] = piece.astype(BF16)
+                    rows[t, part, b * 128 : (b + 1) * 128] = piece.astype(BF16)
                 lane = lax.broadcasted_iota(jnp.int32, piece.shape, 1)
                 total += jnp.sum(jnp.where(lane >= TAIL, piece, 0.0), axis=1, keepdims=True)
             squares.append(total)
-    scale_ref[...] = lax.rsqrt(jnp.concatenate(squares, axis=0) / D + EPSILON)
-
-
-def expert_kernel(
-    rows_ref, scale_ref, weights_ref, to_mine_ref, to_other_ref, flat, rows, w, sems
-):
-    copies = []
-    for t in range(TP):
-        copies.append(
-            (
-                pltpu.make_async_copy(rows_ref.at[t], rows.at[t], sems.at[2 * t]),
-                pltpu.make_async_copy(weights_ref.at[t], w.at[t], sems.at[2 * t + 1]),
-            )
-        )
-        for copy in copies[-1]:
-            copy.start()
+    scale = lax.rsqrt(jnp.concatenate(squares, axis=0) / D + EPSILON)
     sums = jnp.zeros((2 * SLOTS, 2 * MAIN), F32)
     ends = jnp.zeros((2 * SLOTS, 2 * 128), F32)
     for t in range(TP):
-        for copy in copies[t]:
-            copy.wait()
+        copies[t].wait()
         part = rows[t, :, :QUARTER]
         sums += jnp.dot(part, w[t, :, : 2 * MAIN], preferred_element_type=F32)
         ends += jnp.dot(part, w[t, :, 3 * MAIN :], preferred_element_type=F32)
-    scale = scale_ref[...]
     gate = jnp.concatenate([sums[:, :MAIN], ends[:, :TAIL]], axis=1) * scale
     up = jnp.concatenate([sums[:, MAIN:], ends[:, TAIL : 2 * TAIL]], axis=1) * scale
     active = (gate / (1.0 + jnp.exp(-gate)) * up).astype(BF16)
@@ -323,7 +313,8 @@
             projection_kernel,
             [jax.ShapeDtypeStruct((count, QUARTER), F32)] * 2,
             (index, heads, *pieces),
-            scratch=[pltpu.VMEM((2, count, QUARTER), F32)],
+            scratch=[pltpu.VMEM((2, count, QUARTER), F32), pltpu.SemaphoreType.DMA((2,))],
+            made=pltpu.HBM,
             spaces=[pltpu.SMEM] + [pltpu.VMEM] * 10,
             flops=800_000_000,
             moved=4_000_000,
@@ -370,27 +361,17 @@
         partner = shifted(arrived, "core", 1)
 
     with jax.named_scope("experts"):
-        rows, scale = call(
-            rows_kernel,
-            [
-                jax.ShapeDtypeStruct((TP, 2 * SLOTS, PADDED), BF16),
-                jax.ShapeDtypeStruct((2 * SLOTS, 1), F32),
-            ],
-            (arrived, partner),
-            scratch=[flat_scratch],
-            limit=16,
-        )
         to_mine, to_other = call(
             expert_kernel,
             [flat_shape] * 2,
-            (rows, scale, weights),
+            (arrived, partner, weights),
             scratch=[
                 flat_scratch,
                 pltpu.VMEM((TP, 2 * SLOTS, PADDED), BF16),
                 pltpu.VMEM((TP, QUARTER, PACKED), BF16),
-                pltpu.SemaphoreType.DMA((2 * TP,)),
+                pltpu.SemaphoreType.DMA((TP,)),
             ],
-            spaces=[pltpu.HBM, pltpu.VMEM, pltpu.HBM],
+            spaces=[pltpu.VMEM] * 2 + [pltpu.HBM],
             flops=5_000_000_000,
             moved=15_000_000,
             limit=48,

time: 241 us -> 241 us (level)
  local copies, waits for them, and re-layouts: 10.9 us -> 7.83 us
  waiting for transfers between devices: 56.1 us -> 59 us
    unnamed x28 -> x24, local copies, waits for them, and re-layouts: 6.71 us -> 3.63 us
    all_gather x1, waiting for transfers between devices: 0.2 us -> 3.04 us  [shards(): weights = lax.all_gather(packed, 'tp', axis=0, tiled=False)]
    pallas_call x8 -> x7, Pallas kernels: 26.7 us -> 26.3 us  [call(): pl.pallas_call(kernel, out_shape=out_shape, in_specs=[pl.BlockSpec(memory...]
where the time goes in v6:
time: 241 us; the launch traced here: 239 us
  starting transfers between devices  79.2 us (33%)
  waiting for transfers between devices  59 us (24%)
  blocking collectives  49.8 us (21%)
  Pallas kernels  26.3 us (11%)
  between operations  13.9 us (6%)
  local copies, waits for them, and re-layouts  7.83 us (3%)
  other arithmetic  2.64 us (1%)
    all_to_all x1, blocking collectives, exchanged(): lax.all_to_all(block, PLANE, 0, 0, tiled=True).reshape(flat_shape.shape)  49.8 us
    ppermute x11, starting transfers between devices, shifted(): lax.ppermute(block, axis, [(i, (i + distance) % size) for i in range(size)])  38 us
    all_to_all x1, waiting for transfers between devices, exchanged(): lax.all_to_all(block, PLANE, 0, 0, tiled=True).reshape(flat_shape.shape)  31.1 us
    pallas_call x7, Pallas kernels, call(): pl.pallas_call(kernel, out_shape=out_shape, in_specs=[pl.BlockSpec(memory...  26.3 us
    ppermute x11, waiting for transfers between devices, shifted(): lax.ppermute(block, axis, [(i, (i + distance) % size) for i in range(size)])  21.3 us
    all_to_all x1, starting transfers between devices, exchanged(): lax.all_to_all(block, PLANE, 0, 0, tiled=True).reshape(flat_shape.shape)  18.8 us
    all_to_all x1, starting transfers between devices, shards(): column = lax.all_to_all(spread, 'z', 0, 0, tiled=True)  10.9 us
    all_to_all x1, starting transfers between devices, shards(): lax.all_to_all(heads.reshape(2 * TP, 2, count, GROUPS * HALF), ('core', '...  7.08 us
  transfers between devices with their start and end apart: 16, of which 9 were waited for; matrix products, arithmetic and copies ran while one was open for 2% of the time, Pallas kernels for 5%

profile of v6, /device:TPU:1, one launch (start us, length us, event | category | flops | bytes accessed | tf_op | source)
XLA Modules:
  0.0 238.6 jit_solution(9382160270563565498)
XLA Ops:
  6.5 0.0 all-gather.3.cloned.1.call-start
  6.5 3.1 %expert_weights.1 = bf16[720,2176]{1,0:T(8,128)(2,1)} custom-call(bf16[720,720]{1,0:T(8,128)(2,1)} %gate_ref.1, bf16[720,720]{1,0:T(8,128)(2,1)} %up_ref.1, bf16[720,720]{1,0:T(8,128)(2,1)} %down_ref.1), custom_call_target="tpu_custom_call" | custom-call | tf_op jit(solution)/shard_map/expert_weights/pallas_call | solution.py:39
  9.6 0.0 copy-start.4
  9.6 0.0 all-gather.3.cloned.1.call-update
  9.7 0.8 copy-done.4
  10.4 0.0 copy-start.3
  10.4 0.8 broadcast_in_dim.44
  11.2 10.9 %all-to-all-start = ((bf16[8,32,720]{2,1,0:T(8,128)(2,1)}), bf16[8,32,720]{2,1,0:T(8,128)(2,1)S(1)}, u32[]{:S(2)}, u32[]{:S(2)}) async-start(bf16[8,32,720]{2,1,0:T(8,128)(2,1)} %broadcast_in_dim.44), calls=%async_computation | async-start | bytes 786432 | tf_op jit(solution)/shard_map/projection_rows/all_to_all | solution.py:274
  22.1 0.0 copy-done.5
  22.1 0.0 copy-done.6
  22.1 4.5 %collective-permute-start = (bf16[128,256]{1,0:T(8,128)(2,1)S(1)}, bf16[128,256]{1,0:T(8,128)(2,1)S(1)}, u32[]{:S(2)}, u32[]{:S(2)}) collective-permute-start(bf16[128,256]{1,0:T(8,128)(2,1)S(1)} %constant_dynamic-update-slice_fusion.own_ref), channel_id=1, source_target_pairs={{0,4},{4,8},{8,12},{12,16},{16,20},{20,24},{24,28},{28,32},{32,36}... | collective-permute-start | bytes 196616 | tf_op jit(solution)/shard_map/attention/ppermute | solution.py:279
  26.7 0.1 copy.21.start_ref
  26.8 3.5 %collective-permute-done.before_ref = bf16[128,256]{1,0:T(8,128)(2,1)S(1)} collective-permute-done((bf16[128,256]{1,0:T(8,128)(2,1)S(1)}, bf16[128,256]{1,0:T(8,128)(2,1)S(1)}, u32[]{:S(2)}, u32[]{:S(2)}) %collective-permute-start) | collective-permute-done | bytes 65568 | tf_op jit(solution)/shard_map/attention/ppermute | solution.py:279
  30.3 0.0 copy-done.3
  30.3 7.8 %attention.1 = bf16[2,4,2,128,256]{4,3,2,1,0:T(8,128)(2,1)} custom-call(bf16[128,1024]{1,0:T(8,128)(2,1)S(1)} %copy-done.2, bf16[128,256]{1,0:T(8,128)(2,1)S(1)} %constant_dynamic-update-slice_fusion.own_ref, bf16[128,256]{1,0:T(8,128)(2,1)S(1)} %collective-permute-done.before_ref, s32[128,1]{1,0:T(8,128)S(1)} %copy.21.start_ref, f32[16]{0:T(128)S(1)} %copy-done.3), custom_call_target="tpu_custom_call" | custom-call | flops 2000000000 | bytes 2000000 | tf_op jit(solution)/shard_map/attention/pallas_call | solution.py:39
  38.1 0.0 all-to-all-done
  38.1 4.1 %collective-permute-start.2 = (bf16[256,720]{1,0:T(8,128)(2,1)S(1)}, bf16[256,720]{1,0:T(8,128)(2,1)S(1)}, u32[]{:S(2)}, u32[]{:S(2)}) collective-permute-start(bf16[256,720]{1,0:T(8,128)(2,1)S(1)} %bitcast.22), channel_id=1, source_target_pairs={{0,448},{64,0},{128,64},{192,128},{256,192},{320,256},{384,320},{4... | collective-permute-start | bytes 1105928 | tf_op jit(solution)/shard_map/projection_rows/ppermute | solution.py:34
  42.3 1.9 collective-permute-start.1
  44.2 6.4 %collective-permute-done.2.refs_2_ = bf16[256,720]{1,0:T(8,128)(2,1)S(1)} collective-permute-done((bf16[256,720]{1,0:T(8,128)(2,1)S(1)}, bf16[256,720]{1,0:T(8,128)(2,1)S(1)}, u32[]{:S(2)}, u32[]{:S(2)}) %collective-permute-start.2) | collective-permute-done | bytes 368672 | tf_op jit(solution)/shard_map/projection_rows/ppermute | solution.py:34
  50.6 3.8 %collective-permute-start.4 = (bf16[256,720]{1,0:T(8,128)(2,1)S(1)}, bf16[256,720]{1,0:T(8,128)(2,1)S(1)}, u32[]{:S(2)}, u32[]{:S(2)}) collective-permute-start(bf16[256,720]{1,0:T(8,128)(2,1)S(1)} %collective-permute-done.2.refs_2_), channel_id=1, source_target_pairs={{0,448},{64,0},{128,64},{192,128},{256,192},{320,256},{384,320},{4... | collective-permute-start | bytes 1105928 | tf_op jit(solution)/shard_map/projection_rows/ppermute | solution.py:34
  54.4 0.0 collective-permute-done.1.refs_1_
  54.4 1.9 collective-permute-start.3
  56.3 0.0 copy-start.7
  56.3 7.1 %all-to-all-start.1 = ((bf16[8,2,128,256]{3,2,1,0:T(8,128)(2,1)}), bf16[8,2,128,256]{3,2,1,0:T(8,128)(2,1)S(1)}, u32[]{:S(2)}, u32[]{:S(2)}) async-start(bf16[8,2,128,256]{3,2,1,0:T(8,128)(2,1)} %bitcast.11), calls=%async_computation.1 | async-start | bytes 2097152 | tf_op jit(solution)/shard_map/attention/all_to_all | solution.py:306
  63.4 0.0 collective-permute-done.4.refs_4_
  63.4 4.8 %collective-permute-start.6 = (bf16[256,720]{1,0:T(8,128)(2,1)S(1)}, bf16[256,720]{1,0:T(8,128)(2,1)S(1)}, u32[]{:S(2)}, u32[]{:S(2)}) collective-permute-start(bf16[256,720]{1,0:T(8,128)(2,1)S(1)} %collective-permute-done.4.refs_4_), channel_id=1, source_target_pairs={{0,448},{64,0},{128,64},{192,128},{256,192},{320,256},{384,320},{4... | collective-permute-start | bytes 1105928 | tf_op jit(solution)/shard_map/projection_rows/ppermute | solution.py:34
  68.3 0.0 collective-permute-done.3.refs_3_
  68.3 1.9 collective-permute-start.5
  70.2 5.7 %collective-permute-done.6.refs_6_ = bf16[256,720]{1,0:T(8,128)(2,1)S(1)} collective-permute-done((bf16[256,720]{1,0:T(8,128)(2,1)S(1)}, bf16[256,720]{1,0:T(8,128)(2,1)S(1)}, u32[]{:S(2)}, u32[]{:S(2)}) %collective-permute-start.6) | collective-permute-done | bytes 368672 | tf_op jit(solution)/shard_map/projection_rows/ppermute | solution.py:34
  76.0 0.7 slice.9
  76.7 5.4 %collective-permute-start.8 = (bf16[128,720]{1,0:T(8,128)(2,1)}, bf16[128,720]{1,0:T(8,128)(2,1)}, u32[]{:S(2)}, u32[]{:S(2)}) collective-permute-start(bf16[128,720]{1,0:T(8,128)(2,1)} %slice.9), channel_id=1, source_target_pairs={{0,448},{64,0},{128,64},{192,128},{256,192},{320,256},{384,320},{4... | collective-permute-start | bytes 552968 | tf_op jit(solution)/shard_map/projection_rows/ppermute | solution.py:34
  82.1 0.0 collective-permute-done.5.refs_5_
  82.1 0.7 slice.8
  82.8 1.9 collective-permute-start.7
  84.8 0.1 copy.23
  84.9 0.2 reduce_window_sum.11
  85.1 0.6 sub.33
  85.7 0.9 copy.25
  86.7 0.1 stack.39.index_ref
  86.8 0.0 all-to-all-done.1
  86.8 0.0 collective-permute-done.8.refs_8_
  86.8 4.2 %collective-permute-done.7.refs_7_ = bf16[128,720]{1,0:T(8,128)(2,1)} collective-permute-done((bf16[128,720]{1,0:T(8,128)(2,1)}, bf16[128,720]{1,0:T(8,128)(2,1)}, u32[]{:S(2)}, u32[]{:S(2)}) %collective-permute-start.7) | collective-permute-done | bytes 184352 | tf_op jit(solution)/shard_map/projection_rows/ppermute | solution.py:34
  91.0 3.0 %stream.2 = (f32[128,720]{1,0:T(8,128)S(1)}, f32[128,720]{1,0:T(8,128)}) custom-call(s32[9]{0:T(128)S(1)} %stack.39.index_ref, bf16[2,8,128,256]{3,2,1,0:T(8,128)(2,1)S(1)} %bitcast.21, bf16[256,720]{1,0:T(8,128)(2,1)S(1)} %bitcast.24, bf16[256,720]{1,0:T(8,128)(2,1)S(1)} %collective-permute-done.1.refs_1_, ...), custom_call_target="tpu_custom_call" | custom-call | flops 800000000 | bytes 4000000 | tf_op jit(solution)/shard_map/stream/pallas_call | solution.py:39
  94.0 0.8 copy-done
  94.8 4.6 %collective-permute-start.9 = (f32[128,720]{1,0:T(8,128)}, f32[128,720]{1,0:T(8,128)S(1)}, u32[]{:S(2)}, u32[]{:S(2)}) collective-permute-start(f32[128,720]{1,0:T(8,128)} %get-tuple-element.20), channel_id=1, source_target_pairs={{0,4},{4,0},{1,5},{5,1},{2,6},{6,2},{3,7},{7,3},{8,12},{12,8},{9,1... | collective-permute-start | bytes 1105928 | tf_op jit(solution)/shard_map/stream/ppermute | solution.py:34
  99.4 1.1 copy.22.residual_ref
  100.5 0.2 fusion.3.routing_ref
  100.7 0.2 collective-permute-done.9.got_ref
  100.9 1.0 copy-done.1
  101.9 0.2 stream.3
  102.1 0.5 dispatch.1
  102.6 49.8 %all_to_all.20 = bf16[256,9,2,128]{3,2,1,0:T(2,128)(2,1)S(1)} all-to-all(bf16[256,9,2,128]{3,2,1,0:T(2,128)(2,1)S(1)} %bitcast.19), channel_id=1, replica_groups=mesh['y'=8,'z'=8,'core'=2,'tp'=4] {'y','z','tp'}, dimensions={0} | all-to-all | bytes 2359296 | tf_op jit(solution)/shard_map/dispatch/all_to_all | solution.py:354
  152.5 5.1 %collective-permute-start.10 = (bf16[4608,128]{1,0:T(8,128)(2,1)S(1)}, bf16[4608,128]{1,0:T(8,128)(2,1)S(1)}, u32[]{:S(2)}, u32[]{:S(2)}) collective-permute-start(bf16[4608,128]{1,0:T(8,128)(2,1)S(1)} %bitcast.25), channel_id=1, source_target_pairs={{0,4},{4,0},{1,5},{5,1},{2,6},{6,2},{3,7},{7,3},{8,12},{12,8},{9,1... | collective-permute-start | bytes 3538952 | tf_op jit(solution)/shard_map/dispatch/ppermute | solution.py:34
  157.5 2.3 collective-permute-done.10.other_ref
  159.8 3.0 %all-gather.3.cloned.1.call-done = bf16[2880,2176]{1,0:T(8,128)(2,1)} async-done(((bf16[720,2176]{1,0:T(8,128)(2,1)}), bf16[2880,2176]{1,0:T(8,128)(2,1)}) %all-gather.3.cloned.1.call-update) | async-done | bytes 12533776 | tf_op jit(solution)/shard_map/expert_weights/all_gather | solution.py:269
  162.8 11.0 %experts.1 = (bf16[4608,128]{1,0:T(8,128)(2,1)S(1)}, bf16[4608,128]{1,0:T(8,128)(2,1)S(1)}) custom-call(bf16[4608,128]{1,0:T(8,128)(2,1)S(1)} %bitcast.26, bf16[4608,128]{1,0:T(8,128)(2,1)S(1)} %collective-permute-done.10.other_ref, bf16[4,720,2176]{2,1,0:T(8,128)(2,1)} %bitcast.27), custom_call_target="tpu_custom_call" | custom-call | flops 5000000000 | bytes 15000000 | tf_op jit(solution)/shard_map/experts/pallas_call | solution.py:39
  173.8 2.5 %collective-permute-start.11 = (bf16[4608,128]{1,0:T(8,128)(2,1)S(1)}, bf16[4608,128]{1,0:T(8,128)(2,1)S(1)}, u32[]{:S(2)}, u32[]{:S(2)}) collective-permute-start(bf16[4608,128]{1,0:T(8,128)(2,1)S(1)} %get-tuple-element.23), channel_id=1, source_target_pairs={{0,4},{4,0},{1,5},{5,1},{2,6},{6,2},{3,7},{7,3},{8,12},{12,8},{9,1... | collective-permute-start | bytes 3538952 | tf_op jit(solution)/shard_map/experts/ppermute | solution.py:34
  176.4 2.5 %collective-permute-done.11 = bf16[4608,128]{1,0:T(8,128)(2,1)S(1)} collective-permute-done((bf16[4608,128]{1,0:T(8,128)(2,1)S(1)}, bf16[4608,128]{1,0:T(8,128)(2,1)S(1)}, u32[]{:S(2)}, u32[]{:S(2)}) %collective-permute-start.11) | collective-permute-done | bytes 1179680 | tf_op jit(solution)/shard_map/experts/ppermute | solution.py:34
  178.8 1.4 add_convert_fusion
  180.2 18.8 %all-to-all-start.3 = ((bf16[256,9,2,128]{3,2,1,0:T(2,128)(2,1)}), bf16[256,9,2,128]{3,2,1,0:T(2,128)(2,1)S(1)}, u32[]{:S(2)}, u32[]{:S(2)}) async-start(bf16[256,9,2,128]{3,2,1,0:T(2,128)(2,1)} %bitcast.16), calls=%async_computation.3 | async-start | bytes 2359296 | tf_op jit(solution)/shard_map/combine/all_to_all | solution.py:354
  199.0 0.2 fusion.2.mixing_ref
  199.2 31.1 %all-to-all-done.3 = bf16[256,9,2,128]{3,2,1,0:T(2,128)(2,1)S(1)} async-done(((bf16[256,9,2,128]{3,2,1,0:T(2,128)(2,1)}), bf16[256,9,2,128]{3,2,1,0:T(2,128)(2,1)S(1)}, u32[]{:S(2)}, u32[]{:S(2)}) %all-to-all-start.3) | async-done | bytes 1179680 | tf_op jit(solution)/shard_map/combine/all_to_all | solution.py:354
  230.3 0.6 combine.1
  230.9 0.8 copy.26
  (20 shorter events, 0.1 us)
Async XLA Ops:
  6.5 156.3 %all-gather.3.cloned.1.call-start = ((), (), s32[]{:S(2)}) async-start(), calls=%async_computation.4 | async-start | bytes 15667200 | tf_op jit(solution)/shard_map/expert_weights/all_gather | solution.py:269
  9.6 0.8 copy-start.4
  10.4 11.7 %copy-start.5 = (bf16[128,128]{1,0:T(8,128)(2,1)S(1)}, bf16[128,128]{1,0:T(8,128)(2,1)}, u32[]{:S(2)}) copy-start(bf16[128,128]{1,0:T(8,128)(2,1)} %param.14) | copy-start | bytes 98308
  10.4 11.7 %copy-start.6 = (bf16[128,128]{1,0:T(8,128)(2,1)S(1)}, bf16[128,128]{1,0:T(8,128)(2,1)}, u32[]{:S(2)}) copy-start(bf16[128,128]{1,0:T(8,128)(2,1)} %param.15) | copy-start | bytes 98308
  10.4 16.2 %copy-start.10 = (s32[128]{0:T(128)S(1)}, s32[128]{0:T(128)}, u32[]{:S(2)}) copy-start(s32[128]{0:T(128)} %param.17) | copy-start | bytes 1540
  10.4 19.9 %copy-start.2 = (bf16[128,1024]{1,0:T(8,128)(2,1)S(1)}, bf16[128,1024]{1,0:T(8,128)(2,1)}, u32[]{:S(2)}) copy-start(bf16[128,1024]{1,0:T(8,128)(2,1)} %q_ref.1) | copy-start | bytes 786436
  10.4 19.9 %copy-start.3 = (f32[16]{0:T(128)S(1)}, f32[16]{0:T(128)}, u32[]{:S(2)}) copy-start(f32[16]{0:T(128)} %sink_ref.1) | copy-start | bytes 196
  11.2 26.9 %all-to-all-start = ((bf16[8,32,720]{2,1,0:T(8,128)(2,1)}), bf16[8,32,720]{2,1,0:T(8,128)(2,1)S(1)}, u32[]{:S(2)}, u32[]{:S(2)}) async-start(bf16[8,32,720]{2,1,0:T(8,128)(2,1)} %broadcast_in_dim.44), calls=%async_computation | async-start | bytes 786432 | tf_op jit(solution)/shard_map/projection_rows/all_to_all | solution.py:274
  22.1 8.2 %collective-permute-start = (bf16[128,256]{1,0:T(8,128)(2,1)S(1)}, bf16[128,256]{1,0:T(8,128)(2,1)S(1)}, u32[]{:S(2)}, u32[]{:S(2)}) collective-permute-start(bf16[128,256]{1,0:T(8,128)(2,1)S(1)} %constant_dynamic-update-slice_fusion.own_ref), channel_id=1, source_target_pairs={{0,4},{4,8},{8,12},{12,16},{16,20},{20,24},{24,28},{28,32},{32,36}... | collective-permute-start | bytes 196616 | tf_op jit(solution)/shard_map/attention/ppermute | solution.py:279
  38.1 12.4 %collective-permute-start.2 = (bf16[256,720]{1,0:T(8,128)(2,1)S(1)}, bf16[256,720]{1,0:T(8,128)(2,1)S(1)}, u32[]{:S(2)}, u32[]{:S(2)}) collective-permute-start(bf16[256,720]{1,0:T(8,128)(2,1)S(1)} %bitcast.22), channel_id=1, source_target_pairs={{0,448},{64,0},{128,64},{192,128},{256,192},{320,256},{384,320},{4... | collective-permute-start | bytes 1105928 | tf_op jit(solution)/shard_map/projection_rows/ppermute | solution.py:34
  42.3 12.1 %collective-permute-start.1 = (bf16[256,720]{1,0:T(8,128)(2,1)S(1)}, bf16[256,720]{1,0:T(8,128)(2,1)S(1)}, u32[]{:S(2)}, u32[]{:S(2)}) collective-permute-start(bf16[256,720]{1,0:T(8,128)(2,1)S(1)} %bitcast.23), channel_id=1, source_target_pairs={{0,64},{64,128},{128,192},{192,256},{256,320},{320,384},{384,448},... | collective-permute-start | bytes 1105928 | tf_op jit(solution)/shard_map/projection_rows/ppermute | solution.py:34
  50.6 12.8 %collective-permute-start.4 = (bf16[256,720]{1,0:T(8,128)(2,1)S(1)}, bf16[256,720]{1,0:T(8,128)(2,1)S(1)}, u32[]{:S(2)}, u32[]{:S(2)}) collective-permute-start(bf16[256,720]{1,0:T(8,128)(2,1)S(1)} %collective-permute-done.2.refs_2_), channel_id=1, source_target_pairs={{0,448},{64,0},{128,64},{192,128},{256,192},{320,256},{384,320},{4... | collective-permute-start | bytes 1105928 | tf_op jit(solution)/shard_map/projection_rows/ppermute | solution.py:34
  54.4 13.9 %collective-permute-start.3 = (bf16[256,720]{1,0:T(8,128)(2,1)S(1)}, bf16[256,720]{1,0:T(8,128)(2,1)}, u32[]{:S(2)}, u32[]{:S(2)}) collective-permute-start(bf16[256,720]{1,0:T(8,128)(2,1)S(1)} %collective-permute-done.1.refs_1_), channel_id=1, source_target_pairs={{0,64},{64,128},{128,192},{192,256},{256,320},{320,384},{384,448},... | collective-permute-start | bytes 1105928 | tf_op jit(solution)/shard_map/projection_rows/ppermute | solution.py:34
  56.3 28.4 %copy-start.7 = (s32[128,4]{0,1:T(4,128)S(1)}, s32[128,4]{0,1:T(4,128)}, u32[]{:S(2)}) copy-start(s32[128,4]{0,1:T(4,128)} %param.21) | copy-start | bytes 6148
  56.3 30.4 %all-to-all-start.1 = ((bf16[8,2,128,256]{3,2,1,0:T(8,128)(2,1)}), bf16[8,2,128,256]{3,2,1,0:T(8,128)(2,1)S(1)}, u32[]{:S(2)}, u32[]{:S(2)}) async-start(bf16[8,2,128,256]{3,2,1,0:T(8,128)(2,1)} %bitcast.11), calls=%async_computation.1 | async-start | bytes 2097152 | tf_op jit(solution)/shard_map/attention/all_to_all | solution.py:306
  63.4 12.5 %collective-permute-start.6 = (bf16[256,720]{1,0:T(8,128)(2,1)S(1)}, bf16[256,720]{1,0:T(8,128)(2,1)S(1)}, u32[]{:S(2)}, u32[]{:S(2)}) collective-permute-start(bf16[256,720]{1,0:T(8,128)(2,1)S(1)} %collective-permute-done.4.refs_4_), channel_id=1, source_target_pairs={{0,448},{64,0},{128,64},{192,128},{256,192},{320,256},{384,320},{4... | collective-permute-start | bytes 1105928 | tf_op jit(solution)/shard_map/projection_rows/ppermute | solution.py:34
  68.3 13.8 %collective-permute-start.5 = (bf16[256,720]{1,0:T(8,128)(2,1)}, bf16[256,720]{1,0:T(8,128)(2,1)S(1)}, u32[]{:S(2)}, u32[]{:S(2)}) collective-permute-start(bf16[256,720]{1,0:T(8,128)(2,1)} %collective-permute-done.3.refs_3_), channel_id=1, source_target_pairs={{0,64},{64,128},{128,192},{192,256},{256,320},{320,384},{384,448},... | collective-permute-start | bytes 1105928 | tf_op jit(solution)/shard_map/projection_rows/ppermute | solution.py:34
  76.7 10.1 %collective-permute-start.8 = (bf16[128,720]{1,0:T(8,128)(2,1)}, bf16[128,720]{1,0:T(8,128)(2,1)}, u32[]{:S(2)}, u32[]{:S(2)}) collective-permute-start(bf16[128,720]{1,0:T(8,128)(2,1)} %slice.9), channel_id=1, source_target_pairs={{0,448},{64,0},{128,64},{192,128},{256,192},{320,256},{384,320},{4... | collective-permute-start | bytes 552968 | tf_op jit(solution)/shard_map/projection_rows/ppermute | solution.py:34
  82.8 8.2 %collective-permute-start.7 = (bf16[128,720]{1,0:T(8,128)(2,1)}, bf16[128,720]{1,0:T(8,128)(2,1)}, u32[]{:S(2)}, u32[]{:S(2)}) collective-permute-start(bf16[128,720]{1,0:T(8,128)(2,1)} %slice.8), channel_id=1, source_target_pairs={{0,64},{64,128},{128,192},{192,256},{256,320},{320,384},{384,448},... | collective-permute-start | bytes 552968 | tf_op jit(solution)/shard_map/projection_rows/ppermute | solution.py:34
  91.0 8.4 %copy-start.8 = (f32[720]{0:T(1024)S(1)}, f32[720]{0:T(1024)}, u32[]{:S(2)}) copy-start(f32[720]{0:T(1024)} %param.20) | copy-start | bytes 8644
  94.0 0.8 copy-start
  94.8 6.1 %collective-permute-start.9 = (f32[128,720]{1,0:T(8,128)}, f32[128,720]{1,0:T(8,128)S(1)}, u32[]{:S(2)}, u32[]{:S(2)}) collective-permute-start(f32[128,720]{1,0:T(8,128)} %get-tuple-element.20), channel_id=1, source_target_pairs={{0,4},{4,0},{1,5},{5,1},{2,6},{6,2},{3,7},{7,3},{8,12},{12,8},{9,1... | collective-permute-start | bytes 1105928 | tf_op jit(solution)/shard_map/stream/ppermute | solution.py:34
  100.9 1.0 copy-start.1
  152.5 7.3 %collective-permute-start.10 = (bf16[4608,128]{1,0:T(8,128)(2,1)S(1)}, bf16[4608,128]{1,0:T(8,128)(2,1)S(1)}, u32[]{:S(2)}, u32[]{:S(2)}) collective-permute-start(bf16[4608,128]{1,0:T(8,128)(2,1)S(1)} %bitcast.25), channel_id=1, source_target_pairs={{0,4},{4,0},{1,5},{5,1},{2,6},{6,2},{3,7},{7,3},{8,12},{12,8},{9,1... | collective-permute-start | bytes 3538952 | tf_op jit(solution)/shard_map/dispatch/ppermute | solution.py:34
  173.8 5.0 %collective-permute-start.11 = (bf16[4608,128]{1,0:T(8,128)(2,1)S(1)}, bf16[4608,128]{1,0:T(8,128)(2,1)S(1)}, u32[]{:S(2)}, u32[]{:S(2)}) collective-permute-start(bf16[4608,128]{1,0:T(8,128)(2,1)S(1)} %get-tuple-element.23), channel_id=1, source_target_pairs={{0,4},{4,0},{1,5},{5,1},{2,6},{6,2},{3,7},{7,3},{8,12},{12,8},{9,1... | collective-permute-start | bytes 3538952 | tf_op jit(solution)/shard_map/experts/ppermute | solution.py:34
  180.2 18.8 %copy-start.9 = (bf16[128,4]{0,1:T(4,128)(2,1)S(1)}, bf16[128,4]{0,1:T(4,128)(2,1)}, u32[]{:S(2)}) copy-start(bf16[128,4]{0,1:T(4,128)(2,1)} %param.22) | copy-start | bytes 3076
  180.2 50.1 %all-to-all-start.3 = ((bf16[256,9,2,128]{3,2,1,0:T(2,128)(2,1)}), bf16[256,9,2,128]{3,2,1,0:T(2,128)(2,1)S(1)}, u32[]{:S(2)}, u32[]{:S(2)}) async-start(bf16[256,9,2,128]{3,2,1,0:T(2,128)(2,1)} %bitcast.16), calls=%async_computation.3 | async-start | bytes 2359296 | tf_op jit(solution)/shard_map/combine/all_to_all | solution.py:354
Sparse Core Ops, SparseCore 0:
  9.8 153.0 all-gather.2

commit v7 on v6

--- a/solution.py
+++ b/solution.py
@@ -170,8 +170,36 @@
         copy.wait()
 
 
+def give_back(part, main_of, ends_of, flat):
+    for t in range(TP):
+        made = jnp.dot(part, main_of(t), preferred_element_type=F32)
+        last = jnp.dot(part, ends_of(t), preferred_element_type=F32)
+        last = jnp.concatenate(
+            [last[:, 2 * TAIL : 3 * TAIL], jnp.zeros((SLOTS, 128 - TAIL), F32)], axis=1
+        )
+        for k in range(CLASS_SLOTS):
+            group = slice(k * EXPERTS, (k + 1) * EXPERTS)
+            for b in range(6):
+                piece = made[group, b * 128 : (b + 1) * 128] if b < 5 else last[group]
+                flat[pl.ds(t * CHUNK + k * 6 + b, EXPERTS, stride=TP * CHUNK), :] = piece
+
+
+def down_kernel(active_ref, weights_ref, out_ref, flat, w, sems):
+    columns = pl.ds(2 * MAIN, PACKED - 2 * MAIN)
+    copies = [
+        pltpu.make_async_copy(weights_ref.at[t, :, columns], w.at[t], sems.at[t])
+        for t in range(TP)
+    ]
+    for copy in copies:
+        copy.start()
+    for copy in copies:
+        copy.wait()
+    give_back(active_ref[...], lambda t: w[t, :, :MAIN], lambda t: w[t, :, MAIN:], flat)
+    out_ref[...] = flat[...].astype(BF16)
+
+
 def expert_kernel(
-    mine_ref, other_ref, weights_ref, to_mine_ref, to_other_ref, flat, rows, w, sems
+    mine_ref, other_ref, weights_ref, active_ref, to_other_ref, flat, rows, w, sems
 ):
     copies = [pltpu.make_async_copy(weights_ref.at[t], w.at[t], sems.at[t]) for t in range(TP)]
     for copy in copies:
@@ -200,20 +228,14 @@
     gate = jnp.concatenate([sums[:, :MAIN], ends[:, :TAIL]], axis=1) * scale
     up = jnp.concatenate([sums[:, MAIN:], ends[:, TAIL : 2 * TAIL]], axis=1) * scale
     active = (gate / (1.0 + jnp.exp(-gate)) * up).astype(BF16)
-    for n, ref in enumerate((to_mine_ref, to_other_ref)):
-        part = active[n * SLOTS : (n + 1) * SLOTS]
-        for t in range(TP):
-            made = jnp.dot(part, w[t, :, 2 * MAIN : 3 * MAIN], preferred_element_type=F32)
-            last = jnp.dot(part, w[t, :, 3 * MAIN :], preferred_element_type=F32)
-            last = jnp.concatenate(
-                [last[:, 2 * TAIL : 3 * TAIL], jnp.zeros((SLOTS, 128 - TAIL), F32)], axis=1
-            )
-            for k in range(CLASS_SLOTS):
-                group = slice(k * EXPERTS, (k + 1) * EXPERTS)
-                for b in range(6):
-                    piece = made[group, b * 128 : (b + 1) * 128] if b < 5 else last[group]
-                    flat[pl.ds(t * CHUNK + k * 6 + b, EXPERTS, stride=TP * CHUNK), :] = piece
-        ref[...] = flat[...].astype(BF16)
+    active_ref[...] = active[:SLOTS]
+    give_back(
+        active[SLOTS:],
+        lambda t: w[t, :, 2 * MAIN : 3 * MAIN],
+        lambda t: w[t, :, 3 * MAIN :],
+        flat,
+    )
+    to_other_ref[...] = flat[...].astype(BF16)
 
 
 def combine_kernel(back_ref, mixing_ref, stream_ref, out_ref, flat):
@@ -361,9 +383,9 @@
         partner = shifted(arrived, "core", 1)
 
     with jax.named_scope("experts"):
-        to_mine, to_other = call(
+        active, to_other = call(
             expert_kernel,
-            [flat_shape] * 2,
+            [jax.ShapeDtypeStruct((SLOTS, QUARTER), BF16), flat_shape],
             (arrived, partner, weights),
             scratch=[
                 flat_scratch,
@@ -377,6 +399,20 @@
             limit=48,
         )
         received = shifted(to_other, "core", 1)
+        to_mine = call(
+            down_kernel,
+            flat_shape,
+            (active, weights),
+            scratch=[
+                flat_scratch,
+                pltpu.VMEM((TP, QUARTER, PACKED - 2 * MAIN), BF16),
+                pltpu.SemaphoreType.DMA((TP,)),
+            ],
+            spaces=[pltpu.VMEM, pltpu.HBM],
+            flops=1_000_000_000,
+            moved=6_000_000,
+            limit=48,
+        )
         both = (to_mine.astype(F32) + received.astype(F32)).astype(BF16)
 
     with jax.named_scope("combine"):

time: 241 us -> 241 us (level)
  Pallas kernels: 26.3 us -> 29.2 us
    pallas_call x7 -> x8, Pallas kernels: 26.3 us -> 29.2 us  [call(): pl.pallas_call(kernel, out_shape=out_shape, in_specs=[pl.BlockSpec(memory...]
    ppermute x11, waiting for transfers between devices: 21.3 us -> 18.8 us  [shifted(): lax.ppermute(block, axis, [(i, (i + distance) % size) for i in range(size)])]
  transfers between devices with their start and end apart: 16 -> 16, of which waited for: 9 -> 8; matrix products, arithmetic and copies ran while one was open for 2% -> 2% of each run, Pallas kernels for 5% -> 7%
where the time goes in v7:
time: 241 us; the launch traced here: 240 us
  starting transfers between devices  79.3 us (33%)
  waiting for transfers between devices  56.8 us (24%)
  blocking collectives  49.8 us (21%)
  Pallas kernels  29.2 us (12%)
  between operations  13.9 us (6%)
  local copies, waits for them, and re-layouts  7.83 us (3%)
  other arithmetic  2.64 us (1%)
    all_to_all x1, blocking collectives, exchanged(): lax.all_to_all(block, PLANE, 0, 0, tiled=True).reshape(flat_shape.shape)  49.8 us
    ppermute x11, starting transfers between devices, shifted(): lax.ppermute(block, axis, [(i, (i + distance) % size) for i in range(size)])  38.1 us
    all_to_all x1, waiting for transfers between devices, exchanged(): lax.all_to_all(block, PLANE, 0, 0, tiled=True).reshape(flat_shape.shape)  31.5 us
    pallas_call x8, Pallas kernels, call(): pl.pallas_call(kernel, out_shape=out_shape, in_specs=[pl.BlockSpec(memory...  29.2 us
    all_to_all x1, starting transfers between devices, exchanged(): lax.all_to_all(block, PLANE, 0, 0, tiled=True).reshape(flat_shape.shape)  18.8 us
    ppermute x11, waiting for transfers between devices, shifted(): lax.ppermute(block, axis, [(i, (i + distance) % size) for i in range(size)])  18.8 us
    all_to_all x1, starting transfers between devices, shards(): column = lax.all_to_all(spread, 'z', 0, 0, tiled=True)  10.9 us
    all_to_all x1, starting transfers between devices, shards(): lax.all_to_all(heads.reshape(2 * TP, 2, count, GROUPS * HALF), ('core', '...  7.05 us
  transfers between devices with their start and end apart: 16, of which 8 were waited for; matrix products, arithmetic and copies ran while one was open for 2% of the time, Pallas kernels for 7%

profile of v7, /device:TPU:1, one launch (start us, length us, event | category | flops | bytes accessed | tf_op | source)
XLA Modules:
  0.0 239.5 jit_solution(10452502486025462031)
XLA Ops:
  6.5 0.0 all-gather.3.cloned.1.call-start
  6.5 3.1 %expert_weights.1 = bf16[720,2176]{1,0:T(8,128)(2,1)} custom-call(bf16[720,720]{1,0:T(8,128)(2,1)} %gate_ref.1, bf16[720,720]{1,0:T(8,128)(2,1)} %up_ref.1, bf16[720,720]{1,0:T(8,128)(2,1)} %down_ref.1), custom_call_target="tpu_custom_call" | custom-call | tf_op jit(solution)/shard_map/expert_weights/pallas_call | solution.py:39
  9.6 0.0 copy-start.4
  9.6 0.0 all-gather.3.cloned.1.call-update
  9.7 0.8 copy-done.4
  10.4 0.0 copy-start.3
  10.4 0.8 broadcast_in_dim.44
  11.2 10.9 %all-to-all-start = ((bf16[8,32,720]{2,1,0:T(8,128)(2,1)}), bf16[8,32,720]{2,1,0:T(8,128)(2,1)S(1)}, u32[]{:S(2)}, u32[]{:S(2)}) async-start(bf16[8,32,720]{2,1,0:T(8,128)(2,1)} %broadcast_in_dim.44), calls=%async_computation | async-start | bytes 786432 | tf_op jit(solution)/shard_map/projection_rows/all_to_all | solution.py:296
  22.1 0.0 copy-done.5
  22.1 4.5 %collective-permute-start = (bf16[128,256]{1,0:T(8,128)(2,1)S(1)}, bf16[128,256]{1,0:T(8,128)(2,1)S(1)}, u32[]{:S(2)}, u32[]{:S(2)}) collective-permute-start(bf16[128,256]{1,0:T(8,128)(2,1)S(1)} %constant_dynamic-update-slice_fusion.own_ref), channel_id=1, source_target_pairs={{0,4},{4,8},{8,12},{12,16},{16,20},{20,24},{24,28},{28,32},{32,36}... | collective-permute-start | bytes 196616 | tf_op jit(solution)/shard_map/attention/ppermute | solution.py:301
  26.6 0.0 copy-done.10
  26.7 0.1 copy.21.start_ref
  26.8 3.5 %collective-permute-done.before_ref = bf16[128,256]{1,0:T(8,128)(2,1)S(1)} collective-permute-done((bf16[128,256]{1,0:T(8,128)(2,1)S(1)}, bf16[128,256]{1,0:T(8,128)(2,1)S(1)}, u32[]{:S(2)}, u32[]{:S(2)}) %collective-permute-start) | collective-permute-done | bytes 65568 | tf_op jit(solution)/shard_map/attention/ppermute | solution.py:301
  30.3 7.8 %attention.1 = bf16[2,4,2,128,256]{4,3,2,1,0:T(8,128)(2,1)} custom-call(bf16[128,1024]{1,0:T(8,128)(2,1)S(1)} %copy-done.2, bf16[128,256]{1,0:T(8,128)(2,1)S(1)} %constant_dynamic-update-slice_fusion.own_ref, bf16[128,256]{1,0:T(8,128)(2,1)S(1)} %collective-permute-done.before_ref, s32[128,1]{1,0:T(8,128)S(1)} %copy.21.start_ref, f32[16]{0:T(128)S(1)} %copy-done.3), custom_call_target="tpu_custom_call" | custom-call | flops 2000000000 | bytes 2000000 | tf_op jit(solution)/shard_map/attention/pallas_call | solution.py:39
  38.1 0.0 all-to-all-done
  38.1 4.2 %collective-permute-start.2 = (bf16[256,720]{1,0:T(8,128)(2,1)S(1)}, bf16[256,720]{1,0:T(8,128)(2,1)S(1)}, u32[]{:S(2)}, u32[]{:S(2)}) collective-permute-start(bf16[256,720]{1,0:T(8,128)(2,1)S(1)} %bitcast.22), channel_id=1, source_target_pairs={{0,448},{64,0},{128,64},{192,128},{256,192},{320,256},{384,320},{4... | collective-permute-start | bytes 1105928 | tf_op jit(solution)/shard_map/projection_rows/ppermute | solution.py:34
  42.3 1.9 collective-permute-start.1
  44.2 6.3 %collective-permute-done.2.refs_2_ = bf16[256,720]{1,0:T(8,128)(2,1)S(1)} collective-permute-done((bf16[256,720]{1,0:T(8,128)(2,1)S(1)}, bf16[256,720]{1,0:T(8,128)(2,1)S(1)}, u32[]{:S(2)}, u32[]{:S(2)}) %collective-permute-start.2) | collective-permute-done | bytes 368672 | tf_op jit(solution)/shard_map/projection_rows/ppermute | solution.py:34
  50.5 3.9 %collective-permute-start.4 = (bf16[256,720]{1,0:T(8,128)(2,1)S(1)}, bf16[256,720]{1,0:T(8,128)(2,1)S(1)}, u32[]{:S(2)}, u32[]{:S(2)}) collective-permute-start(bf16[256,720]{1,0:T(8,128)(2,1)S(1)} %collective-permute-done.2.refs_2_), channel_id=1, source_target_pairs={{0,448},{64,0},{128,64},{192,128},{256,192},{320,256},{384,320},{4... | collective-permute-start | bytes 1105928 | tf_op jit(solution)/shard_map/projection_rows/ppermute | solution.py:34
  54.4 0.0 collective-permute-done.1.refs_1_
  54.4 1.9 collective-permute-start.3
  56.4 0.0 copy-start.7
  56.4 7.1 %all-to-all-start.1 = ((bf16[8,2,128,256]{3,2,1,0:T(8,128)(2,1)}), bf16[8,2,128,256]{3,2,1,0:T(8,128)(2,1)S(1)}, u32[]{:S(2)}, u32[]{:S(2)}) async-start(bf16[8,2,128,256]{3,2,1,0:T(8,128)(2,1)} %bitcast.11), calls=%async_computation.1 | async-start | bytes 2097152 | tf_op jit(solution)/shard_map/attention/all_to_all | solution.py:328
  63.4 0.0 collective-permute-done.4.refs_4_
  63.4 4.8 %collective-permute-start.6 = (bf16[256,720]{1,0:T(8,128)(2,1)S(1)}, bf16[256,720]{1,0:T(8,128)(2,1)S(1)}, u32[]{:S(2)}, u32[]{:S(2)}) collective-permute-start(bf16[256,720]{1,0:T(8,128)(2,1)S(1)} %collective-permute-done.4.refs_4_), channel_id=1, source_target_pairs={{0,448},{64,0},{128,64},{192,128},{256,192},{320,256},{384,320},{4... | collective-permute-start | bytes 1105928 | tf_op jit(solution)/shard_map/projection_rows/ppermute | solution.py:34
  68.3 0.0 collective-permute-done.3.refs_3_
  68.3 1.9 collective-permute-start.5
  70.2 5.7 %collective-permute-done.6.refs_6_ = bf16[256,720]{1,0:T(8,128)(2,1)S(1)} collective-permute-done((bf16[256,720]{1,0:T(8,128)(2,1)S(1)}, bf16[256,720]{1,0:T(8,128)(2,1)S(1)}, u32[]{:S(2)}, u32[]{:S(2)}) %collective-permute-start.6) | collective-permute-done | bytes 368672 | tf_op jit(solution)/shard_map/projection_rows/ppermute | solution.py:34
  75.9 0.7 slice.9
  76.6 5.4 %collective-permute-start.8 = (bf16[128,720]{1,0:T(8,128)(2,1)}, bf16[128,720]{1,0:T(8,128)(2,1)}, u32[]{:S(2)}, u32[]{:S(2)}) collective-permute-start(bf16[128,720]{1,0:T(8,128)(2,1)} %slice.9), channel_id=1, source_target_pairs={{0,448},{64,0},{128,64},{192,128},{256,192},{320,256},{384,320},{4... | collective-permute-start | bytes 552968 | tf_op jit(solution)/shard_map/projection_rows/ppermute | solution.py:34
  82.1 0.0 collective-permute-done.5.refs_5_
  82.1 0.7 slice.8
  82.8 1.9 collective-permute-start.7
  84.8 0.1 copy.23
  84.9 0.2 reduce_window_sum.11
  85.1 0.6 sub.33
  85.7 0.9 copy.25
  86.7 0.1 stack.39.index_ref
  86.7 0.0 all-to-all-done.1
  86.8 0.0 collective-permute-done.8.refs_8_
  86.8 4.2 %collective-permute-done.7.refs_7_ = bf16[128,720]{1,0:T(8,128)(2,1)} collective-permute-done((bf16[128,720]{1,0:T(8,128)(2,1)}, bf16[128,720]{1,0:T(8,128)(2,1)}, u32[]{:S(2)}, u32[]{:S(2)}) %collective-permute-start.7) | collective-permute-done | bytes 184352 | tf_op jit(solution)/shard_map/projection_rows/ppermute | solution.py:34
  91.0 3.0 %stream.2 = (f32[128,720]{1,0:T(8,128)S(1)}, f32[128,720]{1,0:T(8,128)}) custom-call(s32[9]{0:T(128)S(1)} %stack.39.index_ref, bf16[2,8,128,256]{3,2,1,0:T(8,128)(2,1)S(1)} %bitcast.21, bf16[256,720]{1,0:T(8,128)(2,1)S(1)} %bitcast.24, bf16[256,720]{1,0:T(8,128)(2,1)S(1)} %collective-permute-done.1.refs_1_, ...), custom_call_target="tpu_custom_call" | custom-call | flops 800000000 | bytes 4000000 | tf_op jit(solution)/shard_map/stream/pallas_call | solution.py:39
  94.0 0.8 copy-done
  94.7 4.6 %collective-permute-start.9 = (f32[128,720]{1,0:T(8,128)}, f32[128,720]{1,0:T(8,128)S(1)}, u32[]{:S(2)}, u32[]{:S(2)}) collective-permute-start(f32[128,720]{1,0:T(8,128)} %get-tuple-element.20), channel_id=1, source_target_pairs={{0,4},{4,0},{1,5},{5,1},{2,6},{6,2},{3,7},{7,3},{8,12},{12,8},{9,1... | collective-permute-start | bytes 1105928 | tf_op jit(solution)/shard_map/stream/ppermute | solution.py:34
  99.4 1.1 copy.22.residual_ref
  100.5 0.2 fusion.3.routing_ref
  100.7 0.2 collective-permute-done.9.got_ref
  100.9 1.0 copy-done.1
  101.9 0.2 stream.3
  102.1 0.5 dispatch.1
  102.7 49.8 %all_to_all.20 = bf16[256,9,2,128]{3,2,1,0:T(2,128)(2,1)S(1)} all-to-all(bf16[256,9,2,128]{3,2,1,0:T(2,128)(2,1)S(1)} %bitcast.19), channel_id=1, replica_groups=mesh['y'=8,'z'=8,'core'=2,'tp'=4] {'y','z','tp'}, dimensions={0} | all-to-all | bytes 2359296 | tf_op jit(solution)/shard_map/dispatch/all_to_all | solution.py:376
  152.4 5.0 %collective-permute-start.10 = (bf16[4608,128]{1,0:T(8,128)(2,1)S(1)}, bf16[4608,128]{1,0:T(8,128)(2,1)S(1)}, u32[]{:S(2)}, u32[]{:S(2)}) collective-permute-start(bf16[4608,128]{1,0:T(8,128)(2,1)S(1)} %bitcast.25), channel_id=1, source_target_pairs={{0,4},{4,0},{1,5},{5,1},{2,6},{6,2},{3,7},{7,3},{8,12},{12,8},{9,1... | collective-permute-start | bytes 3538952 | tf_op jit(solution)/shard_map/dispatch/ppermute | solution.py:34
  157.5 2.3 collective-permute-done.10.other_ref
  159.8 3.1 %all-gather.3.cloned.1.call-done = bf16[2880,2176]{1,0:T(8,128)(2,1)} async-done(((bf16[720,2176]{1,0:T(8,128)(2,1)}), bf16[2880,2176]{1,0:T(8,128)(2,1)}) %all-gather.3.cloned.1.call-update) | async-done | bytes 12533776 | tf_op jit(solution)/shard_map/expert_weights/all_gather | solution.py:291
  162.9 9.8 %experts.2 = (bf16[192,720]{1,0:T(8,128)(2,1)S(1)}, bf16[4608,128]{1,0:T(8,128)(2,1)S(1)}) custom-call(bf16[4608,128]{1,0:T(8,128)(2,1)S(1)} %bitcast.26, bf16[4608,128]{1,0:T(8,128)(2,1)S(1)} %collective-permute-done.10.other_ref, bf16[4,720,2176]{2,1,0:T(8,128)(2,1)} %bitcast.27), custom_call_target="tpu_custom_call" | custom-call | flops 5000000000 | bytes 15000000 | tf_op jit(solution)/shard_map/experts/pallas_call | solution.py:39
  172.7 2.5 %collective-permute-start.11 = (bf16[4608,128]{1,0:T(8,128)(2,1)S(1)}, bf16[4608,128]{1,0:T(8,128)(2,1)S(1)}, u32[]{:S(2)}, u32[]{:S(2)}) collective-permute-start(bf16[4608,128]{1,0:T(8,128)(2,1)S(1)} %get-tuple-element.23), channel_id=1, source_target_pairs={{0,4},{4,0},{1,5},{5,1},{2,6},{6,2},{3,7},{7,3},{8,12},{12,8},{9,1... | collective-permute-start | bytes 3538952 | tf_op jit(solution)/shard_map/experts/ppermute | solution.py:34
  175.2 4.2 %experts.3 = bf16[4608,128]{1,0:T(8,128)(2,1)S(1)} custom-call(bf16[192,720]{1,0:T(8,128)(2,1)S(1)} %get-tuple-element.22.active_ref, bf16[4,720,2176]{2,1,0:T(8,128)(2,1)} %bitcast.28), custom_call_target="tpu_custom_call" | custom-call | flops 1000000000 | bytes 6000000 | tf_op jit(solution)/shard_map/experts/pallas_call | solution.py:39
  179.4 0.0 collective-permute-done.11
  179.4 1.4 add_convert_fusion
  180.7 18.8 %all-to-all-start.3 = ((bf16[256,9,2,128]{3,2,1,0:T(2,128)(2,1)}), bf16[256,9,2,128]{3,2,1,0:T(2,128)(2,1)S(1)}, u32[]{:S(2)}, u32[]{:S(2)}) async-start(bf16[256,9,2,128]{3,2,1,0:T(2,128)(2,1)} %bitcast.16), calls=%async_computation.3 | async-start | bytes 2359296 | tf_op jit(solution)/shard_map/combine/all_to_all | solution.py:376
  199.5 0.2 fusion.2.mixing_ref
  199.8 31.5 %all-to-all-done.3 = bf16[256,9,2,128]{3,2,1,0:T(2,128)(2,1)S(1)} async-done(((bf16[256,9,2,128]{3,2,1,0:T(2,128)(2,1)}), bf16[256,9,2,128]{3,2,1,0:T(2,128)(2,1)S(1)}, u32[]{:S(2)}, u32[]{:S(2)}) %all-to-all-start.3) | async-done | bytes 1179680 | tf_op jit(solution)/shard_map/combine/all_to_all | solution.py:376
  231.2 0.6 combine.1
  231.9 0.8 copy.26
  (21 shorter events, 0.1 us)
Async XLA Ops:
  6.5 156.3 %all-gather.3.cloned.1.call-start = ((), (), s32[]{:S(2)}) async-start(), calls=%async_computation.4 | async-start | bytes 15667200 | tf_op jit(solution)/shard_map/expert_weights/all_gather | solution.py:291
  9.6 0.8 copy-start.4
  10.4 11.7 %copy-start.5 = (bf16[128,128]{1,0:T(8,128)(2,1)S(1)}, bf16[128,128]{1,0:T(8,128)(2,1)}, u32[]{:S(2)}) copy-start(bf16[128,128]{1,0:T(8,128)(2,1)} %param.14) | copy-start | bytes 98308
  10.4 11.7 %copy-start.6 = (bf16[128,128]{1,0:T(8,128)(2,1)S(1)}, bf16[128,128]{1,0:T(8,128)(2,1)}, u32[]{:S(2)}) copy-start(bf16[128,128]{1,0:T(8,128)(2,1)} %param.15) | copy-start | bytes 98308
  10.4 16.2 %copy-start.10 = (s32[128]{0:T(128)S(1)}, s32[128]{0:T(128)}, u32[]{:S(2)}) copy-start(s32[128]{0:T(128)} %param.17) | copy-start | bytes 1540
  10.4 19.9 %copy-start.2 = (bf16[128,1024]{1,0:T(8,128)(2,1)S(1)}, bf16[128,1024]{1,0:T(8,128)(2,1)}, u32[]{:S(2)}) copy-start(bf16[128,1024]{1,0:T(8,128)(2,1)} %q_ref.1) | copy-start | bytes 786436
  10.4 19.9 %copy-start.3 = (f32[16]{0:T(128)S(1)}, f32[16]{0:T(128)}, u32[]{:S(2)}) copy-start(f32[16]{0:T(128)} %sink_ref.1) | copy-start | bytes 196
  11.2 26.9 %all-to-all-start = ((bf16[8,32,720]{2,1,0:T(8,128)(2,1)}), bf16[8,32,720]{2,1,0:T(8,128)(2,1)S(1)}, u32[]{:S(2)}, u32[]{:S(2)}) async-start(bf16[8,32,720]{2,1,0:T(8,128)(2,1)} %broadcast_in_dim.44), calls=%async_computation | async-start | bytes 786432 | tf_op jit(solution)/shard_map/projection_rows/all_to_all | solution.py:296
  22.1 8.2 %collective-permute-start = (bf16[128,256]{1,0:T(8,128)(2,1)S(1)}, bf16[128,256]{1,0:T(8,128)(2,1)S(1)}, u32[]{:S(2)}, u32[]{:S(2)}) collective-permute-start(bf16[128,256]{1,0:T(8,128)(2,1)S(1)} %constant_dynamic-update-slice_fusion.own_ref), channel_id=1, source_target_pairs={{0,4},{4,8},{8,12},{12,16},{16,20},{20,24},{24,28},{28,32},{32,36}... | collective-permute-start | bytes 196616 | tf_op jit(solution)/shard_map/attention/ppermute | solution.py:301
  38.1 12.4 %collective-permute-start.2 = (bf16[256,720]{1,0:T(8,128)(2,1)S(1)}, bf16[256,720]{1,0:T(8,128)(2,1)S(1)}, u32[]{:S(2)}, u32[]{:S(2)}) collective-permute-start(bf16[256,720]{1,0:T(8,128)(2,1)S(1)} %bitcast.22), channel_id=1, source_target_pairs={{0,448},{64,0},{128,64},{192,128},{256,192},{320,256},{384,320},{4... | collective-permute-start | bytes 1105928 | tf_op jit(solution)/shard_map/projection_rows/ppermute | solution.py:34
  42.3 12.1 %collective-permute-start.1 = (bf16[256,720]{1,0:T(8,128)(2,1)S(1)}, bf16[256,720]{1,0:T(8,128)(2,1)S(1)}, u32[]{:S(2)}, u32[]{:S(2)}) collective-permute-start(bf16[256,720]{1,0:T(8,128)(2,1)S(1)} %bitcast.23), channel_id=1, source_target_pairs={{0,64},{64,128},{128,192},{192,256},{256,320},{320,384},{384,448},... | collective-permute-start | bytes 1105928 | tf_op jit(solution)/shard_map/projection_rows/ppermute | solution.py:34
  50.5 12.9 %collective-permute-start.4 = (bf16[256,720]{1,0:T(8,128)(2,1)S(1)}, bf16[256,720]{1,0:T(8,128)(2,1)S(1)}, u32[]{:S(2)}, u32[]{:S(2)}) collective-permute-start(bf16[256,720]{1,0:T(8,128)(2,1)S(1)} %collective-permute-done.2.refs_2_), channel_id=1, source_target_pairs={{0,448},{64,0},{128,64},{192,128},{256,192},{320,256},{384,320},{4... | collective-permute-start | bytes 1105928 | tf_op jit(solution)/shard_map/projection_rows/ppermute | solution.py:34
  54.4 13.9 %collective-permute-start.3 = (bf16[256,720]{1,0:T(8,128)(2,1)S(1)}, bf16[256,720]{1,0:T(8,128)(2,1)}, u32[]{:S(2)}, u32[]{:S(2)}) collective-permute-start(bf16[256,720]{1,0:T(8,128)(2,1)S(1)} %collective-permute-done.1.refs_1_), channel_id=1, source_target_pairs={{0,64},{64,128},{128,192},{192,256},{256,320},{320,384},{384,448},... | collective-permute-start | bytes 1105928 | tf_op jit(solution)/shard_map/projection_rows/ppermute | solution.py:34
  56.4 28.4 %copy-start.7 = (s32[128,4]{0,1:T(4,128)S(1)}, s32[128,4]{0,1:T(4,128)}, u32[]{:S(2)}) copy-start(s32[128,4]{0,1:T(4,128)} %param.21) | copy-start | bytes 6148
  56.4 30.4 %all-to-all-start.1 = ((bf16[8,2,128,256]{3,2,1,0:T(8,128)(2,1)}), bf16[8,2,128,256]{3,2,1,0:T(8,128)(2,1)S(1)}, u32[]{:S(2)}, u32[]{:S(2)}) async-start(bf16[8,2,128,256]{3,2,1,0:T(8,128)(2,1)} %bitcast.11), calls=%async_computation.1 | async-start | bytes 2097152 | tf_op jit(solution)/shard_map/attention/all_to_all | solution.py:328
  63.4 12.5 %collective-permute-start.6 = (bf16[256,720]{1,0:T(8,128)(2,1)S(1)}, bf16[256,720]{1,0:T(8,128)(2,1)S(1)}, u32[]{:S(2)}, u32[]{:S(2)}) collective-permute-start(bf16[256,720]{1,0:T(8,128)(2,1)S(1)} %collective-permute-done.4.refs_4_), channel_id=1, source_target_pairs={{0,448},{64,0},{128,64},{192,128},{256,192},{320,256},{384,320},{4... | collective-permute-start | bytes 1105928 | tf_op jit(solution)/shard_map/projection_rows/ppermute | solution.py:34
  68.3 13.8 %collective-permute-start.5 = (bf16[256,720]{1,0:T(8,128)(2,1)}, bf16[256,720]{1,0:T(8,128)(2,1)S(1)}, u32[]{:S(2)}, u32[]{:S(2)}) collective-permute-start(bf16[256,720]{1,0:T(8,128)(2,1)} %collective-permute-done.3.refs_3_), channel_id=1, source_target_pairs={{0,64},{64,128},{128,192},{192,256},{256,320},{320,384},{384,448},... | collective-permute-start | bytes 1105928 | tf_op jit(solution)/shard_map/projection_rows/ppermute | solution.py:34
  76.6 10.1 %collective-permute-start.8 = (bf16[128,720]{1,0:T(8,128)(2,1)}, bf16[128,720]{1,0:T(8,128)(2,1)}, u32[]{:S(2)}, u32[]{:S(2)}) collective-permute-start(bf16[128,720]{1,0:T(8,128)(2,1)} %slice.9), channel_id=1, source_target_pairs={{0,448},{64,0},{128,64},{192,128},{256,192},{320,256},{384,320},{4... | collective-permute-start | bytes 552968 | tf_op jit(solution)/shard_map/projection_rows/ppermute | solution.py:34
  82.8 8.2 %collective-permute-start.7 = (bf16[128,720]{1,0:T(8,128)(2,1)}, bf16[128,720]{1,0:T(8,128)(2,1)}, u32[]{:S(2)}, u32[]{:S(2)}) collective-permute-start(bf16[128,720]{1,0:T(8,128)(2,1)} %slice.8), channel_id=1, source_target_pairs={{0,64},{64,128},{128,192},{192,256},{256,320},{320,384},{384,448},... | collective-permute-start | bytes 552968 | tf_op jit(solution)/shard_map/projection_rows/ppermute | solution.py:34
  91.0 8.4 %copy-start.8 = (f32[720]{0:T(1024)S(1)}, f32[720]{0:T(1024)}, u32[]{:S(2)}) copy-start(f32[720]{0:T(1024)} %param.20) | copy-start | bytes 8644
  94.0 0.8 copy-start
  94.7 6.1 %collective-permute-start.9 = (f32[128,720]{1,0:T(8,128)}, f32[128,720]{1,0:T(8,128)S(1)}, u32[]{:S(2)}, u32[]{:S(2)}) collective-permute-start(f32[128,720]{1,0:T(8,128)} %get-tuple-element.20), channel_id=1, source_target_pairs={{0,4},{4,0},{1,5},{5,1},{2,6},{6,2},{3,7},{7,3},{8,12},{12,8},{9,1... | collective-permute-start | bytes 1105928 | tf_op jit(solution)/shard_map/stream/ppermute | solution.py:34
  100.9 1.0 copy-start.1
  152.4 7.3 %collective-permute-start.10 = (bf16[4608,128]{1,0:T(8,128)(2,1)S(1)}, bf16[4608,128]{1,0:T(8,128)(2,1)S(1)}, u32[]{:S(2)}, u32[]{:S(2)}) collective-permute-start(bf16[4608,128]{1,0:T(8,128)(2,1)S(1)} %bitcast.25), channel_id=1, source_target_pairs={{0,4},{4,0},{1,5},{5,1},{2,6},{6,2},{3,7},{7,3},{8,12},{12,8},{9,1... | collective-permute-start | bytes 3538952 | tf_op jit(solution)/shard_map/dispatch/ppermute | solution.py:34
  172.7 6.7 %collective-permute-start.11 = (bf16[4608,128]{1,0:T(8,128)(2,1)S(1)}, bf16[4608,128]{1,0:T(8,128)(2,1)S(1)}, u32[]{:S(2)}, u32[]{:S(2)}) collective-permute-start(bf16[4608,128]{1,0:T(8,128)(2,1)S(1)} %get-tuple-element.23), channel_id=1, source_target_pairs={{0,4},{4,0},{1,5},{5,1},{2,6},{6,2},{3,7},{7,3},{8,12},{12,8},{9,1... | collective-permute-start | bytes 3538952 | tf_op jit(solution)/shard_map/experts/ppermute | solution.py:34
  180.7 18.8 %copy-start.9 = (bf16[128,4]{0,1:T(4,128)(2,1)S(1)}, bf16[128,4]{0,1:T(4,128)(2,1)}, u32[]{:S(2)}) copy-start(bf16[128,4]{0,1:T(4,128)(2,1)} %param.22) | copy-start | bytes 3076
  180.7 50.5 %all-to-all-start.3 = ((bf16[256,9,2,128]{3,2,1,0:T(2,128)(2,1)}), bf16[256,9,2,128]{3,2,1,0:T(2,128)(2,1)S(1)}, u32[]{:S(2)}, u32[]{:S(2)}) async-start(bf16[256,9,2,128]{3,2,1,0:T(2,128)(2,1)} %bitcast.16), calls=%async_computation.3 | async-start | bytes 2359296 | tf_op jit(solution)/shard_map/combine/all_to_all | solution.py:376
Sparse Core Ops, SparseCore 0:
  9.8 153.0 all-gather.2
